TPU v7x, 256 devices: a whole 4x4x8 slice. The times are simulated.
256 devices in a mesh: row: 8 (over z), col: 4 (over x_hi, core), chan: 8 (over x_lo, y).
Axes of the slice: x: 4 (x_hi: 2, x_lo: 2; x = x_hi * 2 + x_lo), y: 4, z: 8, core: 2. Of those that a mesh axis runs over, the one named last changes fastest.
Arguments:
- alignment_features: bfloat16 [2048, 512, 64], P('col', 'row'), may hold values from -8 to 8
- alignment_row_mask: int32 [2048], P('col'), may hold values 0 or 1
- residue_token_mask: int32 [512], P('row'), may hold values 0 or 1
- layer_norm_gain: float32 [64], replicated, may hold values from 0.25 to 1.75
- layer_norm_bias: float32 [64], replicated, may hold values from -3 to 3
- left_factor_weight: bfloat16 [64, 32], P(None, 'chan'), may hold values from -0.75 to 0.75
- right_factor_weight: bfloat16 [64, 32], replicated, may hold values from -0.75 to 0.75
- output_weight: bfloat16 [1024, 128], P('chan'), may hold values from -0.1875 to 0.1875
- output_bias: float32 [128], replicated, may hold values from -3 to 3
Outputs:
- pair_update: bfloat16 [512, 512, 128], P('col', ('row', 'chan'))
All inputs are finite; a program needn't handle non-finite values. No bound on the sum of `alignment_row_mask` or of `residue_token_mask` on one device may be relied on, other than what follows from the above.
Results may differ from a plain program's by a relative error of at most 0.0038.
Values may be sent and summed in bfloat16 or wider, within the bound.
No kernel may reach another device: no remote copies, remote signals or barrier semaphores. Data moves between devices by JAX's collectives and lax.ppermute only.
A program may use at most 128 MiB of HBM per device.

v0:
```python
import jax
import jax.numpy as jnp
from jax import lax
from jax.sharding import PartitionSpec as P


def apply_layer_norm(features, layer_norm_gain, layer_norm_bias):
    values = features.astype(jnp.float32)
    center = values - jnp.mean(values, axis=-1, keepdims=True)
    spread = jnp.mean(center * center, axis=-1, keepdims=True)
    return (center * lax.rsqrt(spread + 1e-05) * layer_norm_gain + layer_norm_bias).astype(
        jnp.bfloat16
    )


def make_factors(
    features,
    rows_used,
    tokens_used,
    layer_norm_gain,
    layer_norm_bias,
    left_factor_weight,
    right_factor_weight,
):
    normalized_features = apply_layer_norm(features, layer_norm_gain, layer_norm_bias)
    weight = rows_used[:, None].astype(jnp.float32) * tokens_used[None, :].astype(jnp.float32)
    left_part = (
        jnp.einsum(
            "stm,mc->sct",
            normalized_features,
            left_factor_weight,
            preferred_element_type=jnp.float32,
        )
        * weight[:, None, :]
    )
    right_part = (
        jnp.einsum(
            "stm,me->ste",
            normalized_features,
            right_factor_weight,
            preferred_element_type=jnp.float32,
        )
        * weight[:, :, None]
    )
    return (left_part.astype(jnp.bfloat16), right_part.astype(jnp.bfloat16))


def body(
    alignment_features,
    alignment_row_mask,
    residue_token_mask,
    layer_norm_gain,
    layer_norm_bias,
    left_factor_weight,
    right_factor_weight,
    output_weight,
    output_bias,
):
    every_feature, every_row = (
        lax.all_gather(alignment_features, "col", axis=0, tiled=True),
        lax.all_gather(alignment_row_mask, "col", axis=0, tiled=True),
    )
    left_part, right_every = make_factors(
        every_feature,
        every_row,
        residue_token_mask,
        layer_norm_gain,
        layer_norm_bias,
        left_factor_weight,
        right_factor_weight,
    )
    tokens_here = residue_token_mask.shape[0]
    mask_shaped = residue_token_mask.reshape(1, 1, tokens_here)
    owner_count = lax.axis_size("row") // lax.axis_size("col")
    block_tokens = tokens_here * owner_count
    col_index = lax.axis_index("col")
    left_every, mask_every = (
        lax.all_gather(left_part, "row", axis=2, tiled=True),
        lax.all_gather(mask_shaped, "row", axis=2, tiled=True),
    )
    left_block = lax.dynamic_slice_in_dim(left_every, col_index * block_tokens, block_tokens, 2)
    mask_block = lax.dynamic_slice_in_dim(mask_every, col_index * block_tokens, block_tokens, 2)
    products = jnp.einsum(
        "sci,sje->ijce", left_block, right_every, preferred_element_type=jnp.float32
    ).astype(jnp.bfloat16)
    flat_products = products.reshape(block_tokens * tokens_here, -1)
    partial_pairs = jnp.dot(
        flat_products, output_weight, preferred_element_type=jnp.float32
    ).reshape(block_tokens, tokens_here, -1)
    chan_count = lax.axis_size("chan")
    share = tokens_here // chan_count
    chan_index = lax.axis_index("chan")
    total_pairs = lax.psum(partial_pairs, "chan")
    summed = lax.dynamic_slice_in_dim(total_pairs, chan_index * share, share, 1)
    row_total = jnp.sum(every_row).astype(jnp.float32)
    first_used = mask_block.reshape(block_tokens).astype(jnp.float32)
    second_used = lax.dynamic_slice_in_dim(residue_token_mask, chan_index * share, share, 0).astype(
        jnp.float32
    )
    count = jnp.maximum(row_total * first_used[:, None] * second_used[None, :], 1.0)
    return ((summed + output_bias) / count[:, :, None]).astype(jnp.bfloat16)


def solution(mesh):
    in_specs = (
        P("col", "row", None),
        P("col"),
        P("row"),
        P(),
        P(),
        P(None, "chan"),
        P(),
        P("chan", None),
        P(),
    )
    out_specs = P("col", ("row", "chan"), None)
    return jax.shard_map(body, mesh=mesh, in_specs=in_specs, out_specs=out_specs, check_vma=False)
```

profile of v0, /device:TPU:38, one launch (start us, length us, event | category | flops | bytes accessed | tf_op | source)
XLA Modules:
  0.0 388.3 jit_solution(13971857495411139468)
XLA Ops:
  6.5 0.0 copy-start
  6.5 0.0 all-gather.5.cloned.1.call-start
  6.5 0.7 all-gather.5.cloned.1.call-update
  7.3 0.0 all-gather.7.cloned.1.call-start
  7.3 0.7 convert_element_type.49
  8.0 6.8 %all-gather.1 = s32[4,1,512]{2,1,0:T(1,128)S(1)} all-gather(s32[1,1,512]{2,1,0:T(1,128)} %bitcast.35), channel_id=1, replica_groups=mesh['row'=8,'col'=4,'chan'=8] {'col'}, dimensions={0}, use_global_device_ids=true | all-gather | bytes 10240 | tf_op jit(solution)/shard_map/all_gather | solution.py:61
  14.8 0.6 fusion.25
  15.4 0.1 broadcast_multiply_fusion
  15.5 0.0 copy-start.4
  15.5 0.0 copy-start.5
  15.6 107.1 %all-gather.5.cloned.1.call-done = bf16[2048,64,64]{0,2,1:T(8,128)(2,1)} async-done(((bf16[512,64,64]{0,2,1:T(8,128)(2,1)}), bf16[2048,64,64]{0,2,1:T(8,128)(2,1)}) %all-gather.5.cloned.1.call-update) | async-done | bytes 16777232 | tf_op jit(solution)/shard_map/all_gather | solution.py:60
  122.7 0.0 copy-start.1
  122.7 7.4 %convert_reduce_fusion = f32[2048,64]{0,1:T(8,128)S(1)} fusion(bf16[2048,64,64]{0,2,1:T(8,128)(2,1)} %all-gather.5.cloned.1.call-done), kind=kLoop, calls=%fused_computation.1 | loop fusion | flops 16646144 | bytes 17301504 | tf_op jit(solution)/shard_map/reduce_sum | solution.py:9
  130.1 3.2 copy-done.1
  133.3 5.4 %fusion.2 = f32[2048,64]{0,1:T(8,128)S(1)} fusion(bf16[2048,64,64]{0,2,1:T(8,128)(2,1)S(1)} %copy-done.1, f32[2048,64]{0,1:T(8,128)S(1)} %broadcast_multiply_fusion.1), kind=kLoop, calls=%fused_computation.4 | loop fusion | flops 33423360 | bytes 17825792 | tf_op jit(solution)/shard_map/reduce_sum | solution.py:10
  138.7 0.1 add_rsqrt_fusion
  138.8 0.0 copy-done.4
  138.8 0.0 copy-done.5
  138.8 0.0 copy-start.3
  138.9 6.6 %fusion.5 = bf16[2048,64,64]{0,2,1:T(8,128)(2,1)S(1)} fusion(bf16[2048,64,64]{0,2,1:T(8,128)(2,1)S(1)} %copy-done.1, f32[64]{0:T(128)S(1)} %copy-done.4, f32[64]{0:T(128)S(1)} %copy-done.5, f32[2048,64]{0,1:T(8,128)S(1)} %add_rsqrt_fusion, f32[2048,64]{0,1:T(8,128)S(1)} %broadcast_multiply_fusion.1), kind=kLoop, calls=%fused_computation.7 | loop fusion | flops 50331648 | bytes 34603520 | tf_op jit(solution)/shard_map/convert_element_type | solution.py:11
  145.5 0.0 copy-start.2
  145.5 5.7 %copy-done.2 = bf16[2048,64,64]{0,2,1:T(8,128)(2,1)} copy-done((bf16[2048,64,64]{0,2,1:T(8,128)(2,1)}, bf16[2048,64,64]{0,2,1:T(8,128)(2,1)S(1)}, u32[]{:S(2)}) %copy-start.2) | copy-done | bytes 16777240
  151.2 0.0 copy-done.3
  151.2 0.0 copy-start.7
  151.2 5.2 %fusion.13 = bf16[2048,4,64]{0,1,2:T(4,128)(2,1)} fusion(bf16[2048,64,64]{0,2,1:T(8,128)(2,1)S(1)} %fusion.5, f32[2048,64]{0,1:T(8,128)S(1)} %broadcast_multiply_fusion, bf16[64,4]{0,1:T(4,128)(2,1)S(1)} %copy-done.3), kind=kOutput, calls=%fused_computation.15 | convolution fusion | flops 68157440 | bytes 18350592 | tf_op jit(solution)/shard_map/stm,mc->sct/dot_general | solution.py:28
  156.4 0.0 all-gather.7.cloned.1.call-update
  156.4 0.0 all-reduce.3.cloned.1.call-start
  156.5 93.4 %all-gather.7.cloned.1.call-done = bf16[2048,4,512]{0,1,2:T(4,128)(2,1)} async-done(((bf16[2048,4,64]{0,1,2:T(4,128)(2,1)}), bf16[2048,4,512]{0,1,2:T(4,128)(2,1)}) %all-gather.7.cloned.1.call-update) | async-done | bytes 8388624 | tf_op jit(solution)/shard_map/all_gather | solution.py:78
  249.9 2.6 constant_dynamic-slice_fusion
  252.5 3.0 copy.18
  255.5 0.0 copy-done.7
  255.5 0.0 copy-start.9
  255.5 0.0 copy-start.8
  255.5 0.0 copy-start.6
  255.5 11.1 %fusion.15 = bf16[64,32,4,128]{3,1,2,0:T(8,128)(2,1)S(1)} fusion(bf16[2048,4,128]{2,0,1:T(8,128)(2,1)} %copy.18, f32[2048,64]{0,1:T(8,128)S(1)} %broadcast_multiply_fusion, bf16[2048,64,64]{0,2,1:T(8,128)(2,1)} %copy-done.2, bf16[64,32]{0,1:T(8,128)(2,1)S(1)} %copy-done.7), kind=kOutput, calls=%fused_computation.17 | convolution fusion | flops 4841275392 | bytes 21499904 | tf_op jit(solution)/shard_map/sci,sje->ijce/dot_general | solution.py:83
  266.6 0.0 copy-done
  266.6 2.7 fusion.20
  269.3 0.0 all-reduce.3.cloned.1.call-update
  270.0 0.0 copy-done.9
  270.0 0.6 dynamic-slice.1
  271.2 0.0 copy-done.8
  271.2 0.2 dynamic-update-slice
  271.5 12.9 %all-reduce = s32[512]{0:T(512)S(1)} all-reduce(s32[512]{0:T(512)S(1)} %dynamic-update-slice), channel_id=2, replica_groups=mesh['row'=8,'col'=4,'chan'=8] {'row'}, use_global_device_ids=true, to_apply=%add | all-reduce | flops 512 | bytes 4096
  284.4 0.1 dynamic-slice_convert_fusion
  284.4 0.1 convert_multiply_fusion
  284.5 0.1 multiply_maximum_fusion
  284.6 95.0 %all-reduce.3.cloned.1.call-done = f32[128,64,128]{2,0,1:T(8,128)} async-done(((f32[128,64,128]{2,0,1:T(8,128)}), f32[128,64,128]{2,0,1:T(8,128)}) %all-reduce.3.cloned.1.call-update) | async-done | bytes 4194320 | tf_op jit(solution)/shard_map/psum | solution.py:93
  379.6 0.0 copy-done.6
  379.6 1.2 divide_convert_fusion
  380.9 0.9 copy.15
  (2 shorter events, 0.0 us)
Async XLA Ops:
  6.5 260.0 %copy-start = (bf16[128,128]{1,0:T(8,128)(2,1)S(1)}, bf16[128,128]{1,0:T(8,128)(2,1)}, u32[]{:S(2)}) copy-start(bf16[128,128]{1,0:T(8,128)(2,1)} %param.16) | copy-start | bytes 98308
  6.5 116.1 %all-gather.5.cloned.1.call-start = ((), (), s32[]{:S(2)}) async-start(), calls=%async_computation | async-start | bytes 20971520 | tf_op jit(solution)/shard_map/all_gather | solution.py:60
  7.3 242.6 %all-gather.7.cloned.1.call-start = ((), (), s32[]{:S(2)}) async-start(), calls=%async_computation.1 | async-start | bytes 9437184 | tf_op jit(solution)/shard_map/all_gather | solution.py:78
  15.5 123.3 %copy-start.4 = (f32[64]{0:T(128)S(1)}, f32[64]{0:T(128)}, u32[]{:S(2)}) copy-start(f32[64]{0:T(128)} %param.13) | copy-start | bytes 772
  15.5 123.3 %copy-start.5 = (f32[64]{0:T(128)S(1)}, f32[64]{0:T(128)}, u32[]{:S(2)}) copy-start(f32[64]{0:T(128)} %param.12) | copy-start | bytes 772
  122.7 10.7 %copy-start.1 = (bf16[2048,64,64]{0,2,1:T(8,128)(2,1)S(1)}, bf16[2048,64,64]{0,2,1:T(8,128)(2,1)}, u32[]{:S(2)}) copy-start(bf16[2048,64,64]{0,2,1:T(8,128)(2,1)} %all-gather.5.cloned.1.call-done) | copy-start | bytes 50331652
  138.8 12.4 %copy-start.3 = (bf16[64,4]{0,1:T(4,128)(2,1)S(1)}, bf16[64,4]{0,1:T(4,128)(2,1)}, u32[]{:S(2)}) copy-start(bf16[64,4]{0,1:T(4,128)(2,1)} %param.14) | copy-start | bytes 1540
  145.5 5.7 %copy-start.2 = (bf16[2048,64,64]{0,2,1:T(8,128)(2,1)}, bf16[2048,64,64]{0,2,1:T(8,128)(2,1)S(1)}, u32[]{:S(2)}) copy-start(bf16[2048,64,64]{0,2,1:T(8,128)(2,1)S(1)} %fusion.5) | copy-start | bytes 50331652
  151.2 104.3 %copy-start.7 = (bf16[64,32]{0,1:T(8,128)(2,1)S(1)}, bf16[64,32]{0,1:T(8,128)(2,1)}, u32[]{:S(2)}) copy-start(bf16[64,32]{0,1:T(8,128)(2,1)} %param.15) | copy-start | bytes 12292
  156.4 223.2 %all-reduce.3.cloned.1.call-start = ((), (), s32[]{:S(2)}) async-start(), calls=%async_computation.2 | async-start | bytes 8388608 | tf_op jit(solution)/shard_map/psum | solution.py:93
  255.5 14.5 %copy-start.9 = (u32[256]{0:T(256)S(1)}, u32[256]{0:T(256)}, u32[]{:S(2)}) copy-start(u32[256]{0:T(256)} %constant.32) | copy-start | bytes 3076
  255.5 15.7 %copy-start.8 = (s32[64]{0:T(128)S(1)}, s32[64]{0:T(128)}, u32[]{:S(2)}) copy-start(s32[64]{0:T(128)} %param.11) | copy-start | bytes 772
  255.5 124.2 %copy-start.6 = (f32[128]{0:T(128)S(1)}, f32[128]{0:T(128)}, u32[]{:S(2)}) copy-start(f32[128]{0:T(128)} %param.17) | copy-start | bytes 1540
Sparse Core Ops, SparseCore 0:
  9.1 113.4 all-gather.4
  156.5 93.2 all-gather.6
  269.4 110.1 all-reduce.2
where the time goes:
time: 390 us; the launch traced here: 388 us
  waiting for transfers between devices  296 us (76%)
  other arithmetic  22.4 us (6%)
  blocking collectives  19.7 us (5%)
  matrix products  19 us (5%)
  local copies, waits for them, and re-layouts  16.3 us (4%)
  between operations  14.6 us (4%)
    all_gather x1, waiting for transfers between devices, body(): lax.all_gather(alignment_features, 'col', axis=0, tiled=True)  107 us
    psum x1, waiting for transfers between devices, body(): total_pairs = lax.psum(partial_pairs, 'chan')  95 us
    all_gather x1, waiting for transfers between devices, body(): lax.all_gather(left_part, 'row', axis=2, tiled=True)  93.4 us
    unnamed x1, blocking collectives  12.9 us
    unnamed x24, local copies, waits for them, and re-layouts  12.8 us
    dot_general x1, matrix products, body(): jnp.einsum('sci,sje->ijce', left_block, right_every, preferred_element_ty...  11.1 us
  transfers between devices with their start and end apart: 3, of which 3 were waited for; matrix products, arithmetic and copies ran while one was open for 1% of the time, Pallas kernels for 0%

commit v1 on v0

v1 whole, which is shorter than its diff:
```python
import functools

import jax
import jax.numpy as jnp
from jax import lax
from jax.experimental import pallas as pl
from jax.experimental.pallas import tpu as pltpu
from jax.sharding import PartitionSpec as P

F32 = jnp.float32
BF16 = jnp.bfloat16
VMEM = pl.BlockSpec(memory_space=pltpu.VMEM)
ANY = pl.BlockSpec(memory_space=pl.ANY)

S = 512
N = 64
M = 64
C = 32
Z = 128
T = 8
ROWS = N * T
EXTRA = 8


def column_of(row):
    n = row.shape[1]
    r = lax.broadcasted_iota(jnp.int32, (n, n), 0)
    c = lax.broadcasted_iota(jnp.int32, (n, n), 1)
    return jnp.sum(jnp.where(r == c, jnp.broadcast_to(row, (n, n)), 0.0), axis=1, keepdims=True)


def normalize(x, gain, bias):
    values = x.astype(F32)
    center = values - jnp.mean(values, axis=1, keepdims=True)
    spread = jnp.mean(center * center, axis=1, keepdims=True)
    return center * lax.rsqrt(spread + 1e-05) * gain[None] + bias[None]


def right_kernel(x_ref, row_ref, tok_ref, gain_ref, bias_ref, wr_ref, wl_ref, wo_ref, out_ref, pack_ref, buf, sem):
    k = lax.axis_index("chan")
    copy = pltpu.make_async_copy(x_ref.at[pl.ds(k * T, T)], buf, sem)
    copy.start()
    pack_ref[0:Z, :] = wo_ref[...]
    pack_ref[Z : Z + 16, :] = jnp.zeros((16, Z), BF16)
    pack_ref[Z : Z + 4, 0:M] = wl_ref[...]
    gain = column_of(gain_ref[...])
    bias = column_of(bias_ref[...])
    token = tok_ref[...].astype(F32)
    t_iota = lax.broadcasted_iota(jnp.int32, (T, N), 0)
    l_iota = lax.broadcasted_iota(jnp.int32, (T, N), 1)
    token_col = jnp.sum(
        jnp.where(l_iota == t_iota + k * T, jnp.broadcast_to(token, (T, N)), 0.0), axis=1, keepdims=True
    )
    weight = token_col * row_ref[...].astype(F32)
    copy.wait()
    normed = normalize(buf[...], gain, bias).astype(BF16)
    wr = wr_ref[...]
    for t in range(T):
        part = jnp.dot(wr, normed[t], preferred_element_type=F32)
        out_ref[t * C : (t + 1) * C, :] = (part * weight[t : t + 1]).astype(BF16)
    pad = jnp.concatenate([jnp.broadcast_to(token_col, (T, S)), jnp.zeros((T, S), F32)], axis=0)
    out_ref[T * C :, :] = pad.astype(BF16)


def norm_kernel(x_ref, row_ref, tok_ref, gain_ref, bias_ref, out_ref):
    step = pl.program_id(0)
    gain = column_of(gain_ref[...])
    bias = column_of(bias_ref[...])
    token = tok_ref[...].astype(F32)
    t_iota = lax.broadcasted_iota(jnp.int32, (T, N), 0)
    l_iota = lax.broadcasted_iota(jnp.int32, (T, N), 1)
    token_col = jnp.sum(
        jnp.where(l_iota == t_iota + step * T, jnp.broadcast_to(token, (T, N)), 0.0), axis=1, keepdims=True
    )
    weight = token_col * row_ref[...].astype(F32)
    normed = normalize(x_ref[...], gain, bias)
    out_ref[...] = (normed * weight[:, None, :]).astype(BF16).reshape(T * M, S)


def left_kernel(n_ref, wl_ref, out_ref, wide):
    @pl.when(pl.program_id(0) == 0)
    def _():
        rep = (
            lax.broadcasted_iota(jnp.int32, (C * T, C), 0) // T
            == lax.broadcasted_iota(jnp.int32, (C * T, C), 1)
        ).astype(F32).astype(BF16)
        tile = (
            lax.broadcasted_iota(jnp.int32, (M, T * M), 0)
            == lax.broadcasted_iota(jnp.int32, (M, T * M), 1) % M
        ).astype(F32).astype(BF16)
        tall = jnp.dot(rep, wl_ref[...], preferred_element_type=F32).astype(BF16)
        full = jnp.dot(tall, tile, preferred_element_type=F32)
        own = (
            lax.broadcasted_iota(jnp.int32, (C * T, T * M), 0) % T
            == lax.broadcasted_iota(jnp.int32, (C * T, T * M), 1) // M
        )
        wide[...] = jnp.where(own, full, 0.0).astype(BF16)

    part = jnp.dot(wide[...], n_ref[...], preferred_element_type=F32)
    out_ref[...] = part.reshape(C, T, S).astype(BF16)


def pair_block(load, token_rows, lf_ref, w2_ref, row_ref, spread, store):
    for n in range(8):
        for h in range(2):
            part = lax.dot_general(
                load(h),
                lf_ref[n * 256 : (n + 1) * 256, :],
                (((1,), (1,)), ((), ())),
                preferred_element_type=F32,
            ).astype(BF16)
            for q in range(4):
                t = h * 4 + q
                for u in range(2):
                    hi = n * 2 + u
                    spread[t // 2, hi * C : (hi + 1) * C, (t % 2) * 128 : (t % 2) * 128 + 128] = part[
                        q * C : (q + 1) * C, u * 128 : (u + 1) * 128
                    ]
    low = lax.broadcasted_iota(jnp.int32, (Z, 128), 1) < N
    for p in range(T // 2):
        both = jnp.dot(w2_ref[...], spread[p], preferred_element_type=F32)
        x0, y0 = both[:Z, :128], both[Z:, :128]
        x1, y1 = both[:Z, 128:], both[Z:, 128:]
        pair = jnp.where(low, x0, y1) + pltpu.roll(jnp.where(low, x1, y0), N, 1)
        flat = pair.T
        store(pl.ds(2 * p, N, stride=T), flat[:N])
        store(pl.ds(2 * p + 1, N, stride=T), flat[N:])
    rows_used = jnp.sum(row_ref[...].astype(F32), axis=1, keepdims=True)
    lane = lax.broadcasted_iota(jnp.int32, (EXTRA, Z), 1)
    mask = jnp.broadcast_to(token_rows().astype(F32)[:EXTRA, :1], (EXTRA, Z))
    store(pl.ds(ROWS, EXTRA), jnp.where(lane < N, jnp.broadcast_to(rows_used, (EXTRA, Z)), mask))


def whole(ref):
    return (lambda h: ref[h * 128 : (h + 1) * 128, :]), (lambda: ref[T * C :, :])


def halves(first, second):
    return (lambda h: first[...] if h == 0 else second[0:128, :]), (lambda: second[128:, :])


def first_kernel(own, lf, w2, row, out, spread):
    def store(where, value):
        out[where, :] = value

    pair_block(*whole(own), lf, w2, row, spread, store)


def core_kept(offset):
    block = lax.rem(lax.axis_index("row") + offset + 8, 8)
    return lax.rem(block // 2, 2) == lax.rem(lax.axis_index("col"), 2)


def x_kept(offset):
    block = lax.rem(lax.axis_index("row") + offset + 8, 8)
    return block // 4 == lax.axis_index("col") // 2


def keep_or_send(kept, make, send, keep):
    @pl.when(kept)
    def _():
        make(keep)

    @pl.when(jnp.logical_not(kept))
    def _():
        make(send)


def two_kernel(offset, back, ahead, lf, w2, row, out, spread):
    kept = core_kept(offset).astype(jnp.int32)

    def store_ahead(where, value):
        out[kept, where, :] = value

    def store_back(where, value):
        out[1 - kept, where, :] = value

    pair_block(*whole(back), lf, w2, row, spread, store_back)
    pair_block(*whole(ahead), lf, w2, row, spread, store_ahead)


def mixed_kernel(back, ahead, base, lf, w2, row, out, rest, spread):
    kept = core_kept(2).astype(jnp.int32)

    def store_ahead(where, value):
        out[kept, where, :] = value

    def store_back(where, value):
        rest[where, :] = value

    out[1 - kept, :, :] = base[...]
    pair_block(*whole(ahead), lf, w2, row, spread, store_ahead)
    pair_block(*whole(back), lf, w2, row, spread, store_back)


def last_kernel(first, second, rest, lf, w2, row, out, spread):
    kept = core_kept(4).astype(jnp.int32)

    def store(where, value):
        out[kept, where, :] = value

    out[1 - kept, :, :] = rest[...]
    pair_block(*halves(first, second), lf, w2, row, spread, store)


def add_kernel(a_offsets, keep_a, got_a, keep_b, got_b, out):
    first, second = a_offsets
    kept = jnp.where(core_kept(first), x_kept(first), x_kept(second)).astype(jnp.int32)
    out[kept, :, :] = keep_a[...] + got_a[...]
    out[1 - kept, :, :] = keep_b[...] + got_b[...]


def final_kernel(keep, got, tok_ref, bias_ref, out):
    total = keep[...] + got[...]
    tail = total[ROWS:, :]
    rows_used = tail[0:1, 0:1]
    second = (tail[:, N : N + 1] > 0.0).astype(F32)
    first = column_of(tok_ref[...].astype(F32))
    count = jnp.maximum(rows_used[None] * first[:, :, None] * second[None], 1.0)
    pairs = total[:ROWS, :].reshape(N, T, Z)
    out[...] = ((pairs + bias_ref[...][None]) / count).astype(BF16)


def call(kernel, out, *args, specs=None, scratch=(), flops=0, **kw):
    leaves = jax.tree.leaves(out)
    bytes_accessed = sum(a.size * a.dtype.itemsize for a in list(args) + leaves)
    return pl.pallas_call(
        kernel,
        out_shape=out,
        in_specs=specs or [VMEM] * len(args),
        out_specs=jax.tree.map(lambda _: VMEM, out),
        scratch_shapes=scratch,
        cost_estimate=pl.CostEstimate(flops=flops, bytes_accessed=bytes_accessed, transcendentals=0),
        **kw,
    )(*args)


def shape(dims, dtype):
    return jax.ShapeDtypeStruct(dims, dtype)


def body(x, row_mask, token_mask, gain, bias, wl, wr, wo, out_bias):
    xt = x.transpose(1, 2, 0)
    row = row_mask.reshape(1, S)
    tok = token_mask.reshape(1, N)
    gain, bias = gain.reshape(1, M), bias.reshape(1, M)

    ring = [[(i, (i + d) % 8) for i in range(8)] for d in (1, -1)]
    y_ring = [[(a * 4 + b, a * 4 + (b + d) % 4) for a in range(2) for b in range(4)] for d in (1, -1)]
    x_swap = [(c, (c + 4) % 8) for c in range(8)]
    core_swap = [(0, 1), (1, 0), (2, 3), (3, 2)]
    xh_swap = [(0, 2), (1, 3), (2, 0), (3, 1)]

    own, pack = call(
        right_kernel,
        (shape((T * C + 16, S), BF16), shape((Z + 16, Z), BF16)),
        xt, row, tok, gain, bias, wr.T, wl.T, wo,
        specs=[ANY] + [VMEM] * 7,
        scratch=[pltpu.VMEM((T, M, S), BF16), pltpu.SemaphoreType.DMA(())],
    )

    ahead, back = own, own
    from_back, from_ahead = [], []
    for _ in range(3):
        back = lax.ppermute(back, "row", ring[0])
        ahead = lax.ppermute(ahead, "row", ring[1])
        from_back.append(back)
        from_ahead.append(ahead)
    half_a = lax.ppermute(back[:128], "row", ring[0])
    half_b = lax.ppermute(ahead[128:], "row", ring[1])

    up = lax.ppermute(pack, "chan", y_ring[0])
    down = lax.ppermute(pack, "chan", y_ring[1])
    over = lax.ppermute(up, "chan", y_ring[0])
    four = jnp.stack([pack, up, down, over])
    other = lax.ppermute(four, "chan", x_swap)
    packs = jnp.concatenate([four, other], axis=0)
    wl_all = packs[:, Z : Z + 4, :M].reshape(8, 2, 2, M).transpose(0, 2, 1, 3).reshape(C, M)
    w2 = packs[:, :Z, :].reshape(8, 2, 64, Z).transpose(1, 3, 0, 2).reshape(2 * Z, 512)

    normed = pl.pallas_call(
        norm_kernel,
        grid=(N // T,),
        out_shape=shape((N * M, S), BF16),
        in_specs=[
            pl.BlockSpec((T, M, S), lambda i: (i, 0, 0)),
            pl.BlockSpec((1, S), lambda i: (0, 0)),
            pl.BlockSpec((1, N), lambda i: (0, 0)),
            pl.BlockSpec((1, M), lambda i: (0, 0)),
            pl.BlockSpec((1, M), lambda i: (0, 0)),
        ],
        out_specs=pl.BlockSpec((T * M, S), lambda i: (i, 0)),
        cost_estimate=pl.CostEstimate(flops=30_000_000, bytes_accessed=8 << 20, transcendentals=0),
    )(xt, row, tok, gain, bias)
    left = pl.pallas_call(
        left_kernel,
        grid=(N // T,),
        out_shape=shape((C, N, S), BF16),
        in_specs=[
            pl.BlockSpec((T * M, S), lambda i: (i, 0)),
            pl.BlockSpec((C, M), lambda i: (0, 0)),
        ],
        out_specs=pl.BlockSpec((C, T, S), lambda i: (0, i, 0)),
        scratch_shapes=[pltpu.VMEM((C * T, T * M), BF16)],
        cost_estimate=pl.CostEstimate(flops=1 << 30, bytes_accessed=6 << 20, transcendentals=0),
    )(normed, wl_all)
    lf = left.reshape(C * N, S)

    block = shape((ROWS + EXTRA, Z), F32)
    pair = shape((2, ROWS + EXTRA, Z), F32)
    spread = [pltpu.VMEM((T // 2, 512, 256), BF16)]
    one = 800 << 20
    p0 = call(first_kernel, block, own, lf, w2, row, scratch=spread, flops=one)
    p1 = call(functools.partial(two_kernel, 1), pair, from_back[0], from_ahead[0], lf, w2, row, scratch=spread, flops=2 * one)
    p2, rest = call(mixed_kernel, (pair, block), from_back[1], from_ahead[1], p0, lf, w2, row, scratch=spread, flops=2 * one)
    p3 = call(functools.partial(two_kernel, 3), pair, from_back[2], from_ahead[2], lf, w2, row, scratch=spread, flops=2 * one)
    p4 = call(last_kernel, pair, half_a, half_b, rest, lf, w2, row, scratch=spread, flops=one)

    e1 = lax.ppermute(p1[0], "col", core_swap)
    e2 = lax.ppermute(p2[0], "col", core_swap)
    e3 = lax.ppermute(p3[0], "col", core_swap)
    e4 = lax.ppermute(p4[0], "col", core_swap)
    odd = call(functools.partial(add_kernel, (1, -1)), pair, p1[1], e1, p3[1], e3)
    even = call(functools.partial(add_kernel, (0, 2)), pair, p2[1], e2, p4[1], e4)
    f1 = lax.ppermute(odd[0], "col", xh_swap)
    f2 = lax.ppermute(even[0], "col", xh_swap)
    part = shape((N, T, Z), BF16)
    out_bias = out_bias.reshape(1, Z)
    y1 = call(final_kernel, part, odd[1], f1, tok, out_bias)
    y2 = call(final_kernel, part, even[1], f2, tok, out_bias)

    def home(p):
        return [
            (z * 4 + c, (2 * c + ((z % 2) ^ p)) * 4 + z // 2) for z in range(8) for c in range(4)
        ]

    g1 = lax.ppermute(y1, ("row", "col"), home(1))
    g2 = lax.ppermute(y2, ("row", "col"), home(0))
    low_row = lax.axis_index("row") % 2 == 0
    return jnp.where(low_row, jnp.concatenate([g2, g1], 0), jnp.concatenate([g1, g2], 0))


def solution(mesh):
    in_specs = (
        P("col", "row", None),
        P("col"),
        P("row"),
        P(),
        P(),
        P(None, "chan"),
        P(),
        P("chan", None),
        P(),
    )
    out_specs = P("col", ("row", "chan"), None)
    return jax.shard_map(body, mesh=mesh, in_specs=in_specs, out_specs=out_specs, check_vma=False)
```

time: 390 us -> 127 us (0.33)
  waiting for transfers between devices: 296 us -> 21.1 us
  Pallas kernels: 0 us -> 54.9 us
  starting transfers between devices: 0.08 us -> 31.4 us
  other arithmetic: 22.4 us -> 0.75 us
  blocking collectives: 19.7 us -> 0 us
  matrix products: 19 us -> 0 us
  between operations: 14.6 us -> 0.18 us
    all_gather x2 -> x0, waiting for transfers between devices: 200 us -> none  [the longest x1 107 us: body(): lax.all_gather(alignment_features, 'col', axis=0, tiled=True)]
    psum x1 -> x0, waiting for transfers between devices: 95 us -> none  [body(): total_pairs = lax.psum(partial_pairs, 'chan')]
    pallas_call x0 -> x12, Pallas kernels: none -> 54.9 us  [the longest x10 38.3 us: call(): pl.pallas_call(kernel, out_shape=out, in_specs=specs or [VMEM] * len(args...]
    ppermute x0 -> x20, starting transfers between devices: none -> 31.4 us  [the longest x1 5.83 us: body(): g1 = lax.ppermute(y1, ('row', 'col'), home(1))]
    ppermute x0 -> x20, waiting for transfers between devices: none -> 21.1 us  [the longest x1 10.3 us: body(): g2 = lax.ppermute(y2, ('row', 'col'), home(0))]
    dot_general x3 -> x0, matrix products: 19 us -> none  [the longest x1 11.1 us: body(): jnp.einsum('sci,sje->ijce', left_block, right_every, preferred_element_ty...]
    reduce_sum x3 -> x0, other arithmetic: 13.4 us -> none  [the longest x1 7.36 us: apply_layer_norm(): center = values - jnp.mean(values, axis=-1, keepdims=True)]
    unnamed x1 -> x0, blocking collectives: 12.9 us -> none
  transfers between devices with their start and end apart: 3 -> 20, of which waited for: 3 -> 4; matrix products, arithmetic and copies ran while one was open for 1% -> 11% of each run, Pallas kernels for 0% -> 41%
where the time goes in v1:
time: 127 us; the launch traced here: 126 us
  Pallas kernels  54.9 us (43%)
  starting transfers between devices  31.4 us (25%)
  waiting for transfers between devices  21.1 us (17%)
  local copies, waits for them, and re-layouts  17.7 us (14%)
    pallas_call x10, Pallas kernels, call(): pl.pallas_call(kernel, out_shape=out, in_specs=specs or [VMEM] * len(args...  38.3 us
    ppermute x1, waiting for transfers between devices, body(): g2 = lax.ppermute(y2, ('row', 'col'), home(0))  10.3 us
    pallas_call x1, Pallas kernels, body(): pl.pallas_call(norm_kernel, grid=(N // T,), out_shape=shape((N * M, S), B...  9.09 us
    pallas_call x1, Pallas kernels, body(): pl.pallas_call(left_kernel, grid=(N // T,), out_shape=shape((C, N, S), BF...  7.52 us
    ppermute x1, starting transfers between devices, body(): g1 = lax.ppermute(y1, ('row', 'col'), home(1))  5.83 us
    ppermute x3, starting transfers between devices, body(): ahead = lax.ppermute(ahead, 'row', ring[1])  5.64 us
    ppermute x1, starting transfers between devices, body(): g2 = lax.ppermute(y2, ('row', 'col'), home(0))  5.32 us
    unnamed x35, local copies, waits for them, and re-layouts  5.29 us
  transfers between devices with their start and end apart: 20, of which 4 were waited for; matrix products, arithmetic and copies ran while one was open for 11% of the time, Pallas kernels for 41%

profile of v1, /device:TPU:38, one launch (start us, length us, event | category | flops | bytes accessed | tf_op | source)
XLA Modules:
  0.0 126.2 jit_solution(7137709363531790101)
XLA Ops:
  0.0 3.1 %shard_map.91 = (bf16[272,512]{1,0:T(8,128)(2,1)}, bf16[144,128]{1,0:T(8,128)(2,1)}) custom-call(bf16[64,64,512]{2,1,0:T(8,128)(2,1)} %bitcast.54, s32[1,512]{1,0:T(1,128)} %bitcast.70, s32[1,64]{1,0:T(1,128)} %bitcast.78, f32[1,64]{1,0:T(1,128)} %bitcast.82, f32[1,64]{1,0:T(1,128)} %bitcast.84, bf16[32,64]{1,0:T(8,128)(2,1)} %bitcast.77, ...), custom_call_target="tpu_custom_call" | custom-call | bytes 4549888 | tf_op jit(solution)/shard_map/pallas_call | solution.py:227
  3.2 1.7 %collective-permute-start.4 = (bf16[144,128]{1,0:T(8,128)(2,1)}, bf16[144,128]{1,0:T(8,128)(2,1)S(1)}, u32[]{:S(2)}, u32[]{:S(2)}) collective-permute-start(bf16[144,128]{1,0:T(8,128)(2,1)} %get-tuple-element.10), channel_id=1, source_target_pairs={{0,1},{1,2},{2,3},{3,0},{4,5},{5,6},{6,7},{7,4},{8,9},{9,10},{10,1... | collective-permute-start | bytes 110600 | tf_op jit(solution)/shard_map/ppermute | solution.py:272
  4.8 1.7 %collective-permute-start.5 = (bf16[144,128]{1,0:T(8,128)(2,1)}, bf16[144,128]{1,0:T(8,128)(2,1)S(1)}, u32[]{:S(2)}, u32[]{:S(2)}) collective-permute-start(bf16[144,128]{1,0:T(8,128)(2,1)} %get-tuple-element.10), channel_id=1, source_target_pairs={{0,3},{1,0},{2,1},{3,2},{4,7},{5,4},{6,5},{7,6},{8,11},{9,8},{10,9... | collective-permute-start | bytes 110600 | tf_op jit(solution)/shard_map/ppermute | solution.py:273
  6.5 1.9 %collective-permute-start = (bf16[272,512]{1,0:T(8,128)(2,1)}, bf16[272,512]{1,0:T(8,128)(2,1)S(1)}, u32[]{:S(2)}, u32[]{:S(2)}) collective-permute-start(bf16[272,512]{1,0:T(8,128)(2,1)} %get-tuple-element.9.own), channel_id=1, source_target_pairs={{0,32},{32,64},{64,96},{96,128},{128,160},{160,192},{192,224},{224... | collective-permute-start | bytes 835592 | tf_op jit(solution)/shard_map/ppermute | solution.py:265
  8.4 0.1 collective-permute-start.2
  8.5 0.8 constant_dynamic-update-slice_fusion.4
  9.3 9.1 %shard_map.92.n_ref = bf16[4096,512]{1,0:T(8,128)(2,1)} custom-call(bf16[64,64,512]{2,1,0:T(8,128)(2,1)} %bitcast.55, s32[1,512]{1,0:T(1,128)} %bitcast.71, s32[1,64]{1,0:T(1,128)} %bitcast.79, f32[1,64]{1,0:T(1,128)} %bitcast.83, f32[1,64]{1,0:T(1,128)} %bitcast.85), custom_call_target="tpu_custom_call" | custom-call | flops 30000000 | bytes 8388608 | tf_op jit(solution)/shard_map/pallas_call | solution.py:281
  18.4 0.0 collective-permute-done.4
  18.4 0.4 collective-permute-start.6
  18.7 0.0 collective-permute-done.5
  18.8 4.8 %collective-permute-done.6 = bf16[144,128]{1,0:T(8,128)(2,1)S(1)} collective-permute-done((bf16[144,128]{1,0:T(8,128)(2,1)S(1)}, bf16[144,128]{1,0:T(8,128)(2,1)S(1)}, u32[]{:S(2)}, u32[]{:S(2)}) %collective-permute-start.6) | collective-permute-done | bytes 36896 | tf_op jit(solution)/shard_map/ppermute | solution.py:274
  23.6 0.9 collective-permute-start.7
  24.5 4.3 %collective-permute-done.7 = bf16[4,144,128]{2,1,0:T(8,128)(2,1)S(1)} collective-permute-done((bf16[4,144,128]{2,1,0:T(8,128)(2,1)S(1)}, bf16[4,144,128]{2,1,0:T(8,128)(2,1)S(1)}, u32[]{:S(2)}, u32[]{:S(2)}) %collective-permute-start.7) | collective-permute-done | bytes 147488 | tf_op jit(solution)/shard_map/ppermute | solution.py:276
  28.9 0.6 copy.12
  29.5 0.3 copy.13
  29.8 0.8 copy.14.w2
  30.6 7.5 %shard_map.93 = bf16[32,64,512]{2,1,0:T(8,128)(2,1)} custom-call(bf16[4096,512]{1,0:T(8,128)(2,1)} %shard_map.92.n_ref, bf16[32,64]{1,0:T(8,128)(2,1)} %bitcast.68), custom_call_target="tpu_custom_call" | custom-call | flops 1073741824 | bytes 6291456 | tf_op jit(solution)/shard_map/pallas_call | solution.py:295
  38.1 4.4 %shard_map.94.base = f32[520,128]{1,0:T(8,128)} custom-call(bf16[272,512]{1,0:T(8,128)(2,1)} %get-tuple-element.9.own, bf16[2048,512]{1,0:T(8,128)(2,1)} %bitcast.56, bf16[256,512]{1,0:T(8,128)(2,1)} %copy.14.w2, s32[1,512]{1,0:T(1,128)} %bitcast.72), custom_call_target="tpu_custom_call" | custom-call | flops 838860800 | bytes 2906112 | tf_op jit(solution)/shard_map/pallas_call | solution.py:227
  42.5 0.0 collective-permute-done.back
  42.5 1.9 %collective-permute-start.1 = (bf16[272,512]{1,0:T(8,128)(2,1)S(1)}, bf16[272,512]{1,0:T(8,128)(2,1)S(1)}, u32[]{:S(2)}, u32[]{:S(2)}) collective-permute-start(bf16[272,512]{1,0:T(8,128)(2,1)S(1)} %collective-permute-done.back), channel_id=1, source_target_pairs={{0,32},{32,64},{64,96},{96,128},{128,160},{160,192},{192,224},{224... | collective-permute-start | bytes 835592 | tf_op jit(solution)/shard_map/ppermute | solution.py:265
  44.4 0.0 collective-permute-done.2.ahead
  44.4 2.1 %collective-permute-start.3 = (bf16[272,512]{1,0:T(8,128)(2,1)S(1)}, bf16[272,512]{1,0:T(8,128)(2,1)S(1)}, u32[]{:S(2)}, u32[]{:S(2)}) collective-permute-start(bf16[272,512]{1,0:T(8,128)(2,1)S(1)} %collective-permute-done.2.ahead), channel_id=1, source_target_pairs={{0,224},{32,0},{64,32},{96,64},{128,96},{160,128},{192,160},{224,1... | collective-permute-start | bytes 835592 | tf_op jit(solution)/shard_map/ppermute | solution.py:266
  46.6 6.1 %shard_map.99 = f32[2,520,128]{2,1,0:T(8,128)} custom-call(bf16[272,512]{1,0:T(8,128)(2,1)} %copy-done.11, bf16[272,512]{1,0:T(8,128)(2,1)} %copy-done.12, bf16[2048,512]{1,0:T(8,128)(2,1)} %bitcast.57, bf16[256,512]{1,0:T(8,128)(2,1)} %copy.14.w2, s32[1,512]{1,0:T(1,128)} %bitcast.73), custom_call_target="tpu_custom_call" | custom-call | flops 1677721600 | bytes 3450880 | tf_op jit(solution)/shard_map/pallas_call | solution.py:227
  52.7 1.8 %slice_bitcast_fusion.4 = (f32[520,128]{1,0:T(8,128)S(1)}, f32[520,128]{1,0:T(8,128)}) fusion(f32[2,520,128]{2,1,0:T(8,128)} %shard_map.99), kind=kLoop, calls=%fused_computation.4 | loop fusion | bytes 1064960 | tf_op jit(solution)/shard_map/squeeze | solution.py:319
  54.5 3.4 %collective-permute-start.11 = (bf16[272,512]{1,0:T(8,128)(2,1)S(1)}, bf16[272,512]{1,0:T(8,128)(2,1)S(1)}, u32[]{:S(2)}, u32[]{:S(2)}) collective-permute-start(bf16[272,512]{1,0:T(8,128)(2,1)S(1)} %collective-permute-done.3.ahead), channel_id=1, source_target_pairs={{0,224},{32,0},{64,32},{96,64},{128,96},{160,128},{192,160},{224,1... | collective-permute-start | bytes 835592 | tf_op jit(solution)/shard_map/ppermute | solution.py:266
  57.9 0.7 copy-done.13
  58.6 6.0 %shard_map.95 = (f32[2,520,128]{2,1,0:T(8,128)}, f32[520,128]{1,0:T(8,128)}) custom-call(bf16[272,512]{1,0:T(8,128)(2,1)} %copy-done.13, bf16[272,512]{1,0:T(8,128)(2,1)} %copy-done.14, f32[520,128]{1,0:T(8,128)} %shard_map.94.base, bf16[2048,512]{1,0:T(8,128)(2,1)} %bitcast.58, bf16[256,512]{1,0:T(8,128)(2,1)} %copy.14.w2, s32[1,512]{1,0:T(1,128)} %bitcast.74), custom_call_target="tpu_custom_call" | custom-call | flops 1677721600 | bytes 3983360 | tf_op jit(solution)/shard_map/pallas_call | solution.py:227
  64.6 1.8 %slice_bitcast_fusion.10 = (f32[520,128]{1,0:T(8,128)S(1)}, f32[520,128]{1,0:T(8,128)}) fusion(f32[2,520,128]{2,1,0:T(8,128)} %get-tuple-element.11), kind=kLoop, calls=%fused_computation.10 | loop fusion | bytes 1064960 | tf_op jit(solution)/shard_map/squeeze | solution.py:320
  66.4 0.0 collective-permute-start.8
  66.4 0.0 collective-permute-done.11.ahead
  66.4 1.4 %collective-permute-start.12 = (bf16[144,512]{1,0:T(8,128)(2,1)S(1)}, bf16[144,512]{1,0:T(8,128)(2,1)S(1)}, u32[]{:S(2)}, u32[]{:S(2)}) collective-permute-start(bf16[144,512]{1,0:T(8,128)(2,1)S(1)} %slice.67), channel_id=1, source_target_pairs={{0,224},{32,0},{64,32},{96,64},{128,96},{160,128},{192,160},{224,1... | collective-permute-start | bytes 442376 | tf_op jit(solution)/shard_map/ppermute | solution.py:270
  67.8 0.0 collective-permute-done.9.back
  67.9 0.8 collective-permute-start.10
  68.6 6.1 %shard_map.100 = f32[2,520,128]{2,1,0:T(8,128)} custom-call(bf16[272,512]{1,0:T(8,128)(2,1)} %copy-done.10, bf16[272,512]{1,0:T(8,128)(2,1)} %copy-done.9, bf16[2048,512]{1,0:T(8,128)(2,1)} %bitcast.59, bf16[256,512]{1,0:T(8,128)(2,1)} %copy.14.w2, s32[1,512]{1,0:T(1,128)} %bitcast.75), custom_call_target="tpu_custom_call" | custom-call | flops 1677721600 | bytes 3450880 | tf_op jit(solution)/shard_map/pallas_call | solution.py:227
  74.8 1.8 %slice_bitcast_fusion.2 = (f32[520,128]{1,0:T(8,128)S(1)}, f32[520,128]{1,0:T(8,128)}) fusion(f32[2,520,128]{2,1,0:T(8,128)} %shard_map.100), kind=kLoop, calls=%fused_computation.2 | loop fusion | bytes 1064960 | tf_op jit(solution)/shard_map/squeeze | solution.py:321
  76.5 0.1 collective-permute-start.17
  76.7 0.0 collective-permute-done.12.second
  76.7 0.6 copy-done.8
  77.3 0.1 copy-done.6
  77.4 4.6 %shard_map.96 = f32[2,520,128]{2,1,0:T(8,128)} custom-call(bf16[128,512]{1,0:T(8,128)(2,1)} %copy-done.8, bf16[144,512]{1,0:T(8,128)(2,1)} %copy-done.6, f32[520,128]{1,0:T(8,128)} %get-tuple-element.12.rest, bf16[2048,512]{1,0:T(8,128)(2,1)} %bitcast.60, bf16[256,512]{1,0:T(8,128)(2,1)} %copy.14.w2, s32[1,512]{1,0:T(1,128)} %bitcast.76), custom_call_target="tpu_custom_call" | custom-call | flops 838860800 | bytes 3438592 | tf_op jit(solution)/shard_map/pallas_call | solution.py:227
  81.9 1.8 %slice_bitcast_fusion.8 = (f32[520,128]{1,0:T(8,128)S(1)}, f32[520,128]{1,0:T(8,128)}) fusion(f32[2,520,128]{2,1,0:T(8,128)} %shard_map.96), kind=kLoop, calls=%fused_computation.8 | loop fusion | bytes 1064960 | tf_op jit(solution)/shard_map/squeeze | solution.py:322
  83.7 0.4 collective-permute-start.13
  84.1 0.0 collective-permute-done.17.got_b
  84.1 0.7 copy-done
  84.8 0.1 copy-done.2
  84.9 2.1 %shard_map.101 = f32[2,520,128]{2,1,0:T(8,128)} custom-call(f32[520,128]{1,0:T(8,128)} %get-tuple-element.24.keep_a, f32[520,128]{1,0:T(8,128)} %copy-done, f32[520,128]{1,0:T(8,128)} %get-tuple-element.22.keep_b, f32[520,128]{1,0:T(8,128)} %copy-done.2), custom_call_target="tpu_custom_call" | custom-call | bytes 1597440 | tf_op jit(solution)/shard_map/pallas_call | solution.py:227
  87.0 1.8 %slice_bitcast_fusion = (f32[520,128]{1,0:T(8,128)S(1)}, f32[520,128]{1,0:T(8,128)}) fusion(f32[2,520,128]{2,1,0:T(8,128)} %shard_map.101), kind=kLoop, calls=%fused_computation | loop fusion | bytes 1064960 | tf_op jit(solution)/shard_map/squeeze | solution.py:325
  88.7 1.4 %collective-permute-start.18 = (f32[520,128]{1,0:T(8,128)S(1)}, f32[520,128]{1,0:T(8,128)S(1)}, u32[]{:S(2)}, u32[]{:S(2)}) collective-permute-start(f32[520,128]{1,0:T(8,128)S(1)} %get-tuple-element.19), channel_id=1, source_target_pairs={{0,16},{8,24},{16,0},{24,8},{1,17},{9,25},{17,1},{25,9},{2,18},{10... | collective-permute-start | bytes 798728 | tf_op jit(solution)/shard_map/ppermute | solution.py:325
  90.2 0.0 collective-permute-done.13.got_b
  90.2 0.7 copy-done.1
  90.9 0.1 copy-done.3
  91.0 2.1 %shard_map.97 = f32[2,520,128]{2,1,0:T(8,128)} custom-call(f32[520,128]{1,0:T(8,128)} %get-tuple-element.18.keep_a, f32[520,128]{1,0:T(8,128)} %copy-done.1, f32[520,128]{1,0:T(8,128)} %get-tuple-element.16.keep_b, f32[520,128]{1,0:T(8,128)} %copy-done.3), custom_call_target="tpu_custom_call" | custom-call | bytes 1597440 | tf_op jit(solution)/shard_map/pallas_call | solution.py:227
  93.0 1.8 %slice_bitcast_fusion.6 = (f32[520,128]{1,0:T(8,128)S(1)}, f32[520,128]{1,0:T(8,128)}) fusion(f32[2,520,128]{2,1,0:T(8,128)} %shard_map.97), kind=kLoop, calls=%fused_computation.6 | loop fusion | bytes 1064960 | tf_op jit(solution)/shard_map/squeeze | solution.py:326
  94.8 2.1 %collective-permute-start.14 = (f32[520,128]{1,0:T(8,128)S(1)}, f32[520,128]{1,0:T(8,128)S(1)}, u32[]{:S(2)}, u32[]{:S(2)}) collective-permute-start(f32[520,128]{1,0:T(8,128)S(1)} %get-tuple-element.13), channel_id=1, source_target_pairs={{0,16},{8,24},{16,0},{24,8},{1,17},{9,25},{17,1},{25,9},{2,18},{10... | collective-permute-start | bytes 798728 | tf_op jit(solution)/shard_map/ppermute | solution.py:326
  96.9 1.8 %collective-permute-done.18.got = f32[520,128]{1,0:T(8,128)S(1)} collective-permute-done((f32[520,128]{1,0:T(8,128)S(1)}, f32[520,128]{1,0:T(8,128)S(1)}, u32[]{:S(2)}, u32[]{:S(2)}) %collective-permute-start.18) | collective-permute-done | bytes 266272 | tf_op jit(solution)/shard_map/ppermute | solution.py:325
  98.7 0.7 copy-done.4
  99.4 1.9 %shard_map.102 = bf16[64,8,128]{2,1,0:T(8,128)(2,1)} custom-call(f32[520,128]{1,0:T(8,128)} %get-tuple-element.20.keep, f32[520,128]{1,0:T(8,128)} %copy-done.4, s32[1,64]{1,0:T(1,128)} %bitcast.80, f32[1,128]{1,0:T(1,128)} %bitcast.86), custom_call_target="tpu_custom_call" | custom-call | bytes 664320 | tf_op jit(solution)/shard_map/pallas_call | solution.py:227
  101.3 5.8 %collective-permute-start.19 = (bf16[64,8,128]{2,1,0:T(8,128)(2,1)}, bf16[64,8,128]{2,1,0:T(8,128)(2,1)S(1)}, u32[]{:S(2)}, u32[]{:S(2)}) collective-permute-start(bf16[64,8,128]{2,1,0:T(8,128)(2,1)} %shard_map.102), channel_id=1, source_target_pairs={{0,32},{8,96},{16,160},{24,224},{32,0},{40,64},{48,128},{56,192},{... | collective-permute-start | bytes 393224 | tf_op jit(solution)/shard_map/ppermute | solution.py:337
  107.2 0.7 copy-done.5
  107.9 1.9 %shard_map.98 = bf16[64,8,128]{2,1,0:T(8,128)(2,1)} custom-call(f32[520,128]{1,0:T(8,128)} %get-tuple-element.14.keep, f32[520,128]{1,0:T(8,128)} %copy-done.5, s32[1,64]{1,0:T(1,128)} %bitcast.81, f32[1,128]{1,0:T(1,128)} %bitcast.87), custom_call_target="tpu_custom_call" | custom-call | bytes 664320 | tf_op jit(solution)/shard_map/pallas_call | solution.py:227
  109.8 5.3 %collective-permute-start.15 = (bf16[64,8,128]{2,1,0:T(8,128)(2,1)}, bf16[64,8,128]{2,1,0:T(8,128)(2,1)S(1)}, u32[]{:S(2)}, u32[]{:S(2)}) collective-permute-start(bf16[64,8,128]{2,1,0:T(8,128)(2,1)} %shard_map.98), channel_id=1, source_target_pairs={{0,0},{8,64},{16,128},{24,192},{32,32},{40,96},{48,160},{56,224},{... | collective-permute-start | bytes 393224 | tf_op jit(solution)/shard_map/ppermute | solution.py:338
  115.2 0.0 collective-permute-done.19
  115.2 10.3 %collective-permute-done.15 = bf16[64,8,128]{2,1,0:T(8,128)(2,1)S(1)} collective-permute-done((bf16[64,8,128]{2,1,0:T(8,128)(2,1)}, bf16[64,8,128]{2,1,0:T(8,128)(2,1)S(1)}, u32[]{:S(2)}, u32[]{:S(2)}) %collective-permute-start.15) | collective-permute-done | bytes 131104 | tf_op jit(solution)/shard_map/ppermute | solution.py:338
  125.4 0.7 maximum_select_fusion
  (39 shorter events, 0.2 us)
Async XLA Ops:
  3.2 15.2 %collective-permute-start.4 = (bf16[144,128]{1,0:T(8,128)(2,1)}, bf16[144,128]{1,0:T(8,128)(2,1)S(1)}, u32[]{:S(2)}, u32[]{:S(2)}) collective-permute-start(bf16[144,128]{1,0:T(8,128)(2,1)} %get-tuple-element.10), channel_id=1, source_target_pairs={{0,1},{1,2},{2,3},{3,0},{4,5},{5,6},{6,7},{7,4},{8,9},{9,10},{10,1... | collective-permute-start | bytes 110600 | tf_op jit(solution)/shard_map/ppermute | solution.py:272
  4.8 13.9 %collective-permute-start.5 = (bf16[144,128]{1,0:T(8,128)(2,1)}, bf16[144,128]{1,0:T(8,128)(2,1)S(1)}, u32[]{:S(2)}, u32[]{:S(2)}) collective-permute-start(bf16[144,128]{1,0:T(8,128)(2,1)} %get-tuple-element.10), channel_id=1, source_target_pairs={{0,3},{1,0},{2,1},{3,2},{4,7},{5,4},{6,5},{7,6},{8,11},{9,8},{10,9... | collective-permute-start | bytes 110600 | tf_op jit(solution)/shard_map/ppermute | solution.py:273
  6.5 36.0 %collective-permute-start = (bf16[272,512]{1,0:T(8,128)(2,1)}, bf16[272,512]{1,0:T(8,128)(2,1)S(1)}, u32[]{:S(2)}, u32[]{:S(2)}) collective-permute-start(bf16[272,512]{1,0:T(8,128)(2,1)} %get-tuple-element.9.own), channel_id=1, source_target_pairs={{0,32},{32,64},{64,96},{96,128},{128,160},{160,192},{192,224},{224... | collective-permute-start | bytes 835592 | tf_op jit(solution)/shard_map/ppermute | solution.py:265
  8.4 36.0 %collective-permute-start.2 = (bf16[272,512]{1,0:T(8,128)(2,1)}, bf16[272,512]{1,0:T(8,128)(2,1)S(1)}, u32[]{:S(2)}, u32[]{:S(2)}) collective-permute-start(bf16[272,512]{1,0:T(8,128)(2,1)} %get-tuple-element.9.own), channel_id=1, source_target_pairs={{0,224},{32,0},{64,32},{96,64},{128,96},{160,128},{192,160},{224,1... | collective-permute-start | bytes 835592 | tf_op jit(solution)/shard_map/ppermute | solution.py:266
  9.3 14.3 %copy-start.7 = (bf16[144,128]{1,0:T(8,128)(2,1)S(1)}, bf16[144,128]{1,0:T(8,128)(2,1)}, u32[]{:S(2)}) copy-start(bf16[144,128]{1,0:T(8,128)(2,1)} %get-tuple-element.10) | copy-start | bytes 110596
  18.4 5.2 %collective-permute-start.6 = (bf16[144,128]{1,0:T(8,128)(2,1)S(1)}, bf16[144,128]{1,0:T(8,128)(2,1)S(1)}, u32[]{:S(2)}, u32[]{:S(2)}) collective-permute-start(bf16[144,128]{1,0:T(8,128)(2,1)S(1)} %collective-permute-done.4), channel_id=1, source_target_pairs={{0,1},{1,2},{2,3},{3,0},{4,5},{5,6},{6,7},{7,4},{8,9},{9,10},{10,1... | collective-permute-start | bytes 110600 | tf_op jit(solution)/shard_map/ppermute | solution.py:274
  23.6 5.2 %collective-permute-start.7 = (bf16[4,144,128]{2,1,0:T(8,128)(2,1)S(1)}, bf16[4,144,128]{2,1,0:T(8,128)(2,1)S(1)}, u32[]{:S(2)}, u32[]{:S(2)}) collective-permute-start(bf16[4,144,128]{2,1,0:T(8,128)(2,1)S(1)} %pad_maximum_fusion), channel_id=1, source_target_pairs={{0,4},{1,5},{2,6},{3,7},{4,0},{5,1},{6,2},{7,3},{8,12},{9,13},{10,... | collective-permute-start | bytes 442376 | tf_op jit(solution)/shard_map/ppermute | solution.py:276
  42.5 4.1 %copy-start.11 = (bf16[272,512]{1,0:T(8,128)(2,1)}, bf16[272,512]{1,0:T(8,128)(2,1)S(1)}, u32[]{:S(2)}) copy-start(bf16[272,512]{1,0:T(8,128)(2,1)S(1)} %collective-permute-done.back) | copy-start | bytes 835588
  42.5 15.3 %collective-permute-start.1 = (bf16[272,512]{1,0:T(8,128)(2,1)S(1)}, bf16[272,512]{1,0:T(8,128)(2,1)S(1)}, u32[]{:S(2)}, u32[]{:S(2)}) collective-permute-start(bf16[272,512]{1,0:T(8,128)(2,1)S(1)} %collective-permute-done.back), channel_id=1, source_target_pairs={{0,32},{32,64},{64,96},{96,128},{128,160},{160,192},{192,224},{224... | collective-permute-start | bytes 835592 | tf_op jit(solution)/shard_map/ppermute | solution.py:265
  44.4 2.1 %copy-start.12 = (bf16[272,512]{1,0:T(8,128)(2,1)}, bf16[272,512]{1,0:T(8,128)(2,1)S(1)}, u32[]{:S(2)}) copy-start(bf16[272,512]{1,0:T(8,128)(2,1)S(1)} %collective-permute-done.2.ahead) | copy-start | bytes 835588
  44.4 10.0 %collective-permute-start.3 = (bf16[272,512]{1,0:T(8,128)(2,1)S(1)}, bf16[272,512]{1,0:T(8,128)(2,1)S(1)}, u32[]{:S(2)}, u32[]{:S(2)}) collective-permute-start(bf16[272,512]{1,0:T(8,128)(2,1)S(1)} %collective-permute-done.2.ahead), channel_id=1, source_target_pairs={{0,224},{32,0},{64,32},{96,64},{128,96},{160,128},{192,160},{224,1... | collective-permute-start | bytes 835592 | tf_op jit(solution)/shard_map/ppermute | solution.py:266
  54.5 29.6 %collective-permute-start.16 = (f32[520,128]{1,0:T(8,128)S(1)}, f32[520,128]{1,0:T(8,128)S(1)}, u32[]{:S(2)}, u32[]{:S(2)}) collective-permute-start(f32[520,128]{1,0:T(8,128)S(1)} %get-tuple-element.23), channel_id=1, source_target_pairs={{0,8},{8,0},{16,24},{24,16},{1,9},{9,1},{17,25},{25,17},{2,10},{10... | collective-permute-start | bytes 798728 | tf_op jit(solution)/shard_map/ppermute | solution.py:319
  54.5 3.4 %copy-start.14 = (bf16[272,512]{1,0:T(8,128)(2,1)}, bf16[272,512]{1,0:T(8,128)(2,1)S(1)}, u32[]{:S(2)}) copy-start(bf16[272,512]{1,0:T(8,128)(2,1)S(1)} %collective-permute-done.3.ahead) | copy-start | bytes 835588
  54.5 12.0 %collective-permute-start.11 = (bf16[272,512]{1,0:T(8,128)(2,1)S(1)}, bf16[272,512]{1,0:T(8,128)(2,1)S(1)}, u32[]{:S(2)}, u32[]{:S(2)}) collective-permute-start(bf16[272,512]{1,0:T(8,128)(2,1)S(1)} %collective-permute-done.3.ahead), channel_id=1, source_target_pairs={{0,224},{32,0},{64,32},{96,64},{128,96},{160,128},{192,160},{224,1... | collective-permute-start | bytes 835592 | tf_op jit(solution)/shard_map/ppermute | solution.py:266
  57.9 0.7 copy-start.13
  57.9 10.0 %collective-permute-start.9 = (bf16[272,512]{1,0:T(8,128)(2,1)S(1)}, bf16[272,512]{1,0:T(8,128)(2,1)S(1)}, u32[]{:S(2)}, u32[]{:S(2)}) collective-permute-start(bf16[272,512]{1,0:T(8,128)(2,1)S(1)} %collective-permute-done.1.back), channel_id=1, source_target_pairs={{0,32},{32,64},{64,96},{96,128},{128,160},{160,192},{192,224},{224... | collective-permute-start | bytes 835592 | tf_op jit(solution)/shard_map/ppermute | solution.py:265
  66.4 23.7 %collective-permute-start.8 = (f32[520,128]{1,0:T(8,128)S(1)}, f32[520,128]{1,0:T(8,128)S(1)}, u32[]{:S(2)}, u32[]{:S(2)}) collective-permute-start(f32[520,128]{1,0:T(8,128)S(1)} %get-tuple-element.17), channel_id=1, source_target_pairs={{0,8},{8,0},{16,24},{24,16},{1,9},{9,1},{17,25},{25,17},{2,10},{10... | collective-permute-start | bytes 798728 | tf_op jit(solution)/shard_map/ppermute | solution.py:320
  66.4 2.2 %copy-start.9 = (bf16[272,512]{1,0:T(8,128)(2,1)}, bf16[272,512]{1,0:T(8,128)(2,1)S(1)}, u32[]{:S(2)}) copy-start(bf16[272,512]{1,0:T(8,128)(2,1)S(1)} %collective-permute-done.11.ahead) | copy-start | bytes 835588
  66.4 10.2 %collective-permute-start.12 = (bf16[144,512]{1,0:T(8,128)(2,1)S(1)}, bf16[144,512]{1,0:T(8,128)(2,1)S(1)}, u32[]{:S(2)}, u32[]{:S(2)}) collective-permute-start(bf16[144,512]{1,0:T(8,128)(2,1)S(1)} %slice.67), channel_id=1, source_target_pairs={{0,224},{32,0},{64,32},{96,64},{128,96},{160,128},{192,160},{224,1... | collective-permute-start | bytes 442376 | tf_op jit(solution)/shard_map/ppermute | solution.py:270
  67.8 0.8 copy-start.10
  67.9 8.8 %collective-permute-start.10 = (bf16[128,512]{1,0:T(8,128)(2,1)S(1)}, bf16[128,512]{1,0:T(8,128)(2,1)S(1)}, u32[]{:S(2)}, u32[]{:S(2)}) collective-permute-start(bf16[128,512]{1,0:T(8,128)(2,1)S(1)} %slice.66), channel_id=1, source_target_pairs={{0,32},{32,64},{64,96},{96,128},{128,160},{160,192},{192,224},{224... | collective-permute-start | bytes 393224 | tf_op jit(solution)/shard_map/ppermute | solution.py:269
  76.5 7.6 %collective-permute-start.17 = (f32[520,128]{1,0:T(8,128)S(1)}, f32[520,128]{1,0:T(8,128)S(1)}, u32[]{:S(2)}, u32[]{:S(2)}) collective-permute-start(f32[520,128]{1,0:T(8,128)S(1)} %get-tuple-element.21), channel_id=1, source_target_pairs={{0,8},{8,0},{16,24},{24,16},{1,9},{9,1},{17,25},{25,17},{2,10},{10... | collective-permute-start | bytes 798728 | tf_op jit(solution)/shard_map/ppermute | solution.py:321
  76.7 0.6 copy-start.8
  76.7 0.7 copy-start.6
  83.7 6.5 %collective-permute-start.13 = (f32[520,128]{1,0:T(8,128)S(1)}, f32[520,128]{1,0:T(8,128)S(1)}, u32[]{:S(2)}, u32[]{:S(2)}) collective-permute-start(f32[520,128]{1,0:T(8,128)S(1)} %get-tuple-element.15), channel_id=1, source_target_pairs={{0,8},{8,0},{16,24},{24,16},{1,9},{9,1},{17,25},{25,17},{2,10},{10... | collective-permute-start | bytes 798728 | tf_op jit(solution)/shard_map/ppermute | solution.py:322
  84.1 0.7 copy-start
  84.1 0.8 copy-start.2
  88.7 9.9 %collective-permute-start.18 = (f32[520,128]{1,0:T(8,128)S(1)}, f32[520,128]{1,0:T(8,128)S(1)}, u32[]{:S(2)}, u32[]{:S(2)}) collective-permute-start(f32[520,128]{1,0:T(8,128)S(1)} %get-tuple-element.19), channel_id=1, source_target_pairs={{0,16},{8,24},{16,0},{24,8},{1,17},{9,25},{17,1},{25,9},{2,18},{10... | collective-permute-start | bytes 798728 | tf_op jit(solution)/shard_map/ppermute | solution.py:325
  90.1 0.7 copy-start.1
  90.2 0.8 copy-start.3
  94.8 12.4 %collective-permute-start.14 = (f32[520,128]{1,0:T(8,128)S(1)}, f32[520,128]{1,0:T(8,128)S(1)}, u32[]{:S(2)}, u32[]{:S(2)}) collective-permute-start(f32[520,128]{1,0:T(8,128)S(1)} %get-tuple-element.13), channel_id=1, source_target_pairs={{0,16},{8,24},{16,0},{24,8},{1,17},{9,25},{17,1},{25,9},{2,18},{10... | collective-permute-start | bytes 798728 | tf_op jit(solution)/shard_map/ppermute | solution.py:326
  98.7 0.7 copy-start.4
  101.3 13.8 %collective-permute-start.19 = (bf16[64,8,128]{2,1,0:T(8,128)(2,1)}, bf16[64,8,128]{2,1,0:T(8,128)(2,1)S(1)}, u32[]{:S(2)}, u32[]{:S(2)}) collective-permute-start(bf16[64,8,128]{2,1,0:T(8,128)(2,1)} %shard_map.102), channel_id=1, source_target_pairs={{0,32},{8,96},{16,160},{24,224},{32,0},{40,64},{48,128},{56,192},{... | collective-permute-start | bytes 393224 | tf_op jit(solution)/shard_map/ppermute | solution.py:337
  107.2 0.7 copy-start.5
  109.8 15.6 %collective-permute-start.15 = (bf16[64,8,128]{2,1,0:T(8,128)(2,1)}, bf16[64,8,128]{2,1,0:T(8,128)(2,1)S(1)}, u32[]{:S(2)}, u32[]{:S(2)}) collective-permute-start(bf16[64,8,128]{2,1,0:T(8,128)(2,1)} %shard_map.98), channel_id=1, source_target_pairs={{0,0},{8,64},{16,128},{24,192},{32,32},{40,96},{48,160},{56,224},{... | collective-permute-start | bytes 393224 | tf_op jit(solution)/shard_map/ppermute | solution.py:338

commit v2 on v1

v2 whole, which is shorter than its diff:
```python
import functools

import jax
import jax.numpy as jnp
from jax import lax
from jax.experimental import pallas as pl
from jax.experimental.pallas import tpu as pltpu
from jax.sharding import PartitionSpec as P


F32 = jnp.float32
BF16 = jnp.bfloat16
VMEM = pl.BlockSpec(memory_space=pltpu.VMEM)
HBM = pl.BlockSpec(memory_space=pltpu.HBM)

S = 512
N = 64
M = 64
C = 32
Z = 128
T = 8
ROWS = N * T
EXTRA = 8


def column_of(row):
    n = row.shape[1]
    r = lax.broadcasted_iota(jnp.int32, (n, n), 0)
    c = lax.broadcasted_iota(jnp.int32, (n, n), 1)
    return jnp.sum(jnp.where(r == c, jnp.broadcast_to(row, (n, n)), 0.0), axis=1, keepdims=True)


def normalize(x, gain, bias):
    values = x.astype(F32)
    center = values - jnp.mean(values, axis=1, keepdims=True)
    spread = jnp.mean(center * center, axis=1, keepdims=True)
    return center * lax.rsqrt(spread + 1e-05) * gain[None] + bias[None]


def tokens_of(tok_ref, start, count):
    token = tok_ref[...].astype(F32)
    t_iota = lax.broadcasted_iota(jnp.int32, (count, N), 0)
    l_iota = lax.broadcasted_iota(jnp.int32, (count, N), 1)
    return jnp.sum(
        jnp.where(l_iota == t_iota + start, jnp.broadcast_to(token, (count, N)), 0.0), axis=1, keepdims=True
    )


def pack_kernel(wl_ref, wo_ref, out_ref):
    out_ref[0:Z, :] = wo_ref[...]
    out_ref[Z : Z + 16, :] = jnp.zeros((16, Z), BF16)
    out_ref[Z : Z + 4, 0:M] = wl_ref[...]


def stack_kernel(a, b, c, d, out):
    for i, ref in enumerate((a, b, c, d)):
        out[i] = ref[...]


def weight_kernel(near, far, wl_out, w2_out):
    packs = [near[i] for i in range(4)] + [far[i] for i in range(4)]
    for i in range(0, 8, 2):
        a, b = (packs[i + j][:Z, :].astype(F32).T.astype(BF16) for j in range(2))
        w2_out[:Z, i * 64 : i * 64 + 128] = jnp.concatenate([a[:, :64], b[:, :64]], axis=1)
        w2_out[Z:, i * 64 : i * 64 + 128] = jnp.concatenate([a[:, 64:], b[:, 64:]], axis=1)
    lefts = jnp.concatenate([pack[Z:, :M] for pack in packs], axis=0)
    r = lax.broadcasted_iota(jnp.int32, (C, 128), 0)
    c = lax.broadcasted_iota(jnp.int32, (C, 128), 1)
    pick = c == r // 4 * 16 + r % 2 * 2 + r // 2 % 2
    wl_out[...] = jnp.dot(pick.astype(F32).astype(BF16), lefts, preferred_element_type=F32).astype(BF16)


def right_kernel(x_ref, row_ref, tok_ref, gain_ref, bias_ref, wr_ref, out_ref, buf, sem):
    k = lax.axis_index("chan")
    copy = pltpu.make_async_copy(x_ref.at[pl.ds(k * T, T)], buf, sem)
    copy.start()
    gain = column_of(gain_ref[...])
    bias = column_of(bias_ref[...])
    token_col = tokens_of(tok_ref, k * T, T)
    weight = token_col * row_ref[...].astype(F32)
    wr = wr_ref[...]
    pad = jnp.concatenate([jnp.broadcast_to(token_col, (T, S)), jnp.zeros((T, S), F32)], axis=0)
    out_ref[T * C :, :] = pad.astype(BF16)
    copy.wait()
    for t in range(T):
        normed = normalize(buf[t : t + 1], gain, bias).astype(BF16)
        part = jnp.dot(wr, normed[0], preferred_element_type=F32)
        out_ref[t * C : (t + 1) * C, :] = (part * weight[t : t + 1]).astype(BF16)


def norm_kernel(half, x_ref, gain_ref, bias_ref, out_ref, buf, sems):
    copies = [
        pltpu.make_async_copy(x_ref.at[pl.ds(half * N // 2 + g * T, T)], buf.at[g], sems.at[g])
        for g in range(N // 2 // T)
    ]
    for copy in copies:
        copy.start()
    gain = column_of(gain_ref[...])
    bias = column_of(bias_ref[...])
    for g, copy in enumerate(copies):
        copy.wait()

        def one(t, carry):
            normed = normalize(buf[g, pl.ds(t, 1)], gain, bias)
            out_ref[pl.ds(pl.multiple_of((g * T + t) * M, M), M), :] = normed[0].astype(BF16)
            return carry

        lax.fori_loop(0, T, one, 0)


def left_kernel(n_a, n_b, wl_ref, row_ref, tok_ref, out_ref):
    rep = (
        lax.broadcasted_iota(jnp.int32, (C * T, C), 0) // T == lax.broadcasted_iota(jnp.int32, (C * T, C), 1)
    ).astype(F32).astype(BF16)
    tile = (
        lax.broadcasted_iota(jnp.int32, (M, T * M), 0) == lax.broadcasted_iota(jnp.int32, (M, T * M), 1) % M
    ).astype(F32).astype(BF16)
    tall = jnp.dot(rep, wl_ref[...], preferred_element_type=F32).astype(BF16)
    full = jnp.dot(tall, tile, preferred_element_type=F32)
    own = (
        lax.broadcasted_iota(jnp.int32, (C * T, T * M), 0) % T
        == lax.broadcasted_iota(jnp.int32, (C * T, T * M), 1) // M
    )
    wide = jnp.where(own, full, 0.0).astype(BF16)
    rows = row_ref[...].astype(F32)
    for g in range(N // T):
        weight = tokens_of(tok_ref, g * T, T) * rows
        n_ref, at = (n_a, g) if g < N // T // 2 else (n_b, g - N // T // 2)
        part = jnp.dot(wide, n_ref[at * T * M : (at + 1) * T * M, :], preferred_element_type=F32)
        out_ref[:, g * T : (g + 1) * T, :] = (part.reshape(C, T, S) * weight[None]).astype(BF16)


def pair_blocks(blocks, lf_ref, w2_ref, row_ref, spread):
    rhs = jnp.concatenate([rows for rows, _, _ in blocks], axis=0) if len(blocks) > 1 else blocks[0][0]
    for n in range(8):
        part = lax.dot_general(
            rhs, lf_ref[n * 256 : (n + 1) * 256, :], (((1,), (1,)), ((), ())), preferred_element_type=F32
        ).astype(BF16)
        for b in range(len(blocks)):
            for t in range(T):
                for u in range(2):
                    hi = n * 2 + u
                    spread[b * T // 2 + t // 2, hi * C : (hi + 1) * C, (t % 2) * 128 : (t % 2) * 128 + 128] = part[
                        (b * T + t) * C : (b * T + t + 1) * C, u * 128 : (u + 1) * 128
                    ]
    low = lax.broadcasted_iota(jnp.int32, (Z, 128), 1) < N
    rows_used = jnp.sum(row_ref[...].astype(F32), axis=1, keepdims=True)
    lane = lax.broadcasted_iota(jnp.int32, (EXTRA, Z), 1)
    w2 = w2_ref[...]
    for b, (_, extra, store) in enumerate(blocks):
        for p in range(T // 2):
            both = jnp.dot(w2, spread[b * T // 2 + p], preferred_element_type=F32)
            x0, y0 = both[:Z, :128], both[Z:, :128]
            x1, y1 = both[:Z, 128:], both[Z:, 128:]
            pair = jnp.where(low, x0, y1) + pltpu.roll(jnp.where(low, x1, y0), N, 1)
            flat = pair.T
            store(pl.ds(2 * p, N, stride=T), flat[:N])
            store(pl.ds(2 * p + 1, N, stride=T), flat[N:])
        mask = jnp.broadcast_to(extra.astype(F32)[:EXTRA, :1], (EXTRA, Z))
        store(pl.ds(ROWS, EXTRA), jnp.where(lane < N, jnp.broadcast_to(rows_used, (EXTRA, Z)), mask))


def whole(ref):
    return ref[: T * C, :], ref[T * C :, :]


def halves(first, second):
    return jnp.concatenate([first[...], second[:128, :]], axis=0), second[128:, :]


def to(ref):
    def store(where, value):
        ref[where, :] = value

    return store


def to_either(kept, keep, send):
    def store(where, value):
        @pl.when(kept)
        def _():
            keep[where, :] = value

        @pl.when(jnp.logical_not(kept))
        def _():
            send[where, :] = value

    return store


def not_kept(kept):
    return jnp.logical_not(kept)


def core_kept(offset):
    block = lax.rem(lax.axis_index("row") + offset + 8, 8)
    return lax.rem(block // 2, 2) == lax.rem(lax.axis_index("col"), 2)


def x_kept(offset):
    block = lax.rem(lax.axis_index("row") + offset + 8, 8)
    return block // 4 == lax.axis_index("col") // 2


def first_kernel(own, lf, w2, row, out, spread):
    pair_blocks([whole(own) + (to(out),)], lf, w2, row, spread)


def two_kernel(offset, back, ahead, lf, w2, row, keep, send, spread):
    kept = core_kept(offset)
    pair_blocks(
        [
            whole(back) + (to_either(not_kept(kept), keep, send),),
            whole(ahead) + (to_either(kept, keep, send),),
        ],
        lf, w2, row, spread,
    )


def copy_either(kept, value, keep, send):
    @pl.when(kept)
    def _():
        keep[...] = value[...]

    @pl.when(jnp.logical_not(kept))
    def _():
        send[...] = value[...]


def mixed_kernel(back, ahead, base, lf, w2, row, keep, send, rest, spread):
    kept = core_kept(2)
    copy_either(not_kept(kept), base, keep, send)
    pair_blocks(
        [whole(back) + (to(rest),), whole(ahead) + (to_either(kept, keep, send),)], lf, w2, row, spread
    )


def last_kernel(first, second, rest, lf, w2, row, keep, send, spread):
    kept = core_kept(4)
    copy_either(not_kept(kept), rest, keep, send)
    pair_blocks([halves(first, second) + (to_either(kept, keep, send),)], lf, w2, row, spread)


def add_kernel(a_offsets, keep_a, got_a, keep_b, got_b, keep, send):
    first, second = a_offsets
    kept = jnp.where(core_kept(first), x_kept(first), x_kept(second))

    @pl.when(kept)
    def _():
        keep[...] = keep_a[...] + got_a[...]
        send[...] = keep_b[...] + got_b[...]

    @pl.when(jnp.logical_not(kept))
    def _():
        send[...] = keep_a[...] + got_a[...]
        keep[...] = keep_b[...] + got_b[...]


def final_kernel(keep, got, tok_ref, bias_ref, out):
    total = keep[...] + got[...]
    tail = total[ROWS:, :]
    rows_used = tail[0:1, 0:1]
    second = (tail[:, N : N + 1] > 0.0).astype(F32)
    first = column_of(tok_ref[...].astype(F32))
    count = jnp.maximum(rows_used[None] * first[:, :, None] * second[None], 1.0)
    pairs = total[:ROWS, :].reshape(N, T, Z)
    out[...] = ((pairs + bias_ref[...][None]) / count).astype(BF16)


def call(kernel, out, *args, specs=None, scratch=(), flops=0, limit=10):
    leaves = jax.tree.leaves(out)
    bytes_accessed = sum(a.size * a.dtype.itemsize for a in list(args) + leaves)
    return pl.pallas_call(
        kernel,
        out_shape=out,
        in_specs=specs or [VMEM] * len(args),
        out_specs=jax.tree.map(lambda _: VMEM, out),
        scratch_shapes=scratch,
        compiler_params=pltpu.CompilerParams(vmem_limit_bytes=limit << 20),
        cost_estimate=pl.CostEstimate(flops=flops, bytes_accessed=bytes_accessed, transcendentals=0),
    )(*args)


def shape(dims, dtype):
    return jax.ShapeDtypeStruct(dims, dtype)


def program(x, row_mask, token_mask, gain, bias, wl, wr, wo, out_bias):
    xt = pltpu.with_memory_space_constraint(x.transpose(1, 2, 0), pltpu.HBM)
    row = row_mask.reshape(1, S)
    tok = token_mask.reshape(1, N)
    gain, bias = gain.reshape(1, M), bias.reshape(1, M)

    ring = [[(i, (i + d) % 8) for i in range(8)] for d in (1, -1)]
    y_ring = {d: [(a * 4 + b, a * 4 + (b + d) % 4) for a in range(2) for b in range(4)] for d in (1, -1, 2)}
    x_swap = [(c, (c + 4) % 8) for c in range(8)]
    core_swap = [(0, 1), (1, 0), (2, 3), (3, 2)]
    xh_swap = [(0, 2), (1, 3), (2, 0), (3, 1)]

    pack = call(pack_kernel, shape((Z + 16, Z), BF16), wl.T, wo)
    up = lax.ppermute(pack, "chan", y_ring[1])
    down = lax.ppermute(pack, "chan", y_ring[-1])
    over = lax.ppermute(pack, "chan", y_ring[2])
    four = call(stack_kernel, shape((4, Z + 16, Z), BF16), pack, up, down, over, limit=4)
    other = lax.ppermute(four, "chan", x_swap)
    wl_all, w2 = call(weight_kernel, (shape((C, M), BF16), shape((2 * Z, 512), BF16)), four, other, limit=4)

    own = call(
        right_kernel, shape((T * C + 16, S), BF16), xt, row, tok, gain, bias, wr.T,
        specs=[HBM] + [VMEM] * 5,
        scratch=[pltpu.VMEM((T, M, S), BF16), pltpu.SemaphoreType.DMA(())],
        flops=20 << 20, limit=8,
    )

    ahead, back = own, own
    from_back, from_ahead = [], []
    for _ in range(3):
        back = lax.ppermute(back, "row", ring[0])
        ahead = lax.ppermute(ahead, "row", ring[1])
        from_back.append(back)
        from_ahead.append(ahead)
    half_a = lax.ppermute(back[:128], "row", ring[0])
    half_b = lax.ppermute(ahead[128:], "row", ring[1])

    normed = [
        call(
            functools.partial(norm_kernel, half), shape((N * M // 2, S), BF16), xt, gain, bias,
            specs=[HBM, VMEM, VMEM],
            scratch=[pltpu.VMEM((N // 2 // T, T, M, S), BF16), pltpu.SemaphoreType.DMA((N // 2 // T,))],
            flops=15 << 20, limit=8,
        )
        for half in range(2)
    ]
    left = call(left_kernel, shape((C, N, S), BF16), *normed, wl_all, row, tok, flops=1 << 30, limit=8)
    lf = left.reshape(C * N, S)

    block = shape((ROWS + EXTRA, Z), F32)
    pair = (block, block)
    one = 800 << 20
    shared = (lf, w2, row)

    def spread(n):
        return [pltpu.VMEM((n * T // 2, 512, 256), BF16)]

    p0 = call(first_kernel, block, own, *shared, scratch=spread(1), flops=one)
    k1, s1 = call(functools.partial(two_kernel, 1), pair, from_back[0], from_ahead[0], *shared, scratch=spread(2), flops=2 * one)
    k2, s2, rest = call(mixed_kernel, (block,) * 3, from_back[1], from_ahead[1], p0, *shared, scratch=spread(2), flops=2 * one)
    k3, s3 = call(functools.partial(two_kernel, 3), pair, from_back[2], from_ahead[2], *shared, scratch=spread(2), flops=2 * one)
    k4, s4 = call(last_kernel, pair, half_a, half_b, rest, *shared, scratch=spread(1), flops=one)

    e1 = lax.ppermute(s1, "col", core_swap)
    e2 = lax.ppermute(s2, "col", core_swap)
    e3 = lax.ppermute(s3, "col", core_swap)
    e4 = lax.ppermute(s4, "col", core_swap)
    odd, odd_sent = call(functools.partial(add_kernel, (1, -1)), pair, k1, e1, k3, e3)
    f1 = lax.ppermute(odd_sent, "col", xh_swap)
    even, even_sent = call(functools.partial(add_kernel, (0, 2)), pair, k2, e2, k4, e4)
    f2 = lax.ppermute(even_sent, "col", xh_swap)
    part = shape((N, T, Z), BF16)
    out_bias = out_bias.reshape(1, Z)
    y1 = call(final_kernel, part, odd, f1, tok, out_bias)
    y2 = call(final_kernel, part, even, f2, tok, out_bias)

    def home(p):
        return [(z * 4 + c, (2 * c + ((z % 2) ^ p)) * 4 + z // 2) for z in range(8) for c in range(4)]

    g1 = lax.ppermute(y1, ("row", "col"), home(1))
    g2 = lax.ppermute(y2, ("row", "col"), home(0))
    low_row = lax.axis_index("row") % 2 == 0
    return jnp.where(low_row, jnp.concatenate([g2, g1], 0), jnp.concatenate([g1, g2], 0))


def solution(mesh):
    in_specs = (
        P("col", "row", None),
        P("col"),
        P("row"),
        P(),
        P(),
        P(None, "chan"),
        P(),
        P("chan", None),
        P(),
    )
    out_specs = P("col", ("row", "chan"), None)
    return jax.shard_map(program, mesh=mesh, in_specs=in_specs, out_specs=out_specs, check_vma=False)
```

time: 127 us -> 88.1 us (0.69)
  Pallas kernels: 54.9 us -> 26.5 us
  local copies, waits for them, and re-layouts: 17.7 us -> 3.39 us
  starting transfers between devices: 31.4 us -> 33.5 us
    pallas_call x2 -> x0, Pallas kernels: 16.6 us -> none  [the longest x1 9.09 us: body(): pl.pallas_call(norm_kernel, grid=(N // T,), out_shape=shape((N * M, S), B...]
    pallas_call x10 -> x16, Pallas kernels: 38.3 us -> 26.5 us  [call(): pl.pallas_call(kernel, out_shape=out, in_specs=specs or [VMEM] * len(args...]
    squeeze x6 -> x0, local copies, waits for them, and re-layouts: 10.6 us -> none  [the longest x1 1.79 us: body(): e2 = lax.ppermute(p2[0], 'col', core_swap)]
    ppermute x20, starting transfers between devices: 31.4 us -> 33.5 us  [the longest x3 7.43 us: program(): ahead = lax.ppermute(ahead, 'row', ring[1])]
    unnamed x35 -> x22, local copies, waits for them, and re-layouts: 5.29 us -> 3.37 us
    reshape x3 -> x0, local copies, waits for them, and re-layouts: 1.72 us -> none  [the longest x2 1.12 us: body(): packs[:, :Z, :].reshape(8, 2, 64, Z).transpose(1, 3, 0, 2)]
  transfers between devices with their start and end apart: 20 -> 20, of which waited for: 4 -> 8; matrix products, arithmetic and copies ran while one was open for 11% -> 0% of each run, Pallas kernels for 41% -> 29%
where the time goes in v2:
time: 88.1 us; the launch traced here: 86.5 us
  starting transfers between devices  33.5 us (38%)
  Pallas kernels  26.5 us (30%)
  waiting for transfers between devices  22.1 us (25%)
  local copies, waits for them, and re-layouts  3.39 us (4%)
    pallas_call x16, Pallas kernels, call(): pl.pallas_call(kernel, out_shape=out, in_specs=specs or [VMEM] * len(args...  26.5 us
    ppermute x3, starting transfers between devices, program(): ahead = lax.ppermute(ahead, 'row', ring[1])  7.43 us
    ppermute x1, waiting for transfers between devices, program(): f1 = lax.ppermute(odd_sent, 'col', xh_swap)  7.06 us
    ppermute x1, starting transfers between devices, program(): g2 = lax.ppermute(y2, ('row', 'col'), home(0))  6.9 us
    ppermute x1, waiting for transfers between devices, program(): g2 = lax.ppermute(y2, ('row', 'col'), home(0))  6.8 us
    ppermute x1, starting transfers between devices, program(): g1 = lax.ppermute(y1, ('row', 'col'), home(1))  3.57 us
    unnamed x22, local copies, waits for them, and re-layouts  3.37 us
    ppermute x1, starting transfers between devices, program(): half_b = lax.ppermute(ahead[128:], 'row', ring[1])  3.31 us
  transfers between devices with their start and end apart: 20, of which 8 were waited for; matrix products, arithmetic and copies ran while one was open for 0% of the time, Pallas kernels for 29%

profile of v2, /device:TPU:38, one launch (start us, length us, event | category | flops | bytes accessed | tf_op | source)
XLA Modules:
  0.0 86.5 jit_solution(10829826208696639262)
XLA Ops:
  0.0 0.7 copy-done.1
  0.7 0.7 copy-done.3
  1.4 0.7 copy-done.4
  2.0 0.7 copy-done.6
  2.7 0.7 copy-done.8
  3.4 1.6 %shard_map.91.own = bf16[272,512]{1,0:T(8,128)(2,1)S(1)} custom-call(bf16[64,64,512]{2,1,0:T(8,128)(2,1)} %bitcast.35, s32[1,512]{1,0:T(1,128)S(1)} %bitcast.14, s32[1,64]{1,0:T(1,128)S(1)} %bitcast.22, f32[1,64]{1,0:T(1,128)S(1)} %bitcast.26, f32[1,64]{1,0:T(1,128)S(1)} %bitcast.29, bf16[32,64]{1,0:T(8,128)(2,1)S(1)} %bitcast.21), custom_call_target="tpu_custom_call" | custom-call | flops 20971520 | bytes 4479744 | tf_op jit(solution)/shard_map/pallas_call | solution.py:273
  5.0 0.2 collective-permute-start.2
  5.2 1.9 %collective-permute-start = (bf16[272,512]{1,0:T(8,128)(2,1)S(1)}, bf16[272,512]{1,0:T(8,128)(2,1)S(1)}, u32[]{:S(2)}, u32[]{:S(2)}) collective-permute-start(bf16[272,512]{1,0:T(8,128)(2,1)S(1)} %shard_map.91.own), channel_id=1, source_target_pairs={{0,32},{32,64},{64,96},{96,128},{128,160},{160,192},{192,224},{224... | collective-permute-start | bytes 835592 | tf_op jit(solution)/shard_map/ppermute | solution.py:318
  7.1 0.0 copy-done
  7.1 1.7 %collective-permute-start.4 = (bf16[144,128]{1,0:T(8,128)(2,1)S(1)}, bf16[144,128]{1,0:T(8,128)(2,1)S(1)}, u32[]{:S(2)}, u32[]{:S(2)}) collective-permute-start(bf16[144,128]{1,0:T(8,128)(2,1)S(1)} %shard_map.94.a), channel_id=1, source_target_pairs={{0,1},{1,2},{2,3},{3,0},{4,5},{5,6},{6,7},{7,4},{8,9},{9,10},{10,1... | collective-permute-start | bytes 110600 | tf_op jit(solution)/shard_map/ppermute | solution.py:301
  8.8 1.7 %collective-permute-start.5 = (bf16[144,128]{1,0:T(8,128)(2,1)S(1)}, bf16[144,128]{1,0:T(8,128)(2,1)S(1)}, u32[]{:S(2)}, u32[]{:S(2)}) collective-permute-start(bf16[144,128]{1,0:T(8,128)(2,1)S(1)} %shard_map.94.a), channel_id=1, source_target_pairs={{0,3},{1,0},{2,1},{3,2},{4,7},{5,4},{6,5},{7,6},{8,11},{9,8},{10,9... | collective-permute-start | bytes 110600 | tf_op jit(solution)/shard_map/ppermute | solution.py:302
  10.4 2.0 %collective-permute-start.6 = (bf16[144,128]{1,0:T(8,128)(2,1)S(1)}, bf16[144,128]{1,0:T(8,128)(2,1)S(1)}, u32[]{:S(2)}, u32[]{:S(2)}) collective-permute-start(bf16[144,128]{1,0:T(8,128)(2,1)S(1)} %shard_map.94.a), channel_id=1, source_target_pairs={{0,2},{1,3},{2,0},{3,1},{4,6},{5,7},{6,4},{7,5},{8,10},{9,11},{10,... | collective-permute-start | bytes 110600 | tf_op jit(solution)/shard_map/ppermute | solution.py:303
  12.4 0.0 collective-permute-done.4.b
  12.4 0.4 collective-permute-done.5.c
  12.8 3.1 %collective-permute-done.6.d = bf16[144,128]{1,0:T(8,128)(2,1)S(1)} collective-permute-done((bf16[144,128]{1,0:T(8,128)(2,1)S(1)}, bf16[144,128]{1,0:T(8,128)(2,1)S(1)}, u32[]{:S(2)}, u32[]{:S(2)}) %collective-permute-start.6) | collective-permute-done | bytes 36896 | tf_op jit(solution)/shard_map/ppermute | solution.py:303
  15.9 0.9 %collective-permute-start.7 = (bf16[4,144,128]{2,1,0:T(8,128)(2,1)S(1)}, bf16[4,144,128]{2,1,0:T(8,128)(2,1)S(1)}, u32[]{:S(2)}, u32[]{:S(2)}) collective-permute-start(bf16[4,144,128]{2,1,0:T(8,128)(2,1)S(1)} %shard_map.95.near), channel_id=1, source_target_pairs={{0,4},{1,5},{2,6},{3,7},{4,0},{5,1},{6,2},{7,3},{8,12},{9,13},{10,... | collective-permute-start | bytes 442376 | tf_op jit(solution)/shard_map/ppermute | solution.py:305
  16.8 0.0 collective-permute-done.2.ahead
  16.8 3.9 %collective-permute-start.3 = (bf16[272,512]{1,0:T(8,128)(2,1)S(1)}, bf16[272,512]{1,0:T(8,128)(2,1)S(1)}, u32[]{:S(2)}, u32[]{:S(2)}) collective-permute-start(bf16[272,512]{1,0:T(8,128)(2,1)S(1)} %collective-permute-done.2.ahead), channel_id=1, source_target_pairs={{0,224},{32,0},{64,32},{96,64},{128,96},{160,128},{192,160},{224,1... | collective-permute-start | bytes 835592 | tf_op jit(solution)/shard_map/ppermute | solution.py:319
  20.8 0.0 collective-permute-done.back
  20.8 0.0 collective-permute-start.1
  20.8 0.0 copy-done.7
  20.8 3.0 %shard_map.92.n_a = bf16[2048,512]{1,0:T(8,128)(2,1)S(1)} custom-call(bf16[64,64,512]{2,1,0:T(8,128)(2,1)} %bitcast.36, f32[1,64]{1,0:T(1,128)S(1)} %bitcast.27, f32[1,64]{1,0:T(1,128)S(1)} %bitcast.30), custom_call_target="tpu_custom_call" | custom-call | flops 15728640 | bytes 6291968 | tf_op jit(solution)/shard_map/pallas_call | solution.py:273
  23.8 0.0 copy-start.2
  23.8 0.0 copy-start.5
  23.8 3.0 %shard_map.93.n_b = bf16[2048,512]{1,0:T(8,128)(2,1)S(1)} custom-call(bf16[64,64,512]{2,1,0:T(8,128)(2,1)} %bitcast.37, f32[1,64]{1,0:T(1,128)S(1)} %bitcast.28, f32[1,64]{1,0:T(1,128)S(1)} %bitcast.31), custom_call_target="tpu_custom_call" | custom-call | flops 15728640 | bytes 6291968 | tf_op jit(solution)/shard_map/pallas_call | solution.py:273
  26.8 0.0 collective-permute-done.7.far
  26.8 0.3 shard_map.96
  27.1 1.5 %shard_map.97 = bf16[32,64,512]{2,1,0:T(8,128)(2,1)S(1)} custom-call(bf16[2048,512]{1,0:T(8,128)(2,1)S(1)} %shard_map.92.n_a, bf16[2048,512]{1,0:T(8,128)(2,1)S(1)} %shard_map.93.n_b, bf16[32,64]{1,0:T(8,128)(2,1)S(1)} %get-tuple-element.20.wl_ref, s32[1,512]{1,0:T(1,128)S(1)} %bitcast.15, s32[1,64]{1,0:T(1,128)S(1)} %bitcast.23), custom_call_target="tpu_custom_call" | custom-call | flops 1073741824 | bytes 6297856 | tf_op jit(solution)/shard_map/pallas_call | solution.py:273
  28.6 1.2 %shard_map.98.base = f32[520,128]{1,0:T(8,128)S(1)} custom-call(bf16[272,512]{1,0:T(8,128)(2,1)S(1)} %shard_map.91.own, bf16[2048,512]{1,0:T(8,128)(2,1)S(1)} %bitcast.9, bf16[256,512]{1,0:T(8,128)(2,1)S(1)} %get-tuple-element.21.w2, s32[1,512]{1,0:T(1,128)S(1)} %bitcast.16), custom_call_target="tpu_custom_call" | custom-call | flops 838860800 | bytes 2906112 | tf_op jit(solution)/shard_map/pallas_call | solution.py:273
  29.8 0.0 collective-permute-done.3.ahead
  29.8 3.3 %collective-permute-start.11 = (bf16[272,512]{1,0:T(8,128)(2,1)S(1)}, bf16[272,512]{1,0:T(8,128)(2,1)S(1)}, u32[]{:S(2)}, u32[]{:S(2)}) collective-permute-start(bf16[272,512]{1,0:T(8,128)(2,1)S(1)} %collective-permute-done.3.ahead), channel_id=1, source_target_pairs={{0,224},{32,0},{64,32},{96,64},{128,96},{160,128},{192,160},{224,1... | collective-permute-start | bytes 835592 | tf_op jit(solution)/shard_map/ppermute | solution.py:319
  33.1 0.0 collective-permute-done.1.back
  33.1 0.0 collective-permute-start.9
  33.1 4.9 %shard_map.103 = (f32[520,128]{1,0:T(8,128)S(1)}, f32[520,128]{1,0:T(8,128)S(1)}) custom-call(bf16[272,512]{1,0:T(8,128)(2,1)S(1)} %collective-permute-done.back, bf16[272,512]{1,0:T(8,128)(2,1)S(1)} %collective-permute-done.2.ahead, bf16[2048,512]{1,0:T(8,128)(2,1)S(1)} %bitcast.10, bf16[256,512]{1,0:T(8,128)(2,1)S(1)} %get-tuple-element.21.w2, ...), custom_call_target="tpu_custom_call" | custom-call | flops 1677721600 | bytes 3450880 | tf_op jit(solution)/shard_map/pallas_call | solution.py:273
  38.0 0.0 collective-permute-start.16
  38.0 3.3 %shard_map.99 = (f32[520,128]{1,0:T(8,128)S(1)}, f32[520,128]{1,0:T(8,128)S(1)}, f32[520,128]{1,0:T(8,128)S(1)}) custom-call(bf16[272,512]{1,0:T(8,128)(2,1)S(1)} %collective-permute-done.1.back, bf16[272,512]{1,0:T(8,128)(2,1)S(1)} %collective-permute-done.3.ahead, f32[520,128]{1,0:T(8,128)S(1)} %shard_map.98.base, bf16[2048,512]{1,0:T(8,128)(2,1)S(1)} %bitcast.11, ...), custom_call_target="tpu_custom_call" | custom-call | flops 1677721600 | bytes 3983360 | tf_op jit(solution)/shard_map/pallas_call | solution.py:273
  41.3 0.5 collective-permute-start.8
  41.8 0.0 collective-permute-done.11.ahead
  41.8 3.3 %collective-permute-start.12 = (bf16[144,512]{1,0:T(8,128)(2,1)S(1)}, bf16[144,512]{1,0:T(8,128)(2,1)S(1)}, u32[]{:S(2)}, u32[]{:S(2)}) collective-permute-start(bf16[144,512]{1,0:T(8,128)(2,1)S(1)} %slice.9), channel_id=1, source_target_pairs={{0,224},{32,0},{64,32},{96,64},{128,96},{160,128},{192,160},{224,1... | collective-permute-start | bytes 442376 | tf_op jit(solution)/shard_map/ppermute | solution.py:323
  45.1 0.0 collective-permute-done.9.back
  45.1 0.1 collective-permute-start.10
  45.2 4.7 %shard_map.104 = (f32[520,128]{1,0:T(8,128)S(1)}, f32[520,128]{1,0:T(8,128)S(1)}) custom-call(bf16[272,512]{1,0:T(8,128)(2,1)S(1)} %collective-permute-done.9.back, bf16[272,512]{1,0:T(8,128)(2,1)S(1)} %collective-permute-done.11.ahead, bf16[2048,512]{1,0:T(8,128)(2,1)S(1)} %bitcast.12, bf16[256,512]{1,0:T(8,128)(2,1)S(1)} %get-tuple-element.21.w2, ...), custom_call_target="tpu_custom_call" | custom-call | flops 1677721600 | bytes 3450880 | tf_op jit(solution)/shard_map/pallas_call | solution.py:273
  49.9 0.0 collective-permute-start.17
  50.0 1.9 %collective-permute-done.10.first = bf16[128,512]{1,0:T(8,128)(2,1)S(1)} collective-permute-done((bf16[128,512]{1,0:T(8,128)(2,1)S(1)}, bf16[128,512]{1,0:T(8,128)(2,1)S(1)}, u32[]{:S(2)}, u32[]{:S(2)}) %collective-permute-start.10) | collective-permute-done | bytes 131104 | tf_op jit(solution)/shard_map/ppermute | solution.py:322
  51.9 0.0 collective-permute-done.12.second
  51.9 2.4 %shard_map.100 = (f32[520,128]{1,0:T(8,128)S(1)}, f32[520,128]{1,0:T(8,128)S(1)}) custom-call(bf16[128,512]{1,0:T(8,128)(2,1)S(1)} %collective-permute-done.10.first, bf16[144,512]{1,0:T(8,128)(2,1)S(1)} %collective-permute-done.12.second, f32[520,128]{1,0:T(8,128)S(1)} %get-tuple-element.24.rest, bf16[2048,512]{1,0:T(8,128)(2,1)S(1)} %bitcast.13, ...), custom_call_target="tpu_custom_call" | custom-call | flops 838860800 | bytes 3438592 | tf_op jit(solution)/shard_map/pallas_call | solution.py:273
  54.3 0.0 collective-permute-start.13
  54.3 0.0 collective-permute-done.16.got_a
  54.3 0.0 collective-permute-done.17.got_b
  54.3 0.1 shard_map.105
  54.4 1.2 %collective-permute-start.18 = (f32[520,128]{1,0:T(8,128)S(1)}, f32[520,128]{1,0:T(8,128)S(1)}, u32[]{:S(2)}, u32[]{:S(2)}) collective-permute-start(f32[520,128]{1,0:T(8,128)S(1)} %get-tuple-element.34), channel_id=1, source_target_pairs={{0,16},{8,24},{16,0},{24,8},{1,17},{9,25},{17,1},{25,9},{2,18},{10... | collective-permute-start | bytes 798728 | tf_op jit(solution)/shard_map/ppermute | solution.py:356
  55.6 0.0 collective-permute-done.8.got_a
  55.6 0.2 collective-permute-done.13.got_b
  55.8 0.1 shard_map.101
  55.9 2.3 %collective-permute-start.14 = (f32[520,128]{1,0:T(8,128)S(1)}, f32[520,128]{1,0:T(8,128)S(1)}, u32[]{:S(2)}, u32[]{:S(2)}) collective-permute-start(f32[520,128]{1,0:T(8,128)S(1)} %get-tuple-element.28), channel_id=1, source_target_pairs={{0,16},{8,24},{16,0},{24,8},{1,17},{9,25},{17,1},{25,9},{2,18},{10... | collective-permute-start | bytes 798728 | tf_op jit(solution)/shard_map/ppermute | solution.py:358
  58.2 7.1 %collective-permute-done.18.got = f32[520,128]{1,0:T(8,128)S(1)} collective-permute-done((f32[520,128]{1,0:T(8,128)S(1)}, f32[520,128]{1,0:T(8,128)S(1)}, u32[]{:S(2)}, u32[]{:S(2)}) %collective-permute-start.18) | collective-permute-done | bytes 266272 | tf_op jit(solution)/shard_map/ppermute | solution.py:356
  65.3 0.2 shard_map.106
  65.6 3.6 %collective-permute-start.19 = (bf16[64,8,128]{2,1,0:T(8,128)(2,1)S(1)}, bf16[64,8,128]{2,1,0:T(8,128)(2,1)S(1)}, u32[]{:S(2)}, u32[]{:S(2)}) collective-permute-start(bf16[64,8,128]{2,1,0:T(8,128)(2,1)S(1)} %shard_map.106), channel_id=1, source_target_pairs={{0,32},{8,96},{16,160},{24,224},{32,0},{40,64},{48,128},{56,192},{... | collective-permute-start | bytes 393224 | tf_op jit(solution)/shard_map/ppermute | solution.py:367
  69.1 1.4 %collective-permute-done.14.got = f32[520,128]{1,0:T(8,128)S(1)} collective-permute-done((f32[520,128]{1,0:T(8,128)S(1)}, f32[520,128]{1,0:T(8,128)S(1)}, u32[]{:S(2)}, u32[]{:S(2)}) %collective-permute-start.14) | collective-permute-done | bytes 266272 | tf_op jit(solution)/shard_map/ppermute | solution.py:358
  70.5 0.3 shard_map.102
  70.8 6.9 %collective-permute-start.15 = (bf16[64,8,128]{2,1,0:T(8,128)(2,1)S(1)}, bf16[64,8,128]{2,1,0:T(8,128)(2,1)S(1)}, u32[]{:S(2)}, u32[]{:S(2)}) collective-permute-start(bf16[64,8,128]{2,1,0:T(8,128)(2,1)S(1)} %shard_map.102), channel_id=1, source_target_pairs={{0,0},{8,64},{16,128},{24,192},{32,32},{40,96},{48,160},{56,224},{... | collective-permute-start | bytes 393224 | tf_op jit(solution)/shard_map/ppermute | solution.py:368
  77.7 1.3 %collective-permute-done.19 = bf16[64,8,128]{2,1,0:T(8,128)(2,1)S(1)} collective-permute-done((bf16[64,8,128]{2,1,0:T(8,128)(2,1)S(1)}, bf16[64,8,128]{2,1,0:T(8,128)(2,1)S(1)}, u32[]{:S(2)}, u32[]{:S(2)}) %collective-permute-start.19) | collective-permute-done | bytes 131104 | tf_op jit(solution)/shard_map/ppermute | solution.py:367
  79.0 6.8 %collective-permute-done.15 = bf16[64,8,128]{2,1,0:T(8,128)(2,1)S(1)} collective-permute-done((bf16[64,8,128]{2,1,0:T(8,128)(2,1)S(1)}, bf16[64,8,128]{2,1,0:T(8,128)(2,1)S(1)}, u32[]{:S(2)}, u32[]{:S(2)}) %collective-permute-start.15) | collective-permute-done | bytes 131104 | tf_op jit(solution)/shard_map/ppermute | solution.py:368
  85.8 0.7 maximum_select_fusion
  (17 shorter events, 0.1 us)
Async XLA Ops:
  0.0 0.7 copy-start.1
  0.7 0.7 copy-start.3
  1.4 0.7 copy-start.4
  2.0 0.7 copy-start.6
  2.7 0.7 copy-start.8
  3.3 3.7 %copy-start = (bf16[128,128]{1,0:T(8,128)(2,1)S(1)}, bf16[128,128]{1,0:T(8,128)(2,1)}, u32[]{:S(2)}) copy-start(bf16[128,128]{1,0:T(8,128)(2,1)} %wo_ref.1) | copy-start | bytes 98308
  3.3 3.7 %copy-start.10 = (bf16[64,4]{0,1:T(4,128)(2,1)S(1)}, bf16[64,4]{0,1:T(4,128)(2,1)}, u32[]{:S(2)}) copy-start(bf16[64,4]{0,1:T(4,128)(2,1)} %param.14) | copy-start | bytes 1540
  3.4 17.4 %copy-start.7 = (f32[64]{0:T(128)S(1)}, f32[64]{0:T(128)}, u32[]{:S(2)}) copy-start(f32[64]{0:T(128)} %param.12) | copy-start | bytes 772
  5.0 11.8 %collective-permute-start.2 = (bf16[272,512]{1,0:T(8,128)(2,1)S(1)}, bf16[272,512]{1,0:T(8,128)(2,1)S(1)}, u32[]{:S(2)}, u32[]{:S(2)}) collective-permute-start(bf16[272,512]{1,0:T(8,128)(2,1)S(1)} %shard_map.91.own), channel_id=1, source_target_pairs={{0,224},{32,0},{64,32},{96,64},{128,96},{160,128},{192,160},{224,1... | collective-permute-start | bytes 835592 | tf_op jit(solution)/shard_map/ppermute | solution.py:319
  5.2 15.6 %collective-permute-start = (bf16[272,512]{1,0:T(8,128)(2,1)S(1)}, bf16[272,512]{1,0:T(8,128)(2,1)S(1)}, u32[]{:S(2)}, u32[]{:S(2)}) collective-permute-start(bf16[272,512]{1,0:T(8,128)(2,1)S(1)} %shard_map.91.own), channel_id=1, source_target_pairs={{0,32},{32,64},{64,96},{96,128},{128,160},{160,192},{192,224},{224... | collective-permute-start | bytes 835592 | tf_op jit(solution)/shard_map/ppermute | solution.py:318
  7.1 5.3 %collective-permute-start.4 = (bf16[144,128]{1,0:T(8,128)(2,1)S(1)}, bf16[144,128]{1,0:T(8,128)(2,1)S(1)}, u32[]{:S(2)}, u32[]{:S(2)}) collective-permute-start(bf16[144,128]{1,0:T(8,128)(2,1)S(1)} %shard_map.94.a), channel_id=1, source_target_pairs={{0,1},{1,2},{2,3},{3,0},{4,5},{5,6},{6,7},{7,4},{8,9},{9,10},{10,1... | collective-permute-start | bytes 110600 | tf_op jit(solution)/shard_map/ppermute | solution.py:301
  8.8 4.1 %collective-permute-start.5 = (bf16[144,128]{1,0:T(8,128)(2,1)S(1)}, bf16[144,128]{1,0:T(8,128)(2,1)S(1)}, u32[]{:S(2)}, u32[]{:S(2)}) collective-permute-start(bf16[144,128]{1,0:T(8,128)(2,1)S(1)} %shard_map.94.a), channel_id=1, source_target_pairs={{0,3},{1,0},{2,1},{3,2},{4,7},{5,4},{6,5},{7,6},{8,11},{9,8},{10,9... | collective-permute-start | bytes 110600 | tf_op jit(solution)/shard_map/ppermute | solution.py:302
  10.4 5.5 %collective-permute-start.6 = (bf16[144,128]{1,0:T(8,128)(2,1)S(1)}, bf16[144,128]{1,0:T(8,128)(2,1)S(1)}, u32[]{:S(2)}, u32[]{:S(2)}) collective-permute-start(bf16[144,128]{1,0:T(8,128)(2,1)S(1)} %shard_map.94.a), channel_id=1, source_target_pairs={{0,2},{1,3},{2,0},{3,1},{4,6},{5,7},{6,4},{7,5},{8,10},{9,11},{10,... | collective-permute-start | bytes 110600 | tf_op jit(solution)/shard_map/ppermute | solution.py:303
  15.9 10.9 %collective-permute-start.7 = (bf16[4,144,128]{2,1,0:T(8,128)(2,1)S(1)}, bf16[4,144,128]{2,1,0:T(8,128)(2,1)S(1)}, u32[]{:S(2)}, u32[]{:S(2)}) collective-permute-start(bf16[4,144,128]{2,1,0:T(8,128)(2,1)S(1)} %shard_map.95.near), channel_id=1, source_target_pairs={{0,4},{1,5},{2,6},{3,7},{4,0},{5,1},{6,2},{7,3},{8,12},{9,13},{10,... | collective-permute-start | bytes 442376 | tf_op jit(solution)/shard_map/ppermute | solution.py:305
  16.8 13.0 %collective-permute-start.3 = (bf16[272,512]{1,0:T(8,128)(2,1)S(1)}, bf16[272,512]{1,0:T(8,128)(2,1)S(1)}, u32[]{:S(2)}, u32[]{:S(2)}) collective-permute-start(bf16[272,512]{1,0:T(8,128)(2,1)S(1)} %collective-permute-done.2.ahead), channel_id=1, source_target_pairs={{0,224},{32,0},{64,32},{96,64},{128,96},{160,128},{192,160},{224,1... | collective-permute-start | bytes 835592 | tf_op jit(solution)/shard_map/ppermute | solution.py:319
  20.8 12.3 %collective-permute-start.1 = (bf16[272,512]{1,0:T(8,128)(2,1)S(1)}, bf16[272,512]{1,0:T(8,128)(2,1)S(1)}, u32[]{:S(2)}, u32[]{:S(2)}) collective-permute-start(bf16[272,512]{1,0:T(8,128)(2,1)S(1)} %collective-permute-done.back), channel_id=1, source_target_pairs={{0,32},{32,64},{64,96},{96,128},{128,160},{160,192},{192,224},{224... | collective-permute-start | bytes 835592 | tf_op jit(solution)/shard_map/ppermute | solution.py:318
  23.8 3.3 %copy-start.2 = (s32[512]{0:T(512)S(1)}, s32[512]{0:T(512)}, u32[]{:S(2)}) copy-start(s32[512]{0:T(512)} %param.10) | copy-start | bytes 6148
  23.8 3.3 %copy-start.5 = (s32[64]{0:T(128)S(1)}, s32[64]{0:T(128)}, u32[]{:S(2)}) copy-start(s32[64]{0:T(128)} %param.11) | copy-start | bytes 772
  29.8 12.0 %collective-permute-start.11 = (bf16[272,512]{1,0:T(8,128)(2,1)S(1)}, bf16[272,512]{1,0:T(8,128)(2,1)S(1)}, u32[]{:S(2)}, u32[]{:S(2)}) collective-permute-start(bf16[272,512]{1,0:T(8,128)(2,1)S(1)} %collective-permute-done.3.ahead), channel_id=1, source_target_pairs={{0,224},{32,0},{64,32},{96,64},{128,96},{160,128},{192,160},{224,1... | collective-permute-start | bytes 835592 | tf_op jit(solution)/shard_map/ppermute | solution.py:319
  33.1 12.0 %collective-permute-start.9 = (bf16[272,512]{1,0:T(8,128)(2,1)S(1)}, bf16[272,512]{1,0:T(8,128)(2,1)S(1)}, u32[]{:S(2)}, u32[]{:S(2)}) collective-permute-start(bf16[272,512]{1,0:T(8,128)(2,1)S(1)} %collective-permute-done.1.back), channel_id=1, source_target_pairs={{0,32},{32,64},{64,96},{96,128},{128,160},{160,192},{192,224},{224... | collective-permute-start | bytes 835592 | tf_op jit(solution)/shard_map/ppermute | solution.py:318
  38.0 16.3 %collective-permute-start.16 = (f32[520,128]{1,0:T(8,128)S(1)}, f32[520,128]{1,0:T(8,128)S(1)}, u32[]{:S(2)}, u32[]{:S(2)}) collective-permute-start(f32[520,128]{1,0:T(8,128)S(1)} %get-tuple-element.30), channel_id=1, source_target_pairs={{0,8},{8,0},{16,24},{24,16},{1,9},{9,1},{17,25},{25,17},{2,10},{10... | collective-permute-start | bytes 798728 | tf_op jit(solution)/shard_map/ppermute | solution.py:351
  41.3 14.4 %collective-permute-start.8 = (f32[520,128]{1,0:T(8,128)S(1)}, f32[520,128]{1,0:T(8,128)S(1)}, u32[]{:S(2)}, u32[]{:S(2)}) collective-permute-start(f32[520,128]{1,0:T(8,128)S(1)} %get-tuple-element.23), channel_id=1, source_target_pairs={{0,8},{8,0},{16,24},{24,16},{1,9},{9,1},{17,25},{25,17},{2,10},{10... | collective-permute-start | bytes 798728 | tf_op jit(solution)/shard_map/ppermute | solution.py:352
  41.8 10.1 %collective-permute-start.12 = (bf16[144,512]{1,0:T(8,128)(2,1)S(1)}, bf16[144,512]{1,0:T(8,128)(2,1)S(1)}, u32[]{:S(2)}, u32[]{:S(2)}) collective-permute-start(bf16[144,512]{1,0:T(8,128)(2,1)S(1)} %slice.9), channel_id=1, source_target_pairs={{0,224},{32,0},{64,32},{96,64},{128,96},{160,128},{192,160},{224,1... | collective-permute-start | bytes 442376 | tf_op jit(solution)/shard_map/ppermute | solution.py:323
  45.1 6.7 %collective-permute-start.10 = (bf16[128,512]{1,0:T(8,128)(2,1)S(1)}, bf16[128,512]{1,0:T(8,128)(2,1)S(1)}, u32[]{:S(2)}, u32[]{:S(2)}) collective-permute-start(bf16[128,512]{1,0:T(8,128)(2,1)S(1)} %slice.8), channel_id=1, source_target_pairs={{0,32},{32,64},{64,96},{96,128},{128,160},{160,192},{192,224},{224... | collective-permute-start | bytes 393224 | tf_op jit(solution)/shard_map/ppermute | solution.py:322
  49.9 4.4 %collective-permute-start.17 = (f32[520,128]{1,0:T(8,128)S(1)}, f32[520,128]{1,0:T(8,128)S(1)}, u32[]{:S(2)}, u32[]{:S(2)}) collective-permute-start(f32[520,128]{1,0:T(8,128)S(1)} %get-tuple-element.32), channel_id=1, source_target_pairs={{0,8},{8,0},{16,24},{24,16},{1,9},{9,1},{17,25},{25,17},{2,10},{10... | collective-permute-start | bytes 798728 | tf_op jit(solution)/shard_map/ppermute | solution.py:353
  51.9 13.4 %copy-start.9 = (f32[128]{0:T(128)S(1)}, f32[128]{0:T(128)}, u32[]{:S(2)}) copy-start(f32[128]{0:T(128)} %param.17) | copy-start | bytes 1540
  54.3 1.6 %collective-permute-start.13 = (f32[520,128]{1,0:T(8,128)S(1)}, f32[520,128]{1,0:T(8,128)S(1)}, u32[]{:S(2)}, u32[]{:S(2)}) collective-permute-start(f32[520,128]{1,0:T(8,128)S(1)} %get-tuple-element.26), channel_id=1, source_target_pairs={{0,8},{8,0},{16,24},{24,16},{1,9},{9,1},{17,25},{25,17},{2,10},{10... | collective-permute-start | bytes 798728 | tf_op jit(solution)/shard_map/ppermute | solution.py:354
  54.4 10.9 %collective-permute-start.18 = (f32[520,128]{1,0:T(8,128)S(1)}, f32[520,128]{1,0:T(8,128)S(1)}, u32[]{:S(2)}, u32[]{:S(2)}) collective-permute-start(f32[520,128]{1,0:T(8,128)S(1)} %get-tuple-element.34), channel_id=1, source_target_pairs={{0,16},{8,24},{16,0},{24,8},{1,17},{9,25},{17,1},{25,9},{2,18},{10... | collective-permute-start | bytes 798728 | tf_op jit(solution)/shard_map/ppermute | solution.py:356
  55.9 14.6 %collective-permute-start.14 = (f32[520,128]{1,0:T(8,128)S(1)}, f32[520,128]{1,0:T(8,128)S(1)}, u32[]{:S(2)}, u32[]{:S(2)}) collective-permute-start(f32[520,128]{1,0:T(8,128)S(1)} %get-tuple-element.28), channel_id=1, source_target_pairs={{0,16},{8,24},{16,0},{24,8},{1,17},{9,25},{17,1},{25,9},{2,18},{10... | collective-permute-start | bytes 798728 | tf_op jit(solution)/shard_map/ppermute | solution.py:358
  65.6 13.4 %collective-permute-start.19 = (bf16[64,8,128]{2,1,0:T(8,128)(2,1)S(1)}, bf16[64,8,128]{2,1,0:T(8,128)(2,1)S(1)}, u32[]{:S(2)}, u32[]{:S(2)}) collective-permute-start(bf16[64,8,128]{2,1,0:T(8,128)(2,1)S(1)} %shard_map.106), channel_id=1, source_target_pairs={{0,32},{8,96},{16,160},{24,224},{32,0},{40,64},{48,128},{56,192},{... | collective-permute-start | bytes 393224 | tf_op jit(solution)/shard_map/ppermute | solution.py:367
  70.8 15.0 %collective-permute-start.15 = (bf16[64,8,128]{2,1,0:T(8,128)(2,1)S(1)}, bf16[64,8,128]{2,1,0:T(8,128)(2,1)S(1)}, u32[]{:S(2)}, u32[]{:S(2)}) collective-permute-start(bf16[64,8,128]{2,1,0:T(8,128)(2,1)S(1)} %shard_map.102), channel_id=1, source_target_pairs={{0,0},{8,64},{16,128},{24,192},{32,32},{40,96},{48,160},{56,224},{... | collective-permute-start | bytes 393224 | tf_op jit(solution)/shard_map/ppermute | solution.py:368

commit v3 on v2

--- a/solution.py
+++ b/solution.py
@@ -70,10 +70,21 @@
     wl_out[...] = jnp.dot(pick.astype(F32).astype(BF16), lefts, preferred_element_type=F32).astype(BF16)
 
 
-def right_kernel(x_ref, row_ref, tok_ref, gain_ref, bias_ref, wr_ref, out_ref, buf, sem):
+def right_kernel(x_ref, row_hbm, tok_hbm, gain_hbm, bias_hbm, wr_hbm, out_ref, buf, row_ref, tok_ref, gain_ref, bias_ref, wr_ref, sems):
     k = lax.axis_index("chan")
-    copy = pltpu.make_async_copy(x_ref.at[pl.ds(k * T, T)], buf, sem)
-    copy.start()
+    pieces = (
+        (x_ref.at[pl.ds(k * T, T)], buf),
+        (gain_hbm, gain_ref),
+        (bias_hbm, bias_ref),
+        (tok_hbm, tok_ref),
+        (row_hbm, row_ref),
+        (wr_hbm, wr_ref),
+    )
+    copies = [pltpu.make_async_copy(src, dst, sems.at[i]) for i, (src, dst) in enumerate(pieces)]
+    for copy in copies:
+        copy.start()
+    for copy in copies[1:]:
+        copy.wait()
     gain = column_of(gain_ref[...])
     bias = column_of(bias_ref[...])
     token_col = tokens_of(tok_ref, k * T, T)
@@ -81,7 +92,7 @@
     wr = wr_ref[...]
     pad = jnp.concatenate([jnp.broadcast_to(token_col, (T, S)), jnp.zeros((T, S), F32)], axis=0)
     out_ref[T * C :, :] = pad.astype(BF16)
-    copy.wait()
+    copies[0].wait()
     for t in range(T):
         normed = normalize(buf[t : t + 1], gain, bias).astype(BF16)
         part = jnp.dot(wr, normed[0], preferred_element_type=F32)
@@ -105,7 +116,7 @@
             out_ref[pl.ds(pl.multiple_of((g * T + t) * M, M), M), :] = normed[0].astype(BF16)
             return carry
 
-        lax.fori_loop(0, T, one, 0)
+        lax.fori_loop(0, T, one, 0, unroll=4)
 
 
 def left_kernel(n_a, n_b, wl_ref, row_ref, tok_ref, out_ref):
@@ -175,85 +186,45 @@
     return store
 
 
-def to_either(kept, keep, send):
-    def store(where, value):
-        @pl.when(kept)
-        def _():
-            keep[where, :] = value
-
-        @pl.when(jnp.logical_not(kept))
-        def _():
-            send[where, :] = value
-
-    return store
-
-
-def not_kept(kept):
-    return jnp.logical_not(kept)
-
-
-def core_kept(offset):
-    block = lax.rem(lax.axis_index("row") + offset + 8, 8)
-    return lax.rem(block // 2, 2) == lax.rem(lax.axis_index("col"), 2)
-
-
-def x_kept(offset):
-    block = lax.rem(lax.axis_index("row") + offset + 8, 8)
-    return block // 4 == lax.axis_index("col") // 2
+def half_of(ref, b):
+    return to(ref.at[b])
+
+
+def choose(first, a, b, one, two):
+    one[...] = jnp.where(first, a, b)
+    two[...] = jnp.where(first, b, a)
+
+
+def core():
+    return lax.rem(lax.axis_index("col"), 2)
 
 
 def first_kernel(own, lf, w2, row, out, spread):
     pair_blocks([whole(own) + (to(out),)], lf, w2, row, spread)
 
 
-def two_kernel(offset, back, ahead, lf, w2, row, keep, send, spread):
-    kept = core_kept(offset)
-    pair_blocks(
-        [
-            whole(back) + (to_either(not_kept(kept), keep, send),),
-            whole(ahead) + (to_either(kept, keep, send),),
-        ],
-        lf, w2, row, spread,
-    )
-
-
-def copy_either(kept, value, keep, send):
-    @pl.when(kept)
-    def _():
-        keep[...] = value[...]
-
-    @pl.when(jnp.logical_not(kept))
-    def _():
-        send[...] = value[...]
-
-
-def mixed_kernel(back, ahead, base, lf, w2, row, keep, send, rest, spread):
-    kept = core_kept(2)
-    copy_either(not_kept(kept), base, keep, send)
-    pair_blocks(
-        [whole(back) + (to(rest),), whole(ahead) + (to_either(kept, keep, send),)], lf, w2, row, spread
-    )
-
-
-def last_kernel(first, second, rest, lf, w2, row, keep, send, spread):
-    kept = core_kept(4)
-    copy_either(not_kept(kept), rest, keep, send)
-    pair_blocks([halves(first, second) + (to_either(kept, keep, send),)], lf, w2, row, spread)
-
-
-def add_kernel(a_offsets, keep_a, got_a, keep_b, got_b, keep, send):
-    first, second = a_offsets
-    kept = jnp.where(core_kept(first), x_kept(first), x_kept(second))
-
-    @pl.when(kept)
-    def _():
-        keep[...] = keep_a[...] + got_a[...]
-        send[...] = keep_b[...] + got_b[...]
-
-    @pl.when(jnp.logical_not(kept))
-    def _():
-        send[...] = keep_a[...] + got_a[...]
-        keep[...] = keep_b[...] + got_b[...]
+def two_kernel(back, ahead, lf, w2, row, keep, send, spread, both):
+    pair_blocks([whole(back) + (half_of(both, 0),), whole(ahead) + (half_of(both, 1),)], lf, w2, row, spread)
+    choose(core() == 0, both[1], both[0], keep, send)
+
+
+def mixed_kernel(back, ahead, base, lf, w2, row, keep, send, rest, spread, both):
+    pair_blocks([whole(back) + (to(rest),), whole(ahead) + (half_of(both, 0),)], lf, w2, row, spread)
+    choose(core() == 0, base[...], both[0], keep, send)
+
+
+def last_kernel(first, second, rest, lf, w2, row, keep, send, spread, both):
+    pair_blocks([halves(first, second) + (half_of(both, 0),)], lf, w2, row, spread)
+    choose(core() == 0, both[0], rest[...], keep, send)
+
+
+def add_kernel(swapped, keep_a, got_a, keep_b, got_b, keep, send):
+    a = keep_a[...] + got_a[...]
+    b = keep_b[...] + got_b[...]
+    first = lax.axis_index("col") // 2 == 0
+    if swapped:
+        first = lax.axis_index("col") // 2 == core()
+    choose(first, a, b, keep, send)
 
 
 def final_kernel(keep, got, tok_ref, bias_ref, out):
@@ -281,12 +252,16 @@
     )(*args)
 
 
+def in_hbm(value):
+    return pltpu.with_memory_space_constraint(value, pltpu.HBM)
+
+
 def shape(dims, dtype):
     return jax.ShapeDtypeStruct(dims, dtype)
 
 
 def program(x, row_mask, token_mask, gain, bias, wl, wr, wo, out_bias):
-    xt = pltpu.with_memory_space_constraint(x.transpose(1, 2, 0), pltpu.HBM)
+    xt = in_hbm(x.transpose(1, 2, 0))
     row = row_mask.reshape(1, S)
     tok = token_mask.reshape(1, N)
     gain, bias = gain.reshape(1, M), bias.reshape(1, M)
@@ -305,10 +280,11 @@
     other = lax.ppermute(four, "chan", x_swap)
     wl_all, w2 = call(weight_kernel, (shape((C, M), BF16), shape((2 * Z, 512), BF16)), four, other, limit=4)
 
+    small = [in_hbm(a) for a in (row, tok, gain, bias, wr.T)]
     own = call(
-        right_kernel, shape((T * C + 16, S), BF16), xt, row, tok, gain, bias, wr.T,
-        specs=[HBM] + [VMEM] * 5,
-        scratch=[pltpu.VMEM((T, M, S), BF16), pltpu.SemaphoreType.DMA(())],
+        right_kernel, shape((T * C + 16, S), BF16), xt, *small,
+        specs=[HBM] * 6,
+        scratch=[pltpu.VMEM((T, M, S), BF16)] + [pltpu.VMEM(a.shape, a.dtype) for a in small] + [pltpu.SemaphoreType.DMA((6,))],
         flops=20 << 20, limit=8,
     )
 
@@ -340,32 +316,32 @@
     shared = (lf, w2, row)
 
     def spread(n):
-        return [pltpu.VMEM((n * T // 2, 512, 256), BF16)]
-
-    p0 = call(first_kernel, block, own, *shared, scratch=spread(1), flops=one)
-    k1, s1 = call(functools.partial(two_kernel, 1), pair, from_back[0], from_ahead[0], *shared, scratch=spread(2), flops=2 * one)
+        return [pltpu.VMEM((n * T // 2, 512, 256), BF16), pltpu.VMEM((n, ROWS + EXTRA, Z), F32)]
+
+    p0 = call(first_kernel, block, own, *shared, scratch=spread(1)[:1], flops=one)
+    k1, s1 = call(two_kernel, pair, from_back[0], from_ahead[0], *shared, scratch=spread(2), flops=2 * one)
     k2, s2, rest = call(mixed_kernel, (block,) * 3, from_back[1], from_ahead[1], p0, *shared, scratch=spread(2), flops=2 * one)
-    k3, s3 = call(functools.partial(two_kernel, 3), pair, from_back[2], from_ahead[2], *shared, scratch=spread(2), flops=2 * one)
+    k3, s3 = call(two_kernel, pair, from_back[2], from_ahead[2], *shared, scratch=spread(2), flops=2 * one)
     k4, s4 = call(last_kernel, pair, half_a, half_b, rest, *shared, scratch=spread(1), flops=one)
 
     e1 = lax.ppermute(s1, "col", core_swap)
     e2 = lax.ppermute(s2, "col", core_swap)
     e3 = lax.ppermute(s3, "col", core_swap)
     e4 = lax.ppermute(s4, "col", core_swap)
-    odd, odd_sent = call(functools.partial(add_kernel, (1, -1)), pair, k1, e1, k3, e3)
+    odd, odd_sent = call(functools.partial(add_kernel, True), pair, k1, e1, k3, e3)
     f1 = lax.ppermute(odd_sent, "col", xh_swap)
-    even, even_sent = call(functools.partial(add_kernel, (0, 2)), pair, k2, e2, k4, e4)
+    even, even_sent = call(functools.partial(add_kernel, False), pair, k2, e2, k4, e4)
     f2 = lax.ppermute(even_sent, "col", xh_swap)
     part = shape((N, T, Z), BF16)
     out_bias = out_bias.reshape(1, Z)
     y1 = call(final_kernel, part, odd, f1, tok, out_bias)
     y2 = call(final_kernel, part, even, f2, tok, out_bias)
 
-    def home(p):
-        return [(z * 4 + c, (2 * c + ((z % 2) ^ p)) * 4 + z // 2) for z in range(8) for c in range(4)]
-
-    g1 = lax.ppermute(y1, ("row", "col"), home(1))
-    g2 = lax.ppermute(y2, ("row", "col"), home(0))
+    def home(kept):
+        return [(z * 4 + c, (z + kept[c]) % 8 * 4 + z // 2) for z in range(8) for c in range(4)]
+
+    g1 = lax.ppermute(y1, ("row", "col"), home((1, -3, 3, -1)))
+    g2 = lax.ppermute(y2, ("row", "col"), home((0, 2, 4, -2)))
     low_row = lax.axis_index("row") % 2 == 0
     return jnp.where(low_row, jnp.concatenate([g2, g1], 0), jnp.concatenate([g1, g2], 0))
 

time: 88.1 us -> 80.1 us (0.909)
  the two profiles are of different devices: /device:TPU:38 before, /device:TPU:1 now
where the time goes in v3:
time: 80.1 us; the launch traced here: 79.9 us
  starting transfers between devices  33.1 us (41%)
  waiting for transfers between devices  27.8 us (35%)
  Pallas kernels  18.1 us (23%)
    pallas_call x16, Pallas kernels, call(): pl.pallas_call(kernel, out_shape=out, in_specs=specs or [VMEM] * len(args...  18.1 us
    ppermute x3, starting transfers between devices, program(): ahead = lax.ppermute(ahead, 'row', ring[1])  12.1 us
    ppermute x1, waiting for transfers between devices, program(): g2 = lax.ppermute(y2, ('row', 'col'), home((0, 2, 4, -2)))  11.3 us
    ppermute x1, waiting for transfers between devices, program(): f1 = lax.ppermute(odd_sent, 'col', xh_swap)  5.8 us
    ppermute x1, waiting for transfers between devices, program(): f2 = lax.ppermute(even_sent, 'col', xh_swap)  5.32 us
    ppermute x1, starting transfers between devices, program(): e1 = lax.ppermute(s1, 'col', core_swap)  3.79 us
    ppermute x1, starting transfers between devices, program(): half_b = lax.ppermute(ahead[128:], 'row', ring[1])  3.03 us
    ppermute x1, waiting for transfers between devices, program(): over = lax.ppermute(pack, 'chan', y_ring[2])  2.75 us
  transfers between devices with their start and end apart: 20, of which 5 were waited for; matrix products, arithmetic and copies ran while one was open for 0% of the time, Pallas kernels for 21%

profile of v3, /device:TPU:1, one launch (start us, length us, event | category | flops | bytes accessed | tf_op | source)
XLA Modules:
  0.0 79.9 jit_solution(8419969707769680617)
XLA Ops:
  0.0 0.0 copy-start.4
  0.0 1.7 %shard_map.91.own = bf16[272,512]{1,0:T(8,128)(2,1)S(1)} custom-call(bf16[64,64,512]{2,1,0:T(8,128)(2,1)} %bitcast.34, s32[1,512]{1,0:T(1,128)} %bitcast.14, s32[1,64]{1,0:T(1,128)} %bitcast.21, f32[1,64]{1,0:T(1,128)} %bitcast.25, f32[1,64]{1,0:T(1,128)} %bitcast.28, bf16[32,64]{1,0:T(8,128)(2,1)} %bitcast.37), custom_call_target="tpu_custom_call" | custom-call | flops 20971520 | bytes 4479744 | tf_op jit(solution)/shard_map/pallas_call | solution.py:244
  1.7 6.5 %collective-permute-start.2 = (bf16[272,512]{1,0:T(8,128)(2,1)S(1)}, bf16[272,512]{1,0:T(8,128)(2,1)S(1)}, u32[]{:S(2)}, u32[]{:S(2)}) collective-permute-start(bf16[272,512]{1,0:T(8,128)(2,1)S(1)} %shard_map.91.own), channel_id=1, source_target_pairs={{0,224},{32,0},{64,32},{96,64},{128,96},{160,128},{192,160},{224,1... | collective-permute-start | bytes 835592 | tf_op jit(solution)/shard_map/ppermute | solution.py:295
  8.2 0.0 collective-permute-start
  8.2 0.0 copy-done
  8.2 0.0 copy-done.6
  8.2 1.4 %collective-permute-start.4 = (bf16[144,128]{1,0:T(8,128)(2,1)S(1)}, bf16[144,128]{1,0:T(8,128)(2,1)S(1)}, u32[]{:S(2)}, u32[]{:S(2)}) collective-permute-start(bf16[144,128]{1,0:T(8,128)(2,1)S(1)} %shard_map.94.a), channel_id=1, source_target_pairs={{0,1},{1,2},{2,3},{3,0},{4,5},{5,6},{6,7},{7,4},{8,9},{9,10},{10,1... | collective-permute-start | bytes 110600 | tf_op jit(solution)/shard_map/ppermute | solution.py:276
  9.6 1.5 %collective-permute-start.5 = (bf16[144,128]{1,0:T(8,128)(2,1)S(1)}, bf16[144,128]{1,0:T(8,128)(2,1)S(1)}, u32[]{:S(2)}, u32[]{:S(2)}) collective-permute-start(bf16[144,128]{1,0:T(8,128)(2,1)S(1)} %shard_map.94.a), channel_id=1, source_target_pairs={{0,3},{1,0},{2,1},{3,2},{4,7},{5,4},{6,5},{7,6},{8,11},{9,8},{10,9... | collective-permute-start | bytes 110600 | tf_op jit(solution)/shard_map/ppermute | solution.py:277
  11.1 1.6 %collective-permute-start.6 = (bf16[144,128]{1,0:T(8,128)(2,1)S(1)}, bf16[144,128]{1,0:T(8,128)(2,1)S(1)}, u32[]{:S(2)}, u32[]{:S(2)}) collective-permute-start(bf16[144,128]{1,0:T(8,128)(2,1)S(1)} %shard_map.94.a), channel_id=1, source_target_pairs={{0,2},{1,3},{2,0},{3,1},{4,6},{5,7},{6,4},{7,5},{8,10},{9,11},{10,... | collective-permute-start | bytes 110600 | tf_op jit(solution)/shard_map/ppermute | solution.py:278
  12.6 0.0 collective-permute-done.4.b
  12.7 0.0 collective-permute-done.5.c
  12.7 2.8 %collective-permute-done.6.d = bf16[144,128]{1,0:T(8,128)(2,1)S(1)} collective-permute-done((bf16[144,128]{1,0:T(8,128)(2,1)S(1)}, bf16[144,128]{1,0:T(8,128)(2,1)S(1)}, u32[]{:S(2)}, u32[]{:S(2)}) %collective-permute-start.6) | collective-permute-done | bytes 36896 | tf_op jit(solution)/shard_map/ppermute | solution.py:278
  15.4 1.3 %collective-permute-start.7 = (bf16[4,144,128]{2,1,0:T(8,128)(2,1)S(1)}, bf16[4,144,128]{2,1,0:T(8,128)(2,1)S(1)}, u32[]{:S(2)}, u32[]{:S(2)}) collective-permute-start(bf16[4,144,128]{2,1,0:T(8,128)(2,1)S(1)} %shard_map.95.near), channel_id=1, source_target_pairs={{0,4},{1,5},{2,6},{3,7},{4,0},{5,1},{6,2},{7,3},{8,12},{9,13},{10,... | collective-permute-start | bytes 442376 | tf_op jit(solution)/shard_map/ppermute | solution.py:280
  16.7 0.0 collective-permute-done.2.ahead
  16.7 2.9 %collective-permute-start.3 = (bf16[272,512]{1,0:T(8,128)(2,1)S(1)}, bf16[272,512]{1,0:T(8,128)(2,1)S(1)}, u32[]{:S(2)}, u32[]{:S(2)}) collective-permute-start(bf16[272,512]{1,0:T(8,128)(2,1)S(1)} %collective-permute-done.2.ahead), channel_id=1, source_target_pairs={{0,224},{32,0},{64,32},{96,64},{128,96},{160,128},{192,160},{224,1... | collective-permute-start | bytes 835592 | tf_op jit(solution)/shard_map/ppermute | solution.py:295
  19.6 0.0 collective-permute-done.back
  19.6 0.0 collective-permute-start.1
  19.6 0.0 copy-done.3
  19.6 0.0 copy-done.4
  19.6 2.7 %shard_map.92.n_a = bf16[2048,512]{1,0:T(8,128)(2,1)S(1)} custom-call(bf16[64,64,512]{2,1,0:T(8,128)(2,1)} %bitcast.35, f32[1,64]{1,0:T(1,128)S(1)} %bitcast.26, f32[1,64]{1,0:T(1,128)S(1)} %bitcast.29), custom_call_target="tpu_custom_call" | custom-call | flops 15728640 | bytes 6291968 | tf_op jit(solution)/shard_map/pallas_call | solution.py:244
  22.3 0.0 copy-start.1
  22.3 0.0 copy-start.2
  22.3 2.7 %shard_map.93.n_b = bf16[2048,512]{1,0:T(8,128)(2,1)S(1)} custom-call(bf16[64,64,512]{2,1,0:T(8,128)(2,1)} %bitcast.36, f32[1,64]{1,0:T(1,128)S(1)} %bitcast.27, f32[1,64]{1,0:T(1,128)S(1)} %bitcast.30), custom_call_target="tpu_custom_call" | custom-call | flops 15728640 | bytes 6291968 | tf_op jit(solution)/shard_map/pallas_call | solution.py:244
  25.0 0.0 collective-permute-done.7.far
  25.0 0.3 shard_map.96
  25.3 0.0 copy-done.1
  25.3 0.0 copy-done.2
  25.3 1.5 %shard_map.97 = bf16[32,64,512]{2,1,0:T(8,128)(2,1)S(1)} custom-call(bf16[2048,512]{1,0:T(8,128)(2,1)S(1)} %shard_map.92.n_a, bf16[2048,512]{1,0:T(8,128)(2,1)S(1)} %shard_map.93.n_b, bf16[32,64]{1,0:T(8,128)(2,1)S(1)} %get-tuple-element.20.wl_ref, s32[1,512]{1,0:T(1,128)S(1)} %bitcast.15, s32[1,64]{1,0:T(1,128)S(1)} %bitcast.22), custom_call_target="tpu_custom_call" | custom-call | flops 1073741824 | bytes 6297856 | tf_op jit(solution)/shard_map/pallas_call | solution.py:244
  26.8 1.2 %shard_map.98.base = f32[520,128]{1,0:T(8,128)S(1)} custom-call(bf16[272,512]{1,0:T(8,128)(2,1)S(1)} %shard_map.91.own, bf16[2048,512]{1,0:T(8,128)(2,1)S(1)} %bitcast.9, bf16[256,512]{1,0:T(8,128)(2,1)S(1)} %get-tuple-element.21.w2, s32[1,512]{1,0:T(1,128)S(1)} %bitcast.16), custom_call_target="tpu_custom_call" | custom-call | flops 838860800 | bytes 2906112 | tf_op jit(solution)/shard_map/pallas_call | solution.py:244
  28.0 0.0 collective-permute-done.3.ahead
  28.0 2.7 %collective-permute-start.11 = (bf16[272,512]{1,0:T(8,128)(2,1)S(1)}, bf16[272,512]{1,0:T(8,128)(2,1)S(1)}, u32[]{:S(2)}, u32[]{:S(2)}) collective-permute-start(bf16[272,512]{1,0:T(8,128)(2,1)S(1)} %collective-permute-done.3.ahead), channel_id=1, source_target_pairs={{0,224},{32,0},{64,32},{96,64},{128,96},{160,128},{192,160},{224,1... | collective-permute-start | bytes 835592 | tf_op jit(solution)/shard_map/ppermute | solution.py:295
  30.7 0.0 collective-permute-done.1.back
  30.7 0.0 collective-permute-start.9
  30.7 2.0 %shard_map.103 = (f32[520,128]{1,0:T(8,128)S(1)}, f32[520,128]{1,0:T(8,128)S(1)}) custom-call(bf16[272,512]{1,0:T(8,128)(2,1)S(1)} %collective-permute-done.back, bf16[272,512]{1,0:T(8,128)(2,1)S(1)} %collective-permute-done.2.ahead, bf16[2048,512]{1,0:T(8,128)(2,1)S(1)} %bitcast.10, bf16[256,512]{1,0:T(8,128)(2,1)S(1)} %get-tuple-element.21.w2, ...), custom_call_target="tpu_custom_call" | custom-call | flops 1677721600 | bytes 3450880 | tf_op jit(solution)/shard_map/pallas_call | solution.py:244
  32.8 3.8 %collective-permute-start.16 = (f32[520,128]{1,0:T(8,128)S(1)}, f32[520,128]{1,0:T(8,128)S(1)}, u32[]{:S(2)}, u32[]{:S(2)}) collective-permute-start(f32[520,128]{1,0:T(8,128)S(1)} %get-tuple-element.30), channel_id=1, source_target_pairs={{0,8},{8,0},{16,24},{24,16},{1,9},{9,1},{17,25},{25,17},{2,10},{10... | collective-permute-start | bytes 798728 | tf_op jit(solution)/shard_map/ppermute | solution.py:327
  36.6 2.1 %shard_map.99 = (f32[520,128]{1,0:T(8,128)S(1)}, f32[520,128]{1,0:T(8,128)S(1)}, f32[520,128]{1,0:T(8,128)S(1)}) custom-call(bf16[272,512]{1,0:T(8,128)(2,1)S(1)} %collective-permute-done.1.back, bf16[272,512]{1,0:T(8,128)(2,1)S(1)} %collective-permute-done.3.ahead, f32[520,128]{1,0:T(8,128)S(1)} %shard_map.98.base, bf16[2048,512]{1,0:T(8,128)(2,1)S(1)} %bitcast.11, ...), custom_call_target="tpu_custom_call" | custom-call | flops 1677721600 | bytes 3983360 | tf_op jit(solution)/shard_map/pallas_call | solution.py:244
  38.7 0.1 collective-permute-start.8
  38.8 0.0 collective-permute-done.11.ahead
  38.8 3.0 %collective-permute-start.12 = (bf16[144,512]{1,0:T(8,128)(2,1)S(1)}, bf16[144,512]{1,0:T(8,128)(2,1)S(1)}, u32[]{:S(2)}, u32[]{:S(2)}) collective-permute-start(bf16[144,512]{1,0:T(8,128)(2,1)S(1)} %slice.9), channel_id=1, source_target_pairs={{0,224},{32,0},{64,32},{96,64},{128,96},{160,128},{192,160},{224,1... | collective-permute-start | bytes 442376 | tf_op jit(solution)/shard_map/ppermute | solution.py:299
  41.8 0.0 collective-permute-done.9.back
  41.8 0.1 collective-permute-start.10
  41.9 2.1 %shard_map.104 = (f32[520,128]{1,0:T(8,128)S(1)}, f32[520,128]{1,0:T(8,128)S(1)}) custom-call(bf16[272,512]{1,0:T(8,128)(2,1)S(1)} %collective-permute-done.9.back, bf16[272,512]{1,0:T(8,128)(2,1)S(1)} %collective-permute-done.11.ahead, bf16[2048,512]{1,0:T(8,128)(2,1)S(1)} %bitcast.12, bf16[256,512]{1,0:T(8,128)(2,1)S(1)} %get-tuple-element.21.w2, ...), custom_call_target="tpu_custom_call" | custom-call | flops 1677721600 | bytes 3450880 | tf_op jit(solution)/shard_map/pallas_call | solution.py:244
  44.0 0.9 %collective-permute-start.17 = (f32[520,128]{1,0:T(8,128)S(1)}, f32[520,128]{1,0:T(8,128)S(1)}, u32[]{:S(2)}, u32[]{:S(2)}) collective-permute-start(f32[520,128]{1,0:T(8,128)S(1)} %get-tuple-element.32), channel_id=1, source_target_pairs={{0,8},{8,0},{16,24},{24,16},{1,9},{9,1},{17,25},{25,17},{2,10},{10... | collective-permute-start | bytes 798728 | tf_op jit(solution)/shard_map/ppermute | solution.py:329
  44.9 2.5 %collective-permute-done.10.first = bf16[128,512]{1,0:T(8,128)(2,1)S(1)} collective-permute-done((bf16[128,512]{1,0:T(8,128)(2,1)S(1)}, bf16[128,512]{1,0:T(8,128)(2,1)S(1)}, u32[]{:S(2)}, u32[]{:S(2)}) %collective-permute-start.10) | collective-permute-done | bytes 131104 | tf_op jit(solution)/shard_map/ppermute | solution.py:298
  47.4 0.0 collective-permute-done.12.second
  47.4 1.3 %shard_map.100 = (f32[520,128]{1,0:T(8,128)S(1)}, f32[520,128]{1,0:T(8,128)S(1)}) custom-call(bf16[128,512]{1,0:T(8,128)(2,1)S(1)} %collective-permute-done.10.first, bf16[144,512]{1,0:T(8,128)(2,1)S(1)} %collective-permute-done.12.second, f32[520,128]{1,0:T(8,128)S(1)} %get-tuple-element.24.rest, bf16[2048,512]{1,0:T(8,128)(2,1)S(1)} %bitcast.13, ...), custom_call_target="tpu_custom_call" | custom-call | flops 838860800 | bytes 3438592 | tf_op jit(solution)/shard_map/pallas_call | solution.py:244
  48.7 1.7 %collective-permute-start.13 = (f32[520,128]{1,0:T(8,128)S(1)}, f32[520,128]{1,0:T(8,128)S(1)}, u32[]{:S(2)}, u32[]{:S(2)}) collective-permute-start(f32[520,128]{1,0:T(8,128)S(1)} %get-tuple-element.26), channel_id=1, source_target_pairs={{0,8},{8,0},{16,24},{24,16},{1,9},{9,1},{17,25},{25,17},{2,10},{10... | collective-permute-start | bytes 798728 | tf_op jit(solution)/shard_map/ppermute | solution.py:330
  50.4 0.0 collective-permute-done.16.got_a
  50.4 0.0 collective-permute-done.17.got_b
  50.4 0.1 shard_map.105
  50.5 2.5 %collective-permute-start.18 = (f32[520,128]{1,0:T(8,128)S(1)}, f32[520,128]{1,0:T(8,128)S(1)}, u32[]{:S(2)}, u32[]{:S(2)}) collective-permute-start(f32[520,128]{1,0:T(8,128)S(1)} %get-tuple-element.34), channel_id=1, source_target_pairs={{0,16},{8,24},{16,0},{24,8},{1,17},{9,25},{17,1},{25,9},{2,18},{10... | collective-permute-start | bytes 798728 | tf_op jit(solution)/shard_map/ppermute | solution.py:332
  53.0 0.0 collective-permute-done.8.got_a
  53.0 0.0 collective-permute-done.13.got_b
  53.0 0.1 shard_map.101
  53.1 1.1 %collective-permute-start.14 = (f32[520,128]{1,0:T(8,128)S(1)}, f32[520,128]{1,0:T(8,128)S(1)}, u32[]{:S(2)}, u32[]{:S(2)}) collective-permute-start(f32[520,128]{1,0:T(8,128)S(1)} %get-tuple-element.28), channel_id=1, source_target_pairs={{0,16},{8,24},{16,0},{24,8},{1,17},{9,25},{17,1},{25,9},{2,18},{10... | collective-permute-start | bytes 798728 | tf_op jit(solution)/shard_map/ppermute | solution.py:334
  54.2 5.8 %collective-permute-done.18.got = f32[520,128]{1,0:T(8,128)S(1)} collective-permute-done((f32[520,128]{1,0:T(8,128)S(1)}, f32[520,128]{1,0:T(8,128)S(1)}, u32[]{:S(2)}, u32[]{:S(2)}) %collective-permute-start.18) | collective-permute-done | bytes 266272 | tf_op jit(solution)/shard_map/ppermute | solution.py:332
  60.0 0.2 shard_map.106
  60.2 0.1 collective-permute-start.19
  60.4 5.3 %collective-permute-done.14.got = f32[520,128]{1,0:T(8,128)S(1)} collective-permute-done((f32[520,128]{1,0:T(8,128)S(1)}, f32[520,128]{1,0:T(8,128)S(1)}, u32[]{:S(2)}, u32[]{:S(2)}) %collective-permute-start.14) | collective-permute-done | bytes 266272 | tf_op jit(solution)/shard_map/ppermute | solution.py:334
  65.7 0.3 shard_map.102
  66.0 1.9 %collective-permute-start.15 = (bf16[64,8,128]{2,1,0:T(8,128)(2,1)S(1)}, bf16[64,8,128]{2,1,0:T(8,128)(2,1)S(1)}, u32[]{:S(2)}, u32[]{:S(2)}) collective-permute-start(bf16[64,8,128]{2,1,0:T(8,128)(2,1)S(1)} %shard_map.102), channel_id=1, source_target_pairs={{0,0},{8,64},{16,128},{24,192},{32,32},{40,96},{48,160},{56,224},{... | collective-permute-start | bytes 393224 | tf_op jit(solution)/shard_map/ppermute | solution.py:344
  67.9 0.0 collective-permute-done.19
  67.9 11.3 %collective-permute-done.15 = bf16[64,8,128]{2,1,0:T(8,128)(2,1)S(1)} collective-permute-done((bf16[64,8,128]{2,1,0:T(8,128)(2,1)S(1)}, bf16[64,8,128]{2,1,0:T(8,128)(2,1)S(1)}, u32[]{:S(2)}, u32[]{:S(2)}) %collective-permute-start.15) | collective-permute-done | bytes 131104 | tf_op jit(solution)/shard_map/ppermute | solution.py:344
  79.2 0.7 maximum_select_fusion
  (9 shorter events, 0.0 us)
Async XLA Ops:
  0.0 8.2 %copy-start = (bf16[128,128]{1,0:T(8,128)(2,1)S(1)}, bf16[128,128]{1,0:T(8,128)(2,1)}, u32[]{:S(2)}) copy-start(bf16[128,128]{1,0:T(8,128)(2,1)} %wo_ref.1) | copy-start | bytes 98308
  0.0 8.2 %copy-start.6 = (bf16[64,4]{0,1:T(4,128)(2,1)S(1)}, bf16[64,4]{0,1:T(4,128)(2,1)}, u32[]{:S(2)}) copy-start(bf16[64,4]{0,1:T(4,128)(2,1)} %param.14) | copy-start | bytes 1540
  0.0 19.6 %copy-start.3 = (f32[64]{0:T(128)S(1)}, f32[64]{0:T(128)}, u32[]{:S(2)}) copy-start(f32[64]{0:T(128)} %param.12) | copy-start | bytes 772
  0.0 19.6 %copy-start.4 = (f32[64]{0:T(128)S(1)}, f32[64]{0:T(128)}, u32[]{:S(2)}) copy-start(f32[64]{0:T(128)} %param.13) | copy-start | bytes 772
  1.7 15.0 %collective-permute-start.2 = (bf16[272,512]{1,0:T(8,128)(2,1)S(1)}, bf16[272,512]{1,0:T(8,128)(2,1)S(1)}, u32[]{:S(2)}, u32[]{:S(2)}) collective-permute-start(bf16[272,512]{1,0:T(8,128)(2,1)S(1)} %shard_map.91.own), channel_id=1, source_target_pairs={{0,224},{32,0},{64,32},{96,64},{128,96},{160,128},{192,160},{224,1... | collective-permute-start | bytes 835592 | tf_op jit(solution)/shard_map/ppermute | solution.py:295
  8.2 11.4 %collective-permute-start = (bf16[272,512]{1,0:T(8,128)(2,1)S(1)}, bf16[272,512]{1,0:T(8,128)(2,1)S(1)}, u32[]{:S(2)}, u32[]{:S(2)}) collective-permute-start(bf16[272,512]{1,0:T(8,128)(2,1)S(1)} %shard_map.91.own), channel_id=1, source_target_pairs={{0,32},{32,64},{64,96},{96,128},{128,160},{160,192},{192,224},{224... | collective-permute-start | bytes 835592 | tf_op jit(solution)/shard_map/ppermute | solution.py:294
  8.2 4.5 %collective-permute-start.4 = (bf16[144,128]{1,0:T(8,128)(2,1)S(1)}, bf16[144,128]{1,0:T(8,128)(2,1)S(1)}, u32[]{:S(2)}, u32[]{:S(2)}) collective-permute-start(bf16[144,128]{1,0:T(8,128)(2,1)S(1)} %shard_map.94.a), channel_id=1, source_target_pairs={{0,1},{1,2},{2,3},{3,0},{4,5},{5,6},{6,7},{7,4},{8,9},{9,10},{10,1... | collective-permute-start | bytes 110600 | tf_op jit(solution)/shard_map/ppermute | solution.py:276
  9.6 3.1 %collective-permute-start.5 = (bf16[144,128]{1,0:T(8,128)(2,1)S(1)}, bf16[144,128]{1,0:T(8,128)(2,1)S(1)}, u32[]{:S(2)}, u32[]{:S(2)}) collective-permute-start(bf16[144,128]{1,0:T(8,128)(2,1)S(1)} %shard_map.94.a), channel_id=1, source_target_pairs={{0,3},{1,0},{2,1},{3,2},{4,7},{5,4},{6,5},{7,6},{8,11},{9,8},{10,9... | collective-permute-start | bytes 110600 | tf_op jit(solution)/shard_map/ppermute | solution.py:277
  11.1 4.3 %collective-permute-start.6 = (bf16[144,128]{1,0:T(8,128)(2,1)S(1)}, bf16[144,128]{1,0:T(8,128)(2,1)S(1)}, u32[]{:S(2)}, u32[]{:S(2)}) collective-permute-start(bf16[144,128]{1,0:T(8,128)(2,1)S(1)} %shard_map.94.a), channel_id=1, source_target_pairs={{0,2},{1,3},{2,0},{3,1},{4,6},{5,7},{6,4},{7,5},{8,10},{9,11},{10,... | collective-permute-start | bytes 110600 | tf_op jit(solution)/shard_map/ppermute | solution.py:278
  15.4 9.5 %collective-permute-start.7 = (bf16[4,144,128]{2,1,0:T(8,128)(2,1)S(1)}, bf16[4,144,128]{2,1,0:T(8,128)(2,1)S(1)}, u32[]{:S(2)}, u32[]{:S(2)}) collective-permute-start(bf16[4,144,128]{2,1,0:T(8,128)(2,1)S(1)} %shard_map.95.near), channel_id=1, source_target_pairs={{0,4},{1,5},{2,6},{3,7},{4,0},{5,1},{6,2},{7,3},{8,12},{9,13},{10,... | collective-permute-start | bytes 442376 | tf_op jit(solution)/shard_map/ppermute | solution.py:280
  16.7 11.3 %collective-permute-start.3 = (bf16[272,512]{1,0:T(8,128)(2,1)S(1)}, bf16[272,512]{1,0:T(8,128)(2,1)S(1)}, u32[]{:S(2)}, u32[]{:S(2)}) collective-permute-start(bf16[272,512]{1,0:T(8,128)(2,1)S(1)} %collective-permute-done.2.ahead), channel_id=1, source_target_pairs={{0,224},{32,0},{64,32},{96,64},{128,96},{160,128},{192,160},{224,1... | collective-permute-start | bytes 835592 | tf_op jit(solution)/shard_map/ppermute | solution.py:295
  19.6 11.1 %collective-permute-start.1 = (bf16[272,512]{1,0:T(8,128)(2,1)S(1)}, bf16[272,512]{1,0:T(8,128)(2,1)S(1)}, u32[]{:S(2)}, u32[]{:S(2)}) collective-permute-start(bf16[272,512]{1,0:T(8,128)(2,1)S(1)} %collective-permute-done.back), channel_id=1, source_target_pairs={{0,32},{32,64},{64,96},{96,128},{128,160},{160,192},{192,224},{224... | collective-permute-start | bytes 835592 | tf_op jit(solution)/shard_map/ppermute | solution.py:294
  22.3 3.0 %copy-start.1 = (s32[512]{0:T(512)S(1)}, s32[512]{0:T(512)}, u32[]{:S(2)}) copy-start(s32[512]{0:T(512)} %param.10) | copy-start | bytes 6148
  22.3 3.0 %copy-start.2 = (s32[64]{0:T(128)S(1)}, s32[64]{0:T(128)}, u32[]{:S(2)}) copy-start(s32[64]{0:T(128)} %param.11) | copy-start | bytes 772
  28.0 10.8 %collective-permute-start.11 = (bf16[272,512]{1,0:T(8,128)(2,1)S(1)}, bf16[272,512]{1,0:T(8,128)(2,1)S(1)}, u32[]{:S(2)}, u32[]{:S(2)}) collective-permute-start(bf16[272,512]{1,0:T(8,128)(2,1)S(1)} %collective-permute-done.3.ahead), channel_id=1, source_target_pairs={{0,224},{32,0},{64,32},{96,64},{128,96},{160,128},{192,160},{224,1... | collective-permute-start | bytes 835592 | tf_op jit(solution)/shard_map/ppermute | solution.py:295
  30.7 11.1 %collective-permute-start.9 = (bf16[272,512]{1,0:T(8,128)(2,1)S(1)}, bf16[272,512]{1,0:T(8,128)(2,1)S(1)}, u32[]{:S(2)}, u32[]{:S(2)}) collective-permute-start(bf16[272,512]{1,0:T(8,128)(2,1)S(1)} %collective-permute-done.1.back), channel_id=1, source_target_pairs={{0,32},{32,64},{64,96},{96,128},{128,160},{160,192},{192,224},{224... | collective-permute-start | bytes 835592 | tf_op jit(solution)/shard_map/ppermute | solution.py:294
  32.8 17.6 %collective-permute-start.16 = (f32[520,128]{1,0:T(8,128)S(1)}, f32[520,128]{1,0:T(8,128)S(1)}, u32[]{:S(2)}, u32[]{:S(2)}) collective-permute-start(f32[520,128]{1,0:T(8,128)S(1)} %get-tuple-element.30), channel_id=1, source_target_pairs={{0,8},{8,0},{16,24},{24,16},{1,9},{9,1},{17,25},{25,17},{2,10},{10... | collective-permute-start | bytes 798728 | tf_op jit(solution)/shard_map/ppermute | solution.py:327
  38.7 14.4 %collective-permute-start.8 = (f32[520,128]{1,0:T(8,128)S(1)}, f32[520,128]{1,0:T(8,128)S(1)}, u32[]{:S(2)}, u32[]{:S(2)}) collective-permute-start(f32[520,128]{1,0:T(8,128)S(1)} %get-tuple-element.23), channel_id=1, source_target_pairs={{0,8},{8,0},{16,24},{24,16},{1,9},{9,1},{17,25},{25,17},{2,10},{10... | collective-permute-start | bytes 798728 | tf_op jit(solution)/shard_map/ppermute | solution.py:328
  38.8 8.6 %collective-permute-start.12 = (bf16[144,512]{1,0:T(8,128)(2,1)S(1)}, bf16[144,512]{1,0:T(8,128)(2,1)S(1)}, u32[]{:S(2)}, u32[]{:S(2)}) collective-permute-start(bf16[144,512]{1,0:T(8,128)(2,1)S(1)} %slice.9), channel_id=1, source_target_pairs={{0,224},{32,0},{64,32},{96,64},{128,96},{160,128},{192,160},{224,1... | collective-permute-start | bytes 442376 | tf_op jit(solution)/shard_map/ppermute | solution.py:299
  41.8 5.6 %collective-permute-start.10 = (bf16[128,512]{1,0:T(8,128)(2,1)S(1)}, bf16[128,512]{1,0:T(8,128)(2,1)S(1)}, u32[]{:S(2)}, u32[]{:S(2)}) collective-permute-start(bf16[128,512]{1,0:T(8,128)(2,1)S(1)} %slice.8), channel_id=1, source_target_pairs={{0,32},{32,64},{64,96},{96,128},{128,160},{160,192},{192,224},{224... | collective-permute-start | bytes 393224 | tf_op jit(solution)/shard_map/ppermute | solution.py:298
  44.0 6.4 %collective-permute-start.17 = (f32[520,128]{1,0:T(8,128)S(1)}, f32[520,128]{1,0:T(8,128)S(1)}, u32[]{:S(2)}, u32[]{:S(2)}) collective-permute-start(f32[520,128]{1,0:T(8,128)S(1)} %get-tuple-element.32), channel_id=1, source_target_pairs={{0,8},{8,0},{16,24},{24,16},{1,9},{9,1},{17,25},{25,17},{2,10},{10... | collective-permute-start | bytes 798728 | tf_op jit(solution)/shard_map/ppermute | solution.py:329
  47.4 12.6 %copy-start.5 = (f32[128]{0:T(128)S(1)}, f32[128]{0:T(128)}, u32[]{:S(2)}) copy-start(f32[128]{0:T(128)} %param.17) | copy-start | bytes 1540
  48.7 4.3 %collective-permute-start.13 = (f32[520,128]{1,0:T(8,128)S(1)}, f32[520,128]{1,0:T(8,128)S(1)}, u32[]{:S(2)}, u32[]{:S(2)}) collective-permute-start(f32[520,128]{1,0:T(8,128)S(1)} %get-tuple-element.26), channel_id=1, source_target_pairs={{0,8},{8,0},{16,24},{24,16},{1,9},{9,1},{17,25},{25,17},{2,10},{10... | collective-permute-start | bytes 798728 | tf_op jit(solution)/shard_map/ppermute | solution.py:330
  50.5 9.5 %collective-permute-start.18 = (f32[520,128]{1,0:T(8,128)S(1)}, f32[520,128]{1,0:T(8,128)S(1)}, u32[]{:S(2)}, u32[]{:S(2)}) collective-permute-start(f32[520,128]{1,0:T(8,128)S(1)} %get-tuple-element.34), channel_id=1, source_target_pairs={{0,16},{8,24},{16,0},{24,8},{1,17},{9,25},{17,1},{25,9},{2,18},{10... | collective-permute-start | bytes 798728 | tf_op jit(solution)/shard_map/ppermute | solution.py:332
  53.1 12.6 %collective-permute-start.14 = (f32[520,128]{1,0:T(8,128)S(1)}, f32[520,128]{1,0:T(8,128)S(1)}, u32[]{:S(2)}, u32[]{:S(2)}) collective-permute-start(f32[520,128]{1,0:T(8,128)S(1)} %get-tuple-element.28), channel_id=1, source_target_pairs={{0,16},{8,24},{16,0},{24,8},{1,17},{9,25},{17,1},{25,9},{2,18},{10... | collective-permute-start | bytes 798728 | tf_op jit(solution)/shard_map/ppermute | solution.py:334
  60.2 7.7 %collective-permute-start.19 = (bf16[64,8,128]{2,1,0:T(8,128)(2,1)S(1)}, bf16[64,8,128]{2,1,0:T(8,128)(2,1)S(1)}, u32[]{:S(2)}, u32[]{:S(2)}) collective-permute-start(bf16[64,8,128]{2,1,0:T(8,128)(2,1)S(1)} %shard_map.106), channel_id=1, source_target_pairs={{0,32},{8,160},{16,96},{24,224},{32,64},{40,192},{48,128},{56,0},{... | collective-permute-start | bytes 393224 | tf_op jit(solution)/shard_map/ppermute | solution.py:343
  66.0 13.2 %collective-permute-start.15 = (bf16[64,8,128]{2,1,0:T(8,128)(2,1)S(1)}, bf16[64,8,128]{2,1,0:T(8,128)(2,1)S(1)}, u32[]{:S(2)}, u32[]{:S(2)}) collective-permute-start(bf16[64,8,128]{2,1,0:T(8,128)(2,1)S(1)} %shard_map.102), channel_id=1, source_target_pairs={{0,0},{8,64},{16,128},{24,192},{32,32},{40,96},{48,160},{56,224},{... | collective-permute-start | bytes 393224 | tf_op jit(solution)/shard_map/ppermute | solution.py:344

commit v4 on v3

--- a/solution.py
+++ b/solution.py
@@ -90,7 +90,8 @@
     token_col = tokens_of(tok_ref, k * T, T)
     weight = token_col * row_ref[...].astype(F32)
     wr = wr_ref[...]
-    pad = jnp.concatenate([jnp.broadcast_to(token_col, (T, S)), jnp.zeros((T, S), F32)], axis=0)
+    rows = row_ref[...].astype(F32)
+    pad = jnp.concatenate([jnp.broadcast_to(token_col, (T, S)), rows, jnp.zeros((T - 1, S), F32)], axis=0)
     out_ref[T * C :, :] = pad.astype(BF16)
     copies[0].wait()
     for t in range(T):
@@ -141,53 +142,46 @@
         out_ref[:, g * T : (g + 1) * T, :] = (part.reshape(C, T, S) * weight[None]).astype(BF16)
 
 
-def pair_blocks(blocks, lf_ref, w2_ref, row_ref, spread):
-    rhs = jnp.concatenate([rows for rows, _, _ in blocks], axis=0) if len(blocks) > 1 else blocks[0][0]
+def join_kernel(own, got, out):
+    half = T * C
+    out[:half, :] = own[:half, :]
+    out[half : 2 * half, :] = got[:half, :]
+    mine, other = own[half:, :].astype(F32), got[half:, :].astype(F32)
+    pad = jnp.concatenate([mine[: T + 1], other[T : T + 1], jnp.zeros((T - 2, S), F32)], axis=0)
+    out[2 * half :, :] = pad.astype(BF16)
+
+
+def pair_block(right, lf_own, lf_got, w2_ref, spread, out):
+    half = T * C
     for n in range(8):
-        part = lax.dot_general(
-            rhs, lf_ref[n * 256 : (n + 1) * 256, :], (((1,), (1,)), ((), ())), preferred_element_type=F32
+        part = sum(
+            lax.dot_general(
+                right[b * half : (b + 1) * half, :],
+                lf[n * 256 : (n + 1) * 256, :],
+                (((1,), (1,)), ((), ())),
+                preferred_element_type=F32,
+            )
+            for b, lf in enumerate((lf_own, lf_got))
         ).astype(BF16)
-        for b in range(len(blocks)):
-            for t in range(T):
-                for u in range(2):
-                    hi = n * 2 + u
-                    spread[b * T // 2 + t // 2, hi * C : (hi + 1) * C, (t % 2) * 128 : (t % 2) * 128 + 128] = part[
-                        (b * T + t) * C : (b * T + t + 1) * C, u * 128 : (u + 1) * 128
-                    ]
+        for t in range(T):
+            for u in range(2):
+                hi = n * 2 + u
+                spread[t // 2, hi * C : (hi + 1) * C, (t % 2) * 128 : (t % 2) * 128 + 128] = part[
+                    t * C : (t + 1) * C, u * 128 : (u + 1) * 128
+                ]
     low = lax.broadcasted_iota(jnp.int32, (Z, 128), 1) < N
-    rows_used = jnp.sum(row_ref[...].astype(F32), axis=1, keepdims=True)
+    w2 = w2_ref[...]
+    for p in range(T // 2):
+        both = jnp.dot(w2, spread[p], preferred_element_type=F32)
+        x0, y0 = both[:Z, :128], both[Z:, :128]
+        x1, y1 = both[:Z, 128:], both[Z:, 128:]
+        pair = jnp.where(low, x0, y1) + pltpu.roll(jnp.where(low, x1, y0), N, 1)
+        out[p * 128 : (p + 1) * 128, :] = pair.T
+    extra = right[2 * half :, :].astype(F32)
+    counts = jnp.sum(extra[T : T + 2], axis=1, keepdims=True)
+    rows_used = jnp.broadcast_to(counts[0:1] + counts[1:2], (EXTRA, Z))
     lane = lax.broadcasted_iota(jnp.int32, (EXTRA, Z), 1)
-    w2 = w2_ref[...]
-    for b, (_, extra, store) in enumerate(blocks):
-        for p in range(T // 2):
-            both = jnp.dot(w2, spread[b * T // 2 + p], preferred_element_type=F32)
-            x0, y0 = both[:Z, :128], both[Z:, :128]
-            x1, y1 = both[:Z, 128:], both[Z:, 128:]
-            pair = jnp.where(low, x0, y1) + pltpu.roll(jnp.where(low, x1, y0), N, 1)
-            flat = pair.T
-            store(pl.ds(2 * p, N, stride=T), flat[:N])
-            store(pl.ds(2 * p + 1, N, stride=T), flat[N:])
-        mask = jnp.broadcast_to(extra.astype(F32)[:EXTRA, :1], (EXTRA, Z))
-        store(pl.ds(ROWS, EXTRA), jnp.where(lane < N, jnp.broadcast_to(rows_used, (EXTRA, Z)), mask))
-
-
-def whole(ref):
-    return ref[: T * C, :], ref[T * C :, :]
-
-
-def halves(first, second):
-    return jnp.concatenate([first[...], second[:128, :]], axis=0), second[128:, :]
-
-
-def to(ref):
-    def store(where, value):
-        ref[where, :] = value
-
-    return store
-
-
-def half_of(ref, b):
-    return to(ref.at[b])
+    out[ROWS:, :] = jnp.where(lane < N, rows_used, jnp.broadcast_to(extra[:EXTRA, :1], (EXTRA, Z)))
 
 
 def choose(first, a, b, one, two):
@@ -199,32 +193,35 @@
     return lax.rem(lax.axis_index("col"), 2)
 
 
-def first_kernel(own, lf, w2, row, out, spread):
-    pair_blocks([whole(own) + (to(out),)], lf, w2, row, spread)
-
-
-def two_kernel(back, ahead, lf, w2, row, keep, send, spread, both):
-    pair_blocks([whole(back) + (half_of(both, 0),), whole(ahead) + (half_of(both, 1),)], lf, w2, row, spread)
-    choose(core() == 0, both[1], both[0], keep, send)
-
-
-def mixed_kernel(back, ahead, base, lf, w2, row, keep, send, rest, spread, both):
-    pair_blocks([whole(back) + (to(rest),), whole(ahead) + (half_of(both, 0),)], lf, w2, row, spread)
-    choose(core() == 0, base[...], both[0], keep, send)
-
-
-def last_kernel(first, second, rest, lf, w2, row, keep, send, spread, both):
-    pair_blocks([halves(first, second) + (half_of(both, 0),)], lf, w2, row, spread)
-    choose(core() == 0, both[0], rest[...], keep, send)
-
-
-def add_kernel(swapped, keep_a, got_a, keep_b, got_b, keep, send):
-    a = keep_a[...] + got_a[...]
-    b = keep_b[...] + got_b[...]
-    first = lax.axis_index("col") // 2 == 0
-    if swapped:
-        first = lax.axis_index("col") // 2 == core()
-    choose(first, a, b, keep, send)
+def x_half():
+    return lax.axis_index("col") // 2
+
+
+def first_kernel(right, lf_own, lf_got, w2, out, spread):
+    @pl.when(core() == 0)
+    def _():
+        pair_block(right, lf_own, lf_got, w2, spread, out)
+
+
+def next_kernel(right, lf_own, lf_got, w2, out, spread):
+    pair_block(right, lf_own, lf_got, w2, spread, out)
+
+
+def odd_kernel(right, one, lf_own, lf_got, w2, keep, send, spread, three):
+    pair_block(right, lf_own, lf_got, w2, spread, three)
+    choose(x_half() == 0, one[...], three[...], keep, send)
+
+
+def even_kernel(right, zero, two, lf_own, lf_got, w2, keep, send, spread, last):
+    @pl.when(core() == 1)
+    def _():
+        pair_block(right, lf_own, lf_got, w2, spread, last)
+
+    @pl.when(core() == 0)
+    def _():
+        last[...] = zero[...]
+
+    choose(x_half() == 0, two[...], last[...], keep, send)
 
 
 def final_kernel(keep, got, tok_ref, bias_ref, out):
@@ -233,9 +230,18 @@
     rows_used = tail[0:1, 0:1]
     second = (tail[:, N : N + 1] > 0.0).astype(F32)
     first = column_of(tok_ref[...].astype(F32))
-    count = jnp.maximum(rows_used[None] * first[:, :, None] * second[None], 1.0)
-    pairs = total[:ROWS, :].reshape(N, T, Z)
-    out[...] = ((pairs + bias_ref[...][None]) / count).astype(BF16)
+    count = jnp.maximum(rows_used[None] * first[None] * second[:, :, None], 1.0)
+    pairs = total[:ROWS, :].reshape(T, N, Z)
+    out[...] = ((pairs + bias_ref[...][None]) / count).reshape(ROWS, Z).astype(BF16)
+
+
+def assemble_kernel(odd, even, out, flat):
+    low = lax.rem(lax.axis_index("row"), 2) == 0
+    a, b = odd[...].astype(F32), even[...].astype(F32)
+    for h, rows in enumerate((jnp.where(low, b, a), jnp.where(low, a, b))):
+        for t in range(T):
+            flat[h, pl.ds(t, N, stride=T), :] = rows[t * N : (t + 1) * N]
+        out[h * N : (h + 1) * N] = flat[h].reshape(N, T, Z).astype(BF16)
 
 
 def call(kernel, out, *args, specs=None, scratch=(), flops=0, limit=10):
@@ -266,7 +272,6 @@
     tok = token_mask.reshape(1, N)
     gain, bias = gain.reshape(1, M), bias.reshape(1, M)
 
-    ring = [[(i, (i + d) % 8) for i in range(8)] for d in (1, -1)]
     y_ring = {d: [(a * 4 + b, a * 4 + (b + d) % 4) for a in range(2) for b in range(4)] for d in (1, -1, 2)}
     x_swap = [(c, (c + 4) % 8) for c in range(8)]
     core_swap = [(0, 1), (1, 0), (2, 3), (3, 2)]
@@ -288,15 +293,12 @@
         flops=20 << 20, limit=8,
     )
 
-    ahead, back = own, own
-    from_back, from_ahead = [], []
-    for _ in range(3):
-        back = lax.ppermute(back, "row", ring[0])
-        ahead = lax.ppermute(ahead, "row", ring[1])
-        from_back.append(back)
-        from_ahead.append(ahead)
-    half_a = lax.ppermute(back[:128], "row", ring[0])
-    half_b = lax.ppermute(ahead[128:], "row", ring[1])
+    got = lax.ppermute(own, "col", core_swap)
+    right = [call(join_kernel, shape((2 * T * C + 16, S), BF16), own, got, limit=4)]
+
+    for step in range(4):
+        pairs = [(z * 4 + c, (z + 1 - 2 * (c % 2)) % 8 * 4 + c) for z in range(8) for c in range(4) if step < 3 or c % 2]
+        right.append(lax.ppermute(right[-1], ("row", "col"), pairs))
 
     normed = [
         call(
@@ -309,30 +311,21 @@
     ]
     left = call(left_kernel, shape((C, N, S), BF16), *normed, wl_all, row, tok, flops=1 << 30, limit=8)
     lf = left.reshape(C * N, S)
+    lf_got = lax.ppermute(lf, "col", core_swap)
 
     block = shape((ROWS + EXTRA, Z), F32)
-    pair = (block, block)
-    one = 800 << 20
-    shared = (lf, w2, row)
-
-    def spread(n):
-        return [pltpu.VMEM((n * T // 2, 512, 256), BF16), pltpu.VMEM((n, ROWS + EXTRA, Z), F32)]
-
-    p0 = call(first_kernel, block, own, *shared, scratch=spread(1)[:1], flops=one)
-    k1, s1 = call(two_kernel, pair, from_back[0], from_ahead[0], *shared, scratch=spread(2), flops=2 * one)
-    k2, s2, rest = call(mixed_kernel, (block,) * 3, from_back[1], from_ahead[1], p0, *shared, scratch=spread(2), flops=2 * one)
-    k3, s3 = call(two_kernel, pair, from_back[2], from_ahead[2], *shared, scratch=spread(2), flops=2 * one)
-    k4, s4 = call(last_kernel, pair, half_a, half_b, rest, *shared, scratch=spread(1), flops=one)
-
-    e1 = lax.ppermute(s1, "col", core_swap)
-    e2 = lax.ppermute(s2, "col", core_swap)
-    e3 = lax.ppermute(s3, "col", core_swap)
-    e4 = lax.ppermute(s4, "col", core_swap)
-    odd, odd_sent = call(functools.partial(add_kernel, True), pair, k1, e1, k3, e3)
+    one = 1400 << 20
+    shared = (lf, lf_got, w2)
+    spread = [pltpu.VMEM((T // 2, 512, 256), BF16)]
+    more = spread + [pltpu.VMEM((ROWS + EXTRA, Z), F32)]
+    p0 = call(first_kernel, block, right[0], *shared, scratch=spread, flops=one)
+    p1 = call(next_kernel, block, right[1], *shared, scratch=spread, flops=one)
+    p2 = call(next_kernel, block, right[2], *shared, scratch=spread, flops=one)
+    odd, odd_sent = call(odd_kernel, (block,) * 2, right[3], p1, *shared, scratch=more, flops=one)
     f1 = lax.ppermute(odd_sent, "col", xh_swap)
-    even, even_sent = call(functools.partial(add_kernel, False), pair, k2, e2, k4, e4)
+    even, even_sent = call(even_kernel, (block,) * 2, right[4], p0, p2, *shared, scratch=more, flops=one)
     f2 = lax.ppermute(even_sent, "col", xh_swap)
-    part = shape((N, T, Z), BF16)
+    part = shape((ROWS, Z), BF16)
     out_bias = out_bias.reshape(1, Z)
     y1 = call(final_kernel, part, odd, f1, tok, out_bias)
     y2 = call(final_kernel, part, even, f2, tok, out_bias)
@@ -340,10 +333,9 @@
     def home(kept):
         return [(z * 4 + c, (z + kept[c]) % 8 * 4 + z // 2) for z in range(8) for c in range(4)]
 
-    g1 = lax.ppermute(y1, ("row", "col"), home((1, -3, 3, -1)))
-    g2 = lax.ppermute(y2, ("row", "col"), home((0, 2, 4, -2)))
-    low_row = lax.axis_index("row") % 2 == 0
-    return jnp.where(low_row, jnp.concatenate([g2, g1], 0), jnp.concatenate([g1, g2], 0))
+    g1 = lax.ppermute(y1, ("row", "col"), home((-1, 1, -3, 3)))
+    g2 = lax.ppermute(y2, ("row", "col"), home((-2, 2, 0, 4)))
+    return call(assemble_kernel, shape((2 * N, T, Z), BF16), g1, g2, scratch=[pltpu.VMEM((2, ROWS, Z), F32)], limit=4)
 
 
 def solution(mesh):

time: 80.1 us -> 93 us (1.16)
  the two profiles are of different devices: /device:TPU:1 before, /device:TPU:4 now
where the time goes in v4:
time: 93 us; the launch traced here: 92.7 us
  waiting for transfers between devices  55.3 us (59%)
  Pallas kernels  17.4 us (19%)
  starting transfers between devices  17 us (18%)
  local copies, waits for them, and re-layouts  2.77 us (3%)
    ppermute x4, waiting for transfers between devices, program(): right.append(lax.ppermute(right[-1], ('row', 'col'), pairs))  32.4 us
    pallas_call x16, Pallas kernels, call(): pl.pallas_call(kernel, out_shape=out, in_specs=specs or [VMEM] * len(args...  17.4 us
    ppermute x1, waiting for transfers between devices, program(): g2 = lax.ppermute(y2, ('row', 'col'), home((-2, 2, 0, 4)))  8.37 us
    ppermute x1, waiting for transfers between devices, program(): f2 = lax.ppermute(even_sent, 'col', xh_swap)  5.24 us
    ppermute x1, waiting for transfers between devices, program(): f1 = lax.ppermute(odd_sent, 'col', xh_swap)  3.48 us
    ppermute x1, starting transfers between devices, program(): g2 = lax.ppermute(y2, ('row', 'col'), home((-2, 2, 0, 4)))  3.21 us
    ppermute x1, waiting for transfers between devices, program(): over = lax.ppermute(pack, 'chan', y_ring[2])  3.16 us
    ppermute x4, starting transfers between devices, program(): right.append(lax.ppermute(right[-1], ('row', 'col'), pairs))  2.86 us
  transfers between devices with their start and end apart: 14, of which 9 were waited for; matrix products, arithmetic and copies ran while one was open for 0% of the time, Pallas kernels for 16%

profile of v4, /device:TPU:4, one launch (start us, length us, event | category | flops | bytes accessed | tf_op | source)
XLA Modules:
  0.0 92.7 jit_solution(9599485406177971162)
XLA Ops:
  0.0 0.0 copy-start
  0.0 0.8 copy-done
  0.8 0.0 copy-start.8
  0.8 0.7 copy-done.8
  1.4 1.6 %collective-permute-start.4 = (bf16[144,128]{1,0:T(8,128)(2,1)S(1)}, bf16[144,128]{1,0:T(8,128)(2,1)S(1)}, u32[]{:S(2)}, u32[]{:S(2)}) collective-permute-start(bf16[144,128]{1,0:T(8,128)(2,1)S(1)} %shard_map.95.a), channel_id=1, source_target_pairs={{0,1},{1,2},{2,3},{3,0},{4,5},{5,6},{6,7},{7,4},{8,9},{9,10},{10,1... | collective-permute-start | bytes 110600 | tf_op jit(solution)/shard_map/ppermute | solution.py:281
  3.0 1.7 %collective-permute-start.5 = (bf16[144,128]{1,0:T(8,128)(2,1)S(1)}, bf16[144,128]{1,0:T(8,128)(2,1)S(1)}, u32[]{:S(2)}, u32[]{:S(2)}) collective-permute-start(bf16[144,128]{1,0:T(8,128)(2,1)S(1)} %shard_map.95.a), channel_id=1, source_target_pairs={{0,3},{1,0},{2,1},{3,2},{4,7},{5,4},{6,5},{7,6},{8,11},{9,8},{10,9... | collective-permute-start | bytes 110600 | tf_op jit(solution)/shard_map/ppermute | solution.py:282
  4.7 2.0 %collective-permute-start.6 = (bf16[144,128]{1,0:T(8,128)(2,1)S(1)}, bf16[144,128]{1,0:T(8,128)(2,1)S(1)}, u32[]{:S(2)}, u32[]{:S(2)}) collective-permute-start(bf16[144,128]{1,0:T(8,128)(2,1)S(1)} %shard_map.95.a), channel_id=1, source_target_pairs={{0,2},{1,3},{2,0},{3,1},{4,6},{5,7},{6,4},{7,5},{8,10},{9,11},{10,... | collective-permute-start | bytes 110600 | tf_op jit(solution)/shard_map/ppermute | solution.py:283
  6.7 0.0 collective-permute-done.4.b
  6.7 0.3 collective-permute-done.5.c
  7.0 3.2 %collective-permute-done.6.d = bf16[144,128]{1,0:T(8,128)(2,1)S(1)} collective-permute-done((bf16[144,128]{1,0:T(8,128)(2,1)S(1)}, bf16[144,128]{1,0:T(8,128)(2,1)S(1)}, u32[]{:S(2)}, u32[]{:S(2)}) %collective-permute-start.6) | collective-permute-done | bytes 36896 | tf_op jit(solution)/shard_map/ppermute | solution.py:283
  10.2 1.3 %collective-permute-start.7 = (bf16[4,144,128]{2,1,0:T(8,128)(2,1)S(1)}, bf16[4,144,128]{2,1,0:T(8,128)(2,1)S(1)}, u32[]{:S(2)}, u32[]{:S(2)}) collective-permute-start(bf16[4,144,128]{2,1,0:T(8,128)(2,1)S(1)} %shard_map.96.near), channel_id=1, source_target_pairs={{0,4},{1,5},{2,6},{3,7},{4,0},{5,1},{6,2},{7,3},{8,12},{9,13},{10,... | collective-permute-start | bytes 442376 | tf_op jit(solution)/shard_map/ppermute | solution.py:285
  11.4 0.0 copy-start.4
  11.4 0.7 copy-done.4
  12.1 0.0 copy-start.5
  12.1 0.7 copy-done.5
  12.8 0.0 copy-start.6
  12.8 2.7 %shard_map.93.n_a = bf16[2048,512]{1,0:T(8,128)(2,1)S(1)} custom-call(bf16[64,64,512]{2,1,0:T(8,128)(2,1)} %bitcast.30, f32[1,64]{1,0:T(1,128)S(1)} %bitcast.22, f32[1,64]{1,0:T(1,128)S(1)} %bitcast.25), custom_call_target="tpu_custom_call" | custom-call | flops 15728640 | bytes 6291968 | tf_op jit(solution)/shard_map/pallas_call | solution.py:250
  15.4 0.0 copy-done.6
  15.4 0.0 copy-start.1
  15.4 0.0 copy-start.2
  15.5 2.7 %shard_map.94.n_b = bf16[2048,512]{1,0:T(8,128)(2,1)S(1)} custom-call(bf16[64,64,512]{2,1,0:T(8,128)(2,1)} %bitcast.31, f32[1,64]{1,0:T(1,128)S(1)} %bitcast.23, f32[1,64]{1,0:T(1,128)S(1)} %bitcast.26), custom_call_target="tpu_custom_call" | custom-call | flops 15728640 | bytes 6291968 | tf_op jit(solution)/shard_map/pallas_call | solution.py:250
  18.1 0.0 collective-permute-done.7.far
  18.1 0.3 shard_map.97
  18.4 0.0 copy-done.1
  18.4 0.0 copy-done.2
  18.4 1.5 %shard_map.98 = bf16[32,64,512]{2,1,0:T(8,128)(2,1)S(1)} custom-call(bf16[2048,512]{1,0:T(8,128)(2,1)S(1)} %shard_map.93.n_a, bf16[2048,512]{1,0:T(8,128)(2,1)S(1)} %shard_map.94.n_b, bf16[32,64]{1,0:T(8,128)(2,1)S(1)} %get-tuple-element.11.wl_ref, s32[1,512]{1,0:T(1,128)S(1)} %bitcast.16, s32[1,64]{1,0:T(1,128)S(1)} %bitcast.18), custom_call_target="tpu_custom_call" | custom-call | flops 1073741824 | bytes 6297856 | tf_op jit(solution)/shard_map/pallas_call | solution.py:250
  19.9 0.1 collective-permute-start.8
  20.0 1.6 %shard_map.91.own = bf16[272,512]{1,0:T(8,128)(2,1)S(1)} custom-call(bf16[64,64,512]{2,1,0:T(8,128)(2,1)} %bitcast.32, s32[1,512]{1,0:T(1,128)} %bitcast.15, s32[1,64]{1,0:T(1,128)} %bitcast.17, f32[1,64]{1,0:T(1,128)} %bitcast.21, f32[1,64]{1,0:T(1,128)} %bitcast.24, bf16[32,64]{1,0:T(8,128)(2,1)} %bitcast.33), custom_call_target="tpu_custom_call" | custom-call | flops 20971520 | bytes 4479744 | tf_op jit(solution)/shard_map/pallas_call | solution.py:250
  21.7 0.6 collective-permute-start
  22.2 2.3 %collective-permute-done.got = bf16[272,512]{1,0:T(8,128)(2,1)S(1)} collective-permute-done((bf16[272,512]{1,0:T(8,128)(2,1)S(1)}, bf16[272,512]{1,0:T(8,128)(2,1)S(1)}, u32[]{:S(2)}, u32[]{:S(2)}) %collective-permute-start) | collective-permute-done | bytes 278560 | tf_op jit(solution)/shard_map/ppermute | solution.py:296
  24.6 2.0 %collective-permute-start.1 = (bf16[528,512]{1,0:T(8,128)(2,1)S(1)}, bf16[528,512]{1,0:T(8,128)(2,1)S(1)}, u32[]{:S(2)}, u32[]{:S(2)}) collective-permute-start(bf16[528,512]{1,0:T(8,128)(2,1)S(1)} %shard_map.92.right), channel_id=1, source_target_pairs={{0,32},{8,232},{16,48},{24,248},{32,64},{40,8},{48,80},{56,24},{64... | collective-permute-start | bytes 1622024 | tf_op jit(solution)/shard_map/ppermute | solution.py:301
  26.6 11.3 %collective-permute-done.1.right = bf16[528,512]{1,0:T(8,128)(2,1)S(1)} collective-permute-done((bf16[528,512]{1,0:T(8,128)(2,1)S(1)}, bf16[528,512]{1,0:T(8,128)(2,1)S(1)}, u32[]{:S(2)}, u32[]{:S(2)}) %collective-permute-start.1) | collective-permute-done | bytes 540704 | tf_op jit(solution)/shard_map/ppermute | solution.py:301
  37.9 0.0 collective-permute-start.2
  37.9 10.6 %collective-permute-done.2.right = bf16[528,512]{1,0:T(8,128)(2,1)S(1)} collective-permute-done((bf16[528,512]{1,0:T(8,128)(2,1)S(1)}, bf16[528,512]{1,0:T(8,128)(2,1)S(1)}, u32[]{:S(2)}, u32[]{:S(2)}) %collective-permute-start.2) | collective-permute-done | bytes 540704 | tf_op jit(solution)/shard_map/ppermute | solution.py:301
  48.4 0.0 collective-permute-start.3
  48.5 10.6 %collective-permute-done.3.right = bf16[528,512]{1,0:T(8,128)(2,1)S(1)} collective-permute-done((bf16[528,512]{1,0:T(8,128)(2,1)S(1)}, bf16[528,512]{1,0:T(8,128)(2,1)S(1)}, u32[]{:S(2)}, u32[]{:S(2)}) %collective-permute-start.3) | collective-permute-done | bytes 540704 | tf_op jit(solution)/shard_map/ppermute | solution.py:301
  59.0 0.9 collective-permute-start.11
  59.9 0.0 collective-permute-done.8.lf_got
  59.9 1.8 %shard_map.99.one = f32[520,128]{1,0:T(8,128)S(1)} custom-call(bf16[528,512]{1,0:T(8,128)(2,1)S(1)} %collective-permute-done.1.right, bf16[2048,512]{1,0:T(8,128)(2,1)S(1)} %bitcast.10, bf16[2048,512]{1,0:T(8,128)(2,1)S(1)} %collective-permute-done.8.lf_got, bf16[256,512]{1,0:T(8,128)(2,1)S(1)} %get-tuple-element.12.w2), custom_call_target="tpu_custom_call" | custom-call | flops 1468006400 | bytes 5263360 | tf_op jit(solution)/shard_map/pallas_call | solution.py:250
  61.7 1.8 %shard_map.100 = (f32[520,128]{1,0:T(8,128)S(1)}, f32[520,128]{1,0:T(8,128)S(1)}) custom-call(bf16[528,512]{1,0:T(8,128)(2,1)S(1)} %collective-permute-done.3.right, f32[520,128]{1,0:T(8,128)S(1)} %shard_map.99.one, bf16[2048,512]{1,0:T(8,128)(2,1)S(1)} %bitcast.11, bf16[2048,512]{1,0:T(8,128)(2,1)S(1)} %collective-permute-done.8.lf_got, ...), custom_call_target="tpu_custom_call" | custom-call | flops 1468006400 | bytes 5795840 | tf_op jit(solution)/shard_map/pallas_call | solution.py:250
  63.6 0.9 collective-permute-start.9
  64.4 1.8 %shard_map.103.two = f32[520,128]{1,0:T(8,128)S(1)} custom-call(bf16[528,512]{1,0:T(8,128)(2,1)S(1)} %collective-permute-done.2.right, bf16[2048,512]{1,0:T(8,128)(2,1)S(1)} %bitcast.12, bf16[2048,512]{1,0:T(8,128)(2,1)S(1)} %collective-permute-done.8.lf_got, bf16[256,512]{1,0:T(8,128)(2,1)S(1)} %get-tuple-element.12.w2), custom_call_target="tpu_custom_call" | custom-call | flops 1468006400 | bytes 5263360 | tf_op jit(solution)/shard_map/pallas_call | solution.py:250
  66.2 1.8 %shard_map.102.zero = f32[520,128]{1,0:T(8,128)S(1)} custom-call(bf16[528,512]{1,0:T(8,128)(2,1)S(1)} %shard_map.92.right, bf16[2048,512]{1,0:T(8,128)(2,1)S(1)} %bitcast.13, bf16[2048,512]{1,0:T(8,128)(2,1)S(1)} %collective-permute-done.8.lf_got, bf16[256,512]{1,0:T(8,128)(2,1)S(1)} %get-tuple-element.12.w2), custom_call_target="tpu_custom_call" | custom-call | flops 1468006400 | bytes 5263360 | tf_op jit(solution)/shard_map/pallas_call | solution.py:250
  68.0 0.0 copy-start.3
  68.0 0.0 copy-start.7
  68.0 0.0 collective-permute-done.11.right
  68.0 0.1 shard_map.104
  68.1 2.8 %collective-permute-start.12 = (f32[520,128]{1,0:T(8,128)S(1)}, f32[520,128]{1,0:T(8,128)S(1)}, u32[]{:S(2)}, u32[]{:S(2)}) collective-permute-start(f32[520,128]{1,0:T(8,128)S(1)} %get-tuple-element.16), channel_id=1, source_target_pairs={{0,16},{8,24},{16,0},{24,8},{1,17},{9,25},{17,1},{25,9},{2,18},{10... | collective-permute-start | bytes 798728 | tf_op jit(solution)/shard_map/ppermute | solution.py:327
  70.9 3.5 %collective-permute-done.9.got = f32[520,128]{1,0:T(8,128)S(1)} collective-permute-done((f32[520,128]{1,0:T(8,128)S(1)}, f32[520,128]{1,0:T(8,128)S(1)}, u32[]{:S(2)}, u32[]{:S(2)}) %collective-permute-start.9) | collective-permute-done | bytes 266272 | tf_op jit(solution)/shard_map/ppermute | solution.py:325
  74.4 0.0 copy-done.3
  74.4 0.0 copy-done.7
  74.4 0.2 shard_map.101
  74.7 0.1 collective-permute-start.10
  74.8 5.2 %collective-permute-done.12.got = f32[520,128]{1,0:T(8,128)S(1)} collective-permute-done((f32[520,128]{1,0:T(8,128)S(1)}, f32[520,128]{1,0:T(8,128)S(1)}, u32[]{:S(2)}, u32[]{:S(2)}) %collective-permute-start.12) | collective-permute-done | bytes 266272 | tf_op jit(solution)/shard_map/ppermute | solution.py:327
  80.0 0.2 shard_map.105
  80.3 3.2 %collective-permute-start.13 = (bf16[512,128]{1,0:T(8,128)(2,1)S(1)}, bf16[512,128]{1,0:T(8,128)(2,1)S(1)}, u32[]{:S(2)}, u32[]{:S(2)}) collective-permute-start(bf16[512,128]{1,0:T(8,128)(2,1)S(1)} %shard_map.105), channel_id=1, source_target_pairs={{0,192},{8,64},{16,0},{24,128},{32,224},{40,96},{48,32},{56,160},{... | collective-permute-start | bytes 393224 | tf_op jit(solution)/shard_map/ppermute | solution.py:337
  83.5 0.0 collective-permute-done.10.odd
  83.5 8.4 %collective-permute-done.13.even = bf16[512,128]{1,0:T(8,128)(2,1)S(1)} collective-permute-done((bf16[512,128]{1,0:T(8,128)(2,1)S(1)}, bf16[512,128]{1,0:T(8,128)(2,1)S(1)}, u32[]{:S(2)}, u32[]{:S(2)}) %collective-permute-start.13) | collective-permute-done | bytes 131104 | tf_op jit(solution)/shard_map/ppermute | solution.py:337
  91.9 0.8 shard_map.106
  (3 shorter events, 0.1 us)
Async XLA Ops:
  0.0 0.8 copy-start
  0.8 0.7 copy-start.8
  1.4 5.2 %collective-permute-start.4 = (bf16[144,128]{1,0:T(8,128)(2,1)S(1)}, bf16[144,128]{1,0:T(8,128)(2,1)S(1)}, u32[]{:S(2)}, u32[]{:S(2)}) collective-permute-start(bf16[144,128]{1,0:T(8,128)(2,1)S(1)} %shard_map.95.a), channel_id=1, source_target_pairs={{0,1},{1,2},{2,3},{3,0},{4,5},{5,6},{6,7},{7,4},{8,9},{9,10},{10,1... | collective-permute-start | bytes 110600 | tf_op jit(solution)/shard_map/ppermute | solution.py:281
  3.0 4.0 %collective-permute-start.5 = (bf16[144,128]{1,0:T(8,128)(2,1)S(1)}, bf16[144,128]{1,0:T(8,128)(2,1)S(1)}, u32[]{:S(2)}, u32[]{:S(2)}) collective-permute-start(bf16[144,128]{1,0:T(8,128)(2,1)S(1)} %shard_map.95.a), channel_id=1, source_target_pairs={{0,3},{1,0},{2,1},{3,2},{4,7},{5,4},{6,5},{7,6},{8,11},{9,8},{10,9... | collective-permute-start | bytes 110600 | tf_op jit(solution)/shard_map/ppermute | solution.py:282
  4.7 5.5 %collective-permute-start.6 = (bf16[144,128]{1,0:T(8,128)(2,1)S(1)}, bf16[144,128]{1,0:T(8,128)(2,1)S(1)}, u32[]{:S(2)}, u32[]{:S(2)}) collective-permute-start(bf16[144,128]{1,0:T(8,128)(2,1)S(1)} %shard_map.95.a), channel_id=1, source_target_pairs={{0,2},{1,3},{2,0},{3,1},{4,6},{5,7},{6,4},{7,5},{8,10},{9,11},{10,... | collective-permute-start | bytes 110600 | tf_op jit(solution)/shard_map/ppermute | solution.py:283
  10.2 8.0 %collective-permute-start.7 = (bf16[4,144,128]{2,1,0:T(8,128)(2,1)S(1)}, bf16[4,144,128]{2,1,0:T(8,128)(2,1)S(1)}, u32[]{:S(2)}, u32[]{:S(2)}) collective-permute-start(bf16[4,144,128]{2,1,0:T(8,128)(2,1)S(1)} %shard_map.96.near), channel_id=1, source_target_pairs={{0,4},{1,5},{2,6},{3,7},{4,0},{5,1},{6,2},{7,3},{8,12},{9,13},{10,... | collective-permute-start | bytes 442376 | tf_op jit(solution)/shard_map/ppermute | solution.py:285
  11.4 0.7 copy-start.4
  12.1 0.7 copy-start.5
  12.8 2.7 %copy-start.6 = (f32[64]{0:T(128)S(1)}, f32[64]{0:T(128)}, u32[]{:S(2)}) copy-start(f32[64]{0:T(128)} %param.13) | copy-start | bytes 772
  15.4 3.0 %copy-start.1 = (s32[512]{0:T(512)S(1)}, s32[512]{0:T(512)}, u32[]{:S(2)}) copy-start(s32[512]{0:T(512)} %param.10) | copy-start | bytes 6148
  15.4 3.0 %copy-start.2 = (s32[64]{0:T(128)S(1)}, s32[64]{0:T(128)}, u32[]{:S(2)}) copy-start(s32[64]{0:T(128)} %param.11) | copy-start | bytes 772
  19.9 40.0 %collective-permute-start.8 = (bf16[2048,512]{1,0:T(8,128)(2,1)S(1)}, bf16[2048,512]{1,0:T(8,128)(2,1)S(1)}, u32[]{:S(2)}, u32[]{:S(2)}) collective-permute-start(bf16[2048,512]{1,0:T(8,128)(2,1)S(1)} %bitcast.9), channel_id=1, source_target_pairs={{0,8},{8,0},{16,24},{24,16},{1,9},{9,1},{17,25},{25,17},{2,10},{10... | collective-permute-start | bytes 6291464 | tf_op jit(solution)/shard_map/ppermute | solution.py:314
  21.7 2.9 %collective-permute-start = (bf16[272,512]{1,0:T(8,128)(2,1)S(1)}, bf16[272,512]{1,0:T(8,128)(2,1)S(1)}, u32[]{:S(2)}, u32[]{:S(2)}) collective-permute-start(bf16[272,512]{1,0:T(8,128)(2,1)S(1)} %shard_map.91.own), channel_id=1, source_target_pairs={{0,8},{8,0},{16,24},{24,16},{1,9},{9,1},{17,25},{25,17},{2,10},{10... | collective-permute-start | bytes 835592 | tf_op jit(solution)/shard_map/ppermute | solution.py:296
  24.6 13.3 %collective-permute-start.1 = (bf16[528,512]{1,0:T(8,128)(2,1)S(1)}, bf16[528,512]{1,0:T(8,128)(2,1)S(1)}, u32[]{:S(2)}, u32[]{:S(2)}) collective-permute-start(bf16[528,512]{1,0:T(8,128)(2,1)S(1)} %shard_map.92.right), channel_id=1, source_target_pairs={{0,32},{8,232},{16,48},{24,248},{32,64},{40,8},{48,80},{56,24},{64... | collective-permute-start | bytes 1622024 | tf_op jit(solution)/shard_map/ppermute | solution.py:301
  37.9 10.6 %collective-permute-start.2 = (bf16[528,512]{1,0:T(8,128)(2,1)S(1)}, bf16[528,512]{1,0:T(8,128)(2,1)S(1)}, u32[]{:S(2)}, u32[]{:S(2)}) collective-permute-start(bf16[528,512]{1,0:T(8,128)(2,1)S(1)} %collective-permute-done.1.right), channel_id=1, source_target_pairs={{0,32},{8,232},{16,48},{24,248},{32,64},{40,8},{48,80},{56,24},{64... | collective-permute-start | bytes 1622024 | tf_op jit(solution)/shard_map/ppermute | solution.py:301
  48.4 10.6 %collective-permute-start.3 = (bf16[528,512]{1,0:T(8,128)(2,1)S(1)}, bf16[528,512]{1,0:T(8,128)(2,1)S(1)}, u32[]{:S(2)}, u32[]{:S(2)}) collective-permute-start(bf16[528,512]{1,0:T(8,128)(2,1)S(1)} %collective-permute-done.2.right), channel_id=1, source_target_pairs={{0,32},{8,232},{16,48},{24,248},{32,64},{40,8},{48,80},{56,24},{64... | collective-permute-start | bytes 1622024 | tf_op jit(solution)/shard_map/ppermute | solution.py:301
  59.0 9.0 %collective-permute-start.11 = (bf16[528,512]{1,0:T(8,128)(2,1)S(1)}, bf16[528,512]{1,0:T(8,128)(2,1)S(1)}, u32[]{:S(2)}, u32[]{:S(2)}) collective-permute-start(bf16[528,512]{1,0:T(8,128)(2,1)S(1)} %collective-permute-done.3.right), channel_id=1, source_target_pairs={{8,232},{24,248},{40,8},{56,24},{72,40},{88,56},{104,72},{120,88},... | collective-permute-start | bytes 1622024 | tf_op jit(solution)/shard_map/ppermute | solution.py:301
  63.6 10.9 %collective-permute-start.9 = (f32[520,128]{1,0:T(8,128)S(1)}, f32[520,128]{1,0:T(8,128)S(1)}, u32[]{:S(2)}, u32[]{:S(2)}) collective-permute-start(f32[520,128]{1,0:T(8,128)S(1)} %get-tuple-element.14), channel_id=1, source_target_pairs={{0,16},{8,24},{16,0},{24,8},{1,17},{9,25},{17,1},{25,9},{2,18},{10... | collective-permute-start | bytes 798728 | tf_op jit(solution)/shard_map/ppermute | solution.py:325
  68.0 6.4 %copy-start.3 = (s32[64]{0:T(128)S(1)}, s32[64]{0:T(128)}, u32[]{:S(2)}) copy-start(s32[64]{0:T(128)} %param.11) | copy-start | bytes 772
  68.0 6.4 %copy-start.7 = (f32[128]{0:T(128)S(1)}, f32[128]{0:T(128)}, u32[]{:S(2)}) copy-start(f32[128]{0:T(128)} %param.17) | copy-start | bytes 1540
  68.1 11.9 %collective-permute-start.12 = (f32[520,128]{1,0:T(8,128)S(1)}, f32[520,128]{1,0:T(8,128)S(1)}, u32[]{:S(2)}, u32[]{:S(2)}) collective-permute-start(f32[520,128]{1,0:T(8,128)S(1)} %get-tuple-element.16), channel_id=1, source_target_pairs={{0,16},{8,24},{16,0},{24,8},{1,17},{9,25},{17,1},{25,9},{2,18},{10... | collective-permute-start | bytes 798728 | tf_op jit(solution)/shard_map/ppermute | solution.py:327
  74.7 8.8 %collective-permute-start.10 = (bf16[512,128]{1,0:T(8,128)(2,1)S(1)}, bf16[512,128]{1,0:T(8,128)(2,1)S(1)}, u32[]{:S(2)}, u32[]{:S(2)}) collective-permute-start(bf16[512,128]{1,0:T(8,128)(2,1)S(1)} %shard_map.101), channel_id=1, source_target_pairs={{0,224},{8,32},{16,160},{24,96},{32,0},{40,64},{48,192},{56,128},{... | collective-permute-start | bytes 393224 | tf_op jit(solution)/shard_map/ppermute | solution.py:336
  80.3 11.6 %collective-permute-start.13 = (bf16[512,128]{1,0:T(8,128)(2,1)S(1)}, bf16[512,128]{1,0:T(8,128)(2,1)S(1)}, u32[]{:S(2)}, u32[]{:S(2)}) collective-permute-start(bf16[512,128]{1,0:T(8,128)(2,1)S(1)} %shard_map.105), channel_id=1, source_target_pairs={{0,192},{8,64},{16,0},{24,128},{32,224},{40,96},{48,32},{56,160},{... | collective-permute-start | bytes 393224 | tf_op jit(solution)/shard_map/ppermute | solution.py:337

commit v5 on v4

--- a/solution.py
+++ b/solution.py
@@ -142,26 +142,16 @@
         out_ref[:, g * T : (g + 1) * T, :] = (part.reshape(C, T, S) * weight[None]).astype(BF16)
 
 
-def join_kernel(own, got, out):
-    half = T * C
-    out[:half, :] = own[:half, :]
-    out[half : 2 * half, :] = got[:half, :]
-    mine, other = own[half:, :].astype(F32), got[half:, :].astype(F32)
-    pad = jnp.concatenate([mine[: T + 1], other[T : T + 1], jnp.zeros((T - 2, S), F32)], axis=0)
-    out[2 * half :, :] = pad.astype(BF16)
-
-
-def pair_block(right, lf_own, lf_got, w2_ref, spread, out):
-    half = T * C
+def pair_block(right, other, lf_own, lf_got, w2_ref, spread, out):
     for n in range(8):
         part = sum(
             lax.dot_general(
-                right[b * half : (b + 1) * half, :],
+                factor[: T * C, :],
                 lf[n * 256 : (n + 1) * 256, :],
                 (((1,), (1,)), ((), ())),
                 preferred_element_type=F32,
             )
-            for b, lf in enumerate((lf_own, lf_got))
+            for factor, lf in ((right, lf_own), (other, lf_got))
         ).astype(BF16)
         for t in range(T):
             for u in range(2):
@@ -177,9 +167,9 @@
         x1, y1 = both[:Z, 128:], both[Z:, 128:]
         pair = jnp.where(low, x0, y1) + pltpu.roll(jnp.where(low, x1, y0), N, 1)
         out[p * 128 : (p + 1) * 128, :] = pair.T
-    extra = right[2 * half :, :].astype(F32)
-    counts = jnp.sum(extra[T : T + 2], axis=1, keepdims=True)
-    rows_used = jnp.broadcast_to(counts[0:1] + counts[1:2], (EXTRA, Z))
+    extra = right[T * C :, :].astype(F32)
+    rows = extra[T : T + 1] + other[T * C :, :].astype(F32)[T : T + 1]
+    rows_used = jnp.broadcast_to(jnp.sum(rows, axis=1, keepdims=True), (EXTRA, Z))
     lane = lax.broadcasted_iota(jnp.int32, (EXTRA, Z), 1)
     out[ROWS:, :] = jnp.where(lane < N, rows_used, jnp.broadcast_to(extra[:EXTRA, :1], (EXTRA, Z)))
 
@@ -197,25 +187,25 @@
     return lax.axis_index("col") // 2
 
 
-def first_kernel(right, lf_own, lf_got, w2, out, spread):
+def first_kernel(right, other, lf_own, lf_got, w2, out, spread):
     @pl.when(core() == 0)
     def _():
-        pair_block(right, lf_own, lf_got, w2, spread, out)
-
-
-def next_kernel(right, lf_own, lf_got, w2, out, spread):
-    pair_block(right, lf_own, lf_got, w2, spread, out)
-
-
-def odd_kernel(right, one, lf_own, lf_got, w2, keep, send, spread, three):
-    pair_block(right, lf_own, lf_got, w2, spread, three)
+        pair_block(right, other, lf_own, lf_got, w2, spread, out)
+
+
+def next_kernel(right, other, lf_own, lf_got, w2, out, spread):
+    pair_block(right, other, lf_own, lf_got, w2, spread, out)
+
+
+def odd_kernel(right, other, one, lf_own, lf_got, w2, keep, send, spread, three):
+    pair_block(right, other, lf_own, lf_got, w2, spread, three)
     choose(x_half() == 0, one[...], three[...], keep, send)
 
 
-def even_kernel(right, zero, two, lf_own, lf_got, w2, keep, send, spread, last):
+def even_kernel(right, other, zero, two, lf_own, lf_got, w2, keep, send, spread, last):
     @pl.when(core() == 1)
     def _():
-        pair_block(right, lf_own, lf_got, w2, spread, last)
+        pair_block(right, other, lf_own, lf_got, w2, spread, last)
 
     @pl.when(core() == 0)
     def _():
@@ -293,12 +283,12 @@
         flops=20 << 20, limit=8,
     )
 
-    got = lax.ppermute(own, "col", core_swap)
-    right = [call(join_kernel, shape((2 * T * C + 16, S), BF16), own, got, limit=4)]
-
+    chains = [own, lax.ppermute(own, "col", core_swap)]
+    right = [chains]
     for step in range(4):
         pairs = [(z * 4 + c, (z + 1 - 2 * (c % 2)) % 8 * 4 + c) for z in range(8) for c in range(4) if step < 3 or c % 2]
-        right.append(lax.ppermute(right[-1], ("row", "col"), pairs))
+        chains = [lax.ppermute(chains[i], ("row", "col"), pairs) for i in range(2)]
+        right.append(chains)
 
     normed = [
         call(
@@ -318,12 +308,12 @@
     shared = (lf, lf_got, w2)
     spread = [pltpu.VMEM((T // 2, 512, 256), BF16)]
     more = spread + [pltpu.VMEM((ROWS + EXTRA, Z), F32)]
-    p0 = call(first_kernel, block, right[0], *shared, scratch=spread, flops=one)
-    p1 = call(next_kernel, block, right[1], *shared, scratch=spread, flops=one)
-    p2 = call(next_kernel, block, right[2], *shared, scratch=spread, flops=one)
-    odd, odd_sent = call(odd_kernel, (block,) * 2, right[3], p1, *shared, scratch=more, flops=one)
+    p0 = call(first_kernel, block, *right[0], *shared, scratch=spread, flops=one)
+    p1 = call(next_kernel, block, *right[1], *shared, scratch=spread, flops=one)
+    p2 = call(next_kernel, block, *right[2], *shared, scratch=spread, flops=one)
+    odd, odd_sent = call(odd_kernel, (block,) * 2, *right[3], p1, *shared, scratch=more, flops=one)
     f1 = lax.ppermute(odd_sent, "col", xh_swap)
-    even, even_sent = call(even_kernel, (block,) * 2, right[4], p0, p2, *shared, scratch=more, flops=one)
+    even, even_sent = call(even_kernel, (block,) * 2, *right[4], p0, p2, *shared, scratch=more, flops=one)
     f2 = lax.ppermute(even_sent, "col", xh_swap)
     part = shape((ROWS, Z), BF16)
     out_bias = out_bias.reshape(1, Z)

time: 93 us -> 86.4 us (0.929)
  the two profiles are of different devices: /device:TPU:4 before, /device:TPU:1 now
where the time goes in v5:
time: 86.4 us; the launch traced here: 86.1 us
  starting transfers between devices  42.6 us (49%)
  waiting for transfers between devices  23.2 us (27%)
  Pallas kernels  17.2 us (20%)
  local copies, waits for them, and re-layouts  2.77 us (3%)
    ppermute x8, starting transfers between devices, program(): chains = [lax.ppermute(chains[i], ('row', 'col'), pairs) for i in range(2)]  28.1 us
    pallas_call x15, Pallas kernels, call(): pl.pallas_call(kernel, out_shape=out, in_specs=specs or [VMEM] * len(args...  17.2 us
    ppermute x1, waiting for transfers between devices, program(): g1 = lax.ppermute(y1, ('row', 'col'), home((-1, 1, -3, 3)))  9.25 us
    ppermute x1, waiting for transfers between devices, program(): f1 = lax.ppermute(odd_sent, 'col', xh_swap)  5.52 us
    ppermute x8, waiting for transfers between devices, program(): chains = [lax.ppermute(chains[i], ('row', 'col'), pairs) for i in range(2)]  4.46 us
    ppermute x1, starting transfers between devices, program(): lf_got = lax.ppermute(lf, 'col', core_swap)  2.85 us
    ppermute x1, waiting for transfers between devices, program(): over = lax.ppermute(pack, 'chan', y_ring[2])  2.84 us
    unnamed x18, local copies, waits for them, and re-layouts  2.77 us
  transfers between devices with their start and end apart: 18, of which 8 were waited for; matrix products, arithmetic and copies ran while one was open for 0% of the time, Pallas kernels for 15%

profile of v5, /device:TPU:1, one launch (start us, length us, event | category | flops | bytes accessed | tf_op | source)
XLA Modules:
  0.0 86.1 jit_solution(7338450906456633344)
XLA Ops:
  0.0 0.0 copy-start
  0.0 0.8 copy-done
  0.8 0.0 copy-start.8
  0.8 0.7 copy-done.8
  1.4 2.1 %collective-permute-start.7 = (bf16[144,128]{1,0:T(8,128)(2,1)S(1)}, bf16[144,128]{1,0:T(8,128)(2,1)S(1)}, u32[]{:S(2)}, u32[]{:S(2)}) collective-permute-start(bf16[144,128]{1,0:T(8,128)(2,1)S(1)} %shard_map.94.a), channel_id=1, source_target_pairs={{0,1},{1,2},{2,3},{3,0},{4,5},{5,6},{6,7},{7,4},{8,9},{9,10},{10,1... | collective-permute-start | bytes 110600 | tf_op jit(solution)/shard_map/ppermute | solution.py:271
  3.6 1.5 %collective-permute-start.8 = (bf16[144,128]{1,0:T(8,128)(2,1)S(1)}, bf16[144,128]{1,0:T(8,128)(2,1)S(1)}, u32[]{:S(2)}, u32[]{:S(2)}) collective-permute-start(bf16[144,128]{1,0:T(8,128)(2,1)S(1)} %shard_map.94.a), channel_id=1, source_target_pairs={{0,3},{1,0},{2,1},{3,2},{4,7},{5,4},{6,5},{7,6},{8,11},{9,8},{10,9... | collective-permute-start | bytes 110600 | tf_op jit(solution)/shard_map/ppermute | solution.py:272
  5.1 1.6 %collective-permute-start.9 = (bf16[144,128]{1,0:T(8,128)(2,1)S(1)}, bf16[144,128]{1,0:T(8,128)(2,1)S(1)}, u32[]{:S(2)}, u32[]{:S(2)}) collective-permute-start(bf16[144,128]{1,0:T(8,128)(2,1)S(1)} %shard_map.94.a), channel_id=1, source_target_pairs={{0,2},{1,3},{2,0},{3,1},{4,6},{5,7},{6,4},{7,5},{8,10},{9,11},{10,... | collective-permute-start | bytes 110600 | tf_op jit(solution)/shard_map/ppermute | solution.py:273
  6.6 0.0 collective-permute-done.7.b
  6.6 0.0 collective-permute-done.8.c
  6.6 2.8 %collective-permute-done.9.d = bf16[144,128]{1,0:T(8,128)(2,1)S(1)} collective-permute-done((bf16[144,128]{1,0:T(8,128)(2,1)S(1)}, bf16[144,128]{1,0:T(8,128)(2,1)S(1)}, u32[]{:S(2)}, u32[]{:S(2)}) %collective-permute-start.9) | collective-permute-done | bytes 36896 | tf_op jit(solution)/shard_map/ppermute | solution.py:273
  9.5 1.2 %collective-permute-start.10 = (bf16[4,144,128]{2,1,0:T(8,128)(2,1)S(1)}, bf16[4,144,128]{2,1,0:T(8,128)(2,1)S(1)}, u32[]{:S(2)}, u32[]{:S(2)}) collective-permute-start(bf16[4,144,128]{2,1,0:T(8,128)(2,1)S(1)} %shard_map.95.near), channel_id=1, source_target_pairs={{0,4},{1,5},{2,6},{3,7},{4,0},{5,1},{6,2},{7,3},{8,12},{9,13},{10,... | collective-permute-start | bytes 442376 | tf_op jit(solution)/shard_map/ppermute | solution.py:275
  10.7 0.0 copy-start.4
  10.7 0.7 copy-done.4
  11.4 0.7 copy-done.5
  12.0 0.0 copy-start.6
  12.0 2.7 %shard_map.92.n_a = bf16[2048,512]{1,0:T(8,128)(2,1)S(1)} custom-call(bf16[64,64,512]{2,1,0:T(8,128)(2,1)} %bitcast.30, f32[1,64]{1,0:T(1,128)S(1)} %bitcast.22, f32[1,64]{1,0:T(1,128)S(1)} %bitcast.25), custom_call_target="tpu_custom_call" | custom-call | flops 15728640 | bytes 6291968 | tf_op jit(solution)/shard_map/pallas_call | solution.py:240
  14.7 0.0 copy-done.6
  14.7 0.0 copy-start.1
  14.7 0.0 copy-start.2
  14.7 2.7 %shard_map.93.n_b = bf16[2048,512]{1,0:T(8,128)(2,1)S(1)} custom-call(bf16[64,64,512]{2,1,0:T(8,128)(2,1)} %bitcast.31, f32[1,64]{1,0:T(1,128)S(1)} %bitcast.23, f32[1,64]{1,0:T(1,128)S(1)} %bitcast.26), custom_call_target="tpu_custom_call" | custom-call | flops 15728640 | bytes 6291968 | tf_op jit(solution)/shard_map/pallas_call | solution.py:240
  17.4 0.0 collective-permute-done.10.far
  17.4 0.3 shard_map.96
  17.7 0.0 copy-done.1
  17.7 0.0 copy-done.2
  17.7 1.5 %shard_map.97 = bf16[32,64,512]{2,1,0:T(8,128)(2,1)S(1)} custom-call(bf16[2048,512]{1,0:T(8,128)(2,1)S(1)} %shard_map.92.n_a, bf16[2048,512]{1,0:T(8,128)(2,1)S(1)} %shard_map.93.n_b, bf16[32,64]{1,0:T(8,128)(2,1)S(1)} %get-tuple-element.11.wl_ref, s32[1,512]{1,0:T(1,128)S(1)} %bitcast.16, s32[1,64]{1,0:T(1,128)S(1)} %bitcast.18), custom_call_target="tpu_custom_call" | custom-call | flops 1073741824 | bytes 6297856 | tf_op jit(solution)/shard_map/pallas_call | solution.py:240
  19.2 2.8 %collective-permute-start.11 = (bf16[2048,512]{1,0:T(8,128)(2,1)S(1)}, bf16[2048,512]{1,0:T(8,128)(2,1)S(1)}, u32[]{:S(2)}, u32[]{:S(2)}) collective-permute-start(bf16[2048,512]{1,0:T(8,128)(2,1)S(1)} %bitcast.9), channel_id=1, source_target_pairs={{0,8},{8,0},{16,24},{24,16},{1,9},{9,1},{17,25},{25,17},{2,10},{10... | collective-permute-start | bytes 6291464 | tf_op jit(solution)/shard_map/ppermute | solution.py:304
  22.0 1.6 %shard_map.91.right = bf16[272,512]{1,0:T(8,128)(2,1)S(1)} custom-call(bf16[64,64,512]{2,1,0:T(8,128)(2,1)} %bitcast.32, s32[1,512]{1,0:T(1,128)} %bitcast.15, s32[1,64]{1,0:T(1,128)} %bitcast.17, f32[1,64]{1,0:T(1,128)} %bitcast.21, f32[1,64]{1,0:T(1,128)} %bitcast.24, bf16[32,64]{1,0:T(8,128)(2,1)} %bitcast.33), custom_call_target="tpu_custom_call" | custom-call | flops 20971520 | bytes 4479744 | tf_op jit(solution)/shard_map/pallas_call | solution.py:240
  23.7 0.1 collective-permute-start.3
  23.8 5.4 %collective-permute-start = (bf16[272,512]{1,0:T(8,128)(2,1)S(1)}, bf16[272,512]{1,0:T(8,128)(2,1)S(1)}, u32[]{:S(2)}, u32[]{:S(2)}) collective-permute-start(bf16[272,512]{1,0:T(8,128)(2,1)S(1)} %shard_map.91.right), channel_id=1, source_target_pairs={{0,32},{8,232},{16,48},{24,248},{32,64},{40,8},{48,80},{56,24},{64... | collective-permute-start | bytes 835592 | tf_op jit(solution)/shard_map/ppermute | solution.py:290
  29.2 0.0 collective-permute-done.3.other
  29.2 2.4 %collective-permute-start.4 = (bf16[272,512]{1,0:T(8,128)(2,1)S(1)}, bf16[272,512]{1,0:T(8,128)(2,1)S(1)}, u32[]{:S(2)}, u32[]{:S(2)}) collective-permute-start(bf16[272,512]{1,0:T(8,128)(2,1)S(1)} %collective-permute-done.3.other), channel_id=1, source_target_pairs={{0,32},{8,232},{16,48},{24,248},{32,64},{40,8},{48,80},{56,24},{64... | collective-permute-start | bytes 835592 | tf_op jit(solution)/shard_map/ppermute | solution.py:290
  31.6 1.1 %collective-permute-done.right = bf16[272,512]{1,0:T(8,128)(2,1)S(1)} collective-permute-done((bf16[272,512]{1,0:T(8,128)(2,1)S(1)}, bf16[272,512]{1,0:T(8,128)(2,1)S(1)}, u32[]{:S(2)}, u32[]{:S(2)}) %collective-permute-start) | collective-permute-done | bytes 278560 | tf_op jit(solution)/shard_map/ppermute | solution.py:290
  32.7 3.1 %collective-permute-start.1 = (bf16[272,512]{1,0:T(8,128)(2,1)S(1)}, bf16[272,512]{1,0:T(8,128)(2,1)S(1)}, u32[]{:S(2)}, u32[]{:S(2)}) collective-permute-start(bf16[272,512]{1,0:T(8,128)(2,1)S(1)} %collective-permute-done.right), channel_id=1, source_target_pairs={{0,32},{8,232},{16,48},{24,248},{32,64},{40,8},{48,80},{56,24},{64... | collective-permute-start | bytes 835592 | tf_op jit(solution)/shard_map/ppermute | solution.py:290
  35.8 0.0 collective-permute-done.4.other
  35.8 3.0 %collective-permute-start.5 = (bf16[272,512]{1,0:T(8,128)(2,1)S(1)}, bf16[272,512]{1,0:T(8,128)(2,1)S(1)}, u32[]{:S(2)}, u32[]{:S(2)}) collective-permute-start(bf16[272,512]{1,0:T(8,128)(2,1)S(1)} %collective-permute-done.4.other), channel_id=1, source_target_pairs={{0,32},{8,232},{16,48},{24,248},{32,64},{40,8},{48,80},{56,24},{64... | collective-permute-start | bytes 835592 | tf_op jit(solution)/shard_map/ppermute | solution.py:290
  38.8 0.5 collective-permute-done.1.right
  39.3 3.1 %collective-permute-start.2 = (bf16[272,512]{1,0:T(8,128)(2,1)S(1)}, bf16[272,512]{1,0:T(8,128)(2,1)S(1)}, u32[]{:S(2)}, u32[]{:S(2)}) collective-permute-start(bf16[272,512]{1,0:T(8,128)(2,1)S(1)} %collective-permute-done.1.right), channel_id=1, source_target_pairs={{0,32},{8,232},{16,48},{24,248},{32,64},{40,8},{48,80},{56,24},{64... | collective-permute-start | bytes 835592 | tf_op jit(solution)/shard_map/ppermute | solution.py:290
  42.4 0.0 collective-permute-done.5.other
  42.4 3.0 %collective-permute-start.6 = (bf16[272,512]{1,0:T(8,128)(2,1)S(1)}, bf16[272,512]{1,0:T(8,128)(2,1)S(1)}, u32[]{:S(2)}, u32[]{:S(2)}) collective-permute-start(bf16[272,512]{1,0:T(8,128)(2,1)S(1)} %collective-permute-done.5.other), channel_id=1, source_target_pairs={{0,32},{8,232},{16,48},{24,248},{32,64},{40,8},{48,80},{56,24},{64... | collective-permute-start | bytes 835592 | tf_op jit(solution)/shard_map/ppermute | solution.py:290
  45.4 0.5 collective-permute-done.2.right
  45.9 5.0 %collective-permute-start.14 = (bf16[272,512]{1,0:T(8,128)(2,1)S(1)}, bf16[272,512]{1,0:T(8,128)(2,1)S(1)}, u32[]{:S(2)}, u32[]{:S(2)}) collective-permute-start(bf16[272,512]{1,0:T(8,128)(2,1)S(1)} %collective-permute-done.2.right), channel_id=1, source_target_pairs={{8,232},{24,248},{40,8},{56,24},{72,40},{88,56},{104,72},{120,88},... | collective-permute-start | bytes 835592 | tf_op jit(solution)/shard_map/ppermute | solution.py:290
  50.9 0.0 collective-permute-done.6.other
  50.9 3.1 %collective-permute-start.15 = (bf16[272,512]{1,0:T(8,128)(2,1)S(1)}, bf16[272,512]{1,0:T(8,128)(2,1)S(1)}, u32[]{:S(2)}, u32[]{:S(2)}) collective-permute-start(bf16[272,512]{1,0:T(8,128)(2,1)S(1)} %collective-permute-done.6.other), channel_id=1, source_target_pairs={{8,232},{24,248},{40,8},{56,24},{72,40},{88,56},{104,72},{120,88},... | collective-permute-start | bytes 835592 | tf_op jit(solution)/shard_map/ppermute | solution.py:290
  54.1 0.0 collective-permute-done.11.lf_got
  54.1 1.8 %shard_map.102.two = f32[520,128]{1,0:T(8,128)S(1)} custom-call(bf16[272,512]{1,0:T(8,128)(2,1)S(1)} %collective-permute-done.1.right, bf16[272,512]{1,0:T(8,128)(2,1)S(1)} %collective-permute-done.5.other, bf16[2048,512]{1,0:T(8,128)(2,1)S(1)} %bitcast.10, bf16[2048,512]{1,0:T(8,128)(2,1)S(1)} %collective-permute-done.11.lf_got, ...), custom_call_target="tpu_custom_call" | custom-call | flops 1468006400 | bytes 5279744 | tf_op jit(solution)/shard_map/pallas_call | solution.py:240
  55.9 0.0 collective-permute-done.14.right
  55.9 2.3 %collective-permute-done.15.other = bf16[272,512]{1,0:T(8,128)(2,1)S(1)} collective-permute-done((bf16[272,512]{1,0:T(8,128)(2,1)S(1)}, bf16[272,512]{1,0:T(8,128)(2,1)S(1)}, u32[]{:S(2)}, u32[]{:S(2)}) %collective-permute-start.15) | collective-permute-done | bytes 278560 | tf_op jit(solution)/shard_map/ppermute | solution.py:290
  58.2 1.8 %shard_map.103 = (f32[520,128]{1,0:T(8,128)S(1)}, f32[520,128]{1,0:T(8,128)S(1)}) custom-call(bf16[272,512]{1,0:T(8,128)(2,1)S(1)} %collective-permute-done.14.right, bf16[272,512]{1,0:T(8,128)(2,1)S(1)} %collective-permute-done.15.other, f32[520,128]{1,0:T(8,128)S(1)} %shard_map.101.zero, f32[520,128]{1,0:T(8,128)S(1)} %shard_map.102.two, ...), custom_call_target="tpu_custom_call" | custom-call | flops 1468006400 | bytes 6078464 | tf_op jit(solution)/shard_map/pallas_call | solution.py:240
  60.0 2.5 %collective-permute-start.16 = (f32[520,128]{1,0:T(8,128)S(1)}, f32[520,128]{1,0:T(8,128)S(1)}, u32[]{:S(2)}, u32[]{:S(2)}) collective-permute-start(f32[520,128]{1,0:T(8,128)S(1)} %get-tuple-element.16), channel_id=1, source_target_pairs={{0,16},{8,24},{16,0},{24,8},{1,17},{9,25},{17,1},{25,9},{2,18},{10... | collective-permute-start | bytes 798728 | tf_op jit(solution)/shard_map/ppermute | solution.py:317
  62.6 1.8 %shard_map.98.one = f32[520,128]{1,0:T(8,128)S(1)} custom-call(bf16[272,512]{1,0:T(8,128)(2,1)S(1)} %collective-permute-done.right, bf16[272,512]{1,0:T(8,128)(2,1)S(1)} %collective-permute-done.4.other, bf16[2048,512]{1,0:T(8,128)(2,1)S(1)} %bitcast.13, bf16[2048,512]{1,0:T(8,128)(2,1)S(1)} %collective-permute-done.11.lf_got, ...), custom_call_target="tpu_custom_call" | custom-call | flops 1468006400 | bytes 5279744 | tf_op jit(solution)/shard_map/pallas_call | solution.py:240
  64.4 0.0 copy-start.7
  64.4 1.8 %shard_map.99 = (f32[520,128]{1,0:T(8,128)S(1)}, f32[520,128]{1,0:T(8,128)S(1)}) custom-call(bf16[272,512]{1,0:T(8,128)(2,1)S(1)} %collective-permute-done.2.right, bf16[272,512]{1,0:T(8,128)(2,1)S(1)} %collective-permute-done.6.other, f32[520,128]{1,0:T(8,128)S(1)} %shard_map.98.one, bf16[2048,512]{1,0:T(8,128)(2,1)S(1)} %bitcast.14, ...), custom_call_target="tpu_custom_call" | custom-call | flops 1468006400 | bytes 5812224 | tf_op jit(solution)/shard_map/pallas_call | solution.py:240
  66.2 0.6 collective-permute-start.12
  66.8 1.1 %collective-permute-done.16.got = f32[520,128]{1,0:T(8,128)S(1)} collective-permute-done((f32[520,128]{1,0:T(8,128)S(1)}, f32[520,128]{1,0:T(8,128)S(1)}, u32[]{:S(2)}, u32[]{:S(2)}) %collective-permute-start.16) | collective-permute-done | bytes 266272 | tf_op jit(solution)/shard_map/ppermute | solution.py:317
  67.9 0.0 copy-done.3
  67.9 0.0 copy-done.7
  67.9 0.2 shard_map.104
  68.2 1.9 %collective-permute-start.17 = (bf16[512,128]{1,0:T(8,128)(2,1)S(1)}, bf16[512,128]{1,0:T(8,128)(2,1)S(1)}, u32[]{:S(2)}, u32[]{:S(2)}) collective-permute-start(bf16[512,128]{1,0:T(8,128)(2,1)S(1)} %shard_map.104), channel_id=1, source_target_pairs={{0,192},{8,64},{16,0},{24,128},{32,224},{40,96},{48,32},{56,160},{... | collective-permute-start | bytes 393224 | tf_op jit(solution)/shard_map/ppermute | solution.py:327
  70.1 5.5 %collective-permute-done.12.got = f32[520,128]{1,0:T(8,128)S(1)} collective-permute-done((f32[520,128]{1,0:T(8,128)S(1)}, f32[520,128]{1,0:T(8,128)S(1)}, u32[]{:S(2)}, u32[]{:S(2)}) %collective-permute-start.12) | collective-permute-done | bytes 266272 | tf_op jit(solution)/shard_map/ppermute | solution.py:315
  75.6 0.2 shard_map.100
  75.9 0.1 collective-permute-start.13
  76.0 0.0 collective-permute-done.17.even
  76.0 9.2 %collective-permute-done.13.odd = bf16[512,128]{1,0:T(8,128)(2,1)S(1)} collective-permute-done((bf16[512,128]{1,0:T(8,128)(2,1)S(1)}, bf16[512,128]{1,0:T(8,128)(2,1)S(1)}, u32[]{:S(2)}, u32[]{:S(2)}) %collective-permute-start.13) | collective-permute-done | bytes 131104 | tf_op jit(solution)/shard_map/ppermute | solution.py:326
  85.2 0.8 shard_map.105
  (5 shorter events, 0.0 us)
Async XLA Ops:
  0.0 0.8 copy-start
  0.8 0.7 copy-start.8
  1.4 5.2 %collective-permute-start.7 = (bf16[144,128]{1,0:T(8,128)(2,1)S(1)}, bf16[144,128]{1,0:T(8,128)(2,1)S(1)}, u32[]{:S(2)}, u32[]{:S(2)}) collective-permute-start(bf16[144,128]{1,0:T(8,128)(2,1)S(1)} %shard_map.94.a), channel_id=1, source_target_pairs={{0,1},{1,2},{2,3},{3,0},{4,5},{5,6},{6,7},{7,4},{8,9},{9,10},{10,1... | collective-permute-start | bytes 110600 | tf_op jit(solution)/shard_map/ppermute | solution.py:271
  3.6 3.1 %collective-permute-start.8 = (bf16[144,128]{1,0:T(8,128)(2,1)S(1)}, bf16[144,128]{1,0:T(8,128)(2,1)S(1)}, u32[]{:S(2)}, u32[]{:S(2)}) collective-permute-start(bf16[144,128]{1,0:T(8,128)(2,1)S(1)} %shard_map.94.a), channel_id=1, source_target_pairs={{0,3},{1,0},{2,1},{3,2},{4,7},{5,4},{6,5},{7,6},{8,11},{9,8},{10,9... | collective-permute-start | bytes 110600 | tf_op jit(solution)/shard_map/ppermute | solution.py:272
  5.1 4.4 %collective-permute-start.9 = (bf16[144,128]{1,0:T(8,128)(2,1)S(1)}, bf16[144,128]{1,0:T(8,128)(2,1)S(1)}, u32[]{:S(2)}, u32[]{:S(2)}) collective-permute-start(bf16[144,128]{1,0:T(8,128)(2,1)S(1)} %shard_map.94.a), channel_id=1, source_target_pairs={{0,2},{1,3},{2,0},{3,1},{4,6},{5,7},{6,4},{7,5},{8,10},{9,11},{10,... | collective-permute-start | bytes 110600 | tf_op jit(solution)/shard_map/ppermute | solution.py:273
  9.5 7.9 %collective-permute-start.10 = (bf16[4,144,128]{2,1,0:T(8,128)(2,1)S(1)}, bf16[4,144,128]{2,1,0:T(8,128)(2,1)S(1)}, u32[]{:S(2)}, u32[]{:S(2)}) collective-permute-start(bf16[4,144,128]{2,1,0:T(8,128)(2,1)S(1)} %shard_map.95.near), channel_id=1, source_target_pairs={{0,4},{1,5},{2,6},{3,7},{4,0},{5,1},{6,2},{7,3},{8,12},{9,13},{10,... | collective-permute-start | bytes 442376 | tf_op jit(solution)/shard_map/ppermute | solution.py:275
  10.7 0.7 copy-start.4
  11.4 0.7 copy-start.5
  12.0 2.7 %copy-start.6 = (f32[64]{0:T(128)S(1)}, f32[64]{0:T(128)}, u32[]{:S(2)}) copy-start(f32[64]{0:T(128)} %param.13) | copy-start | bytes 772
  14.7 3.0 %copy-start.1 = (s32[512]{0:T(512)S(1)}, s32[512]{0:T(512)}, u32[]{:S(2)}) copy-start(s32[512]{0:T(512)} %param.10) | copy-start | bytes 6148
  14.7 3.0 %copy-start.2 = (s32[64]{0:T(128)S(1)}, s32[64]{0:T(128)}, u32[]{:S(2)}) copy-start(s32[64]{0:T(128)} %param.11) | copy-start | bytes 772
  19.2 34.9 %collective-permute-start.11 = (bf16[2048,512]{1,0:T(8,128)(2,1)S(1)}, bf16[2048,512]{1,0:T(8,128)(2,1)S(1)}, u32[]{:S(2)}, u32[]{:S(2)}) collective-permute-start(bf16[2048,512]{1,0:T(8,128)(2,1)S(1)} %bitcast.9), channel_id=1, source_target_pairs={{0,8},{8,0},{16,24},{24,16},{1,9},{9,1},{17,25},{25,17},{2,10},{10... | collective-permute-start | bytes 6291464 | tf_op jit(solution)/shard_map/ppermute | solution.py:304
  23.7 5.5 %collective-permute-start.3 = (bf16[272,512]{1,0:T(8,128)(2,1)S(1)}, bf16[272,512]{1,0:T(8,128)(2,1)S(1)}, u32[]{:S(2)}, u32[]{:S(2)}) collective-permute-start(bf16[272,512]{1,0:T(8,128)(2,1)S(1)} %shard_map.91.right), channel_id=1, source_target_pairs={{0,8},{8,0},{16,24},{24,16},{1,9},{9,1},{17,25},{25,17},{2,10},{10... | collective-permute-start | bytes 835592 | tf_op jit(solution)/shard_map/ppermute | solution.py:286
  23.8 8.9 %collective-permute-start = (bf16[272,512]{1,0:T(8,128)(2,1)S(1)}, bf16[272,512]{1,0:T(8,128)(2,1)S(1)}, u32[]{:S(2)}, u32[]{:S(2)}) collective-permute-start(bf16[272,512]{1,0:T(8,128)(2,1)S(1)} %shard_map.91.right), channel_id=1, source_target_pairs={{0,32},{8,232},{16,48},{24,248},{32,64},{40,8},{48,80},{56,24},{64... | collective-permute-start | bytes 835592 | tf_op jit(solution)/shard_map/ppermute | solution.py:290
  29.2 6.6 %collective-permute-start.4 = (bf16[272,512]{1,0:T(8,128)(2,1)S(1)}, bf16[272,512]{1,0:T(8,128)(2,1)S(1)}, u32[]{:S(2)}, u32[]{:S(2)}) collective-permute-start(bf16[272,512]{1,0:T(8,128)(2,1)S(1)} %collective-permute-done.3.other), channel_id=1, source_target_pairs={{0,32},{8,232},{16,48},{24,248},{32,64},{40,8},{48,80},{56,24},{64... | collective-permute-start | bytes 835592 | tf_op jit(solution)/shard_map/ppermute | solution.py:290
  32.7 6.6 %collective-permute-start.1 = (bf16[272,512]{1,0:T(8,128)(2,1)S(1)}, bf16[272,512]{1,0:T(8,128)(2,1)S(1)}, u32[]{:S(2)}, u32[]{:S(2)}) collective-permute-start(bf16[272,512]{1,0:T(8,128)(2,1)S(1)} %collective-permute-done.right), channel_id=1, source_target_pairs={{0,32},{8,232},{16,48},{24,248},{32,64},{40,8},{48,80},{56,24},{64... | collective-permute-start | bytes 835592 | tf_op jit(solution)/shard_map/ppermute | solution.py:290
  35.8 6.6 %collective-permute-start.5 = (bf16[272,512]{1,0:T(8,128)(2,1)S(1)}, bf16[272,512]{1,0:T(8,128)(2,1)S(1)}, u32[]{:S(2)}, u32[]{:S(2)}) collective-permute-start(bf16[272,512]{1,0:T(8,128)(2,1)S(1)} %collective-permute-done.4.other), channel_id=1, source_target_pairs={{0,32},{8,232},{16,48},{24,248},{32,64},{40,8},{48,80},{56,24},{64... | collective-permute-start | bytes 835592 | tf_op jit(solution)/shard_map/ppermute | solution.py:290
  39.3 6.6 %collective-permute-start.2 = (bf16[272,512]{1,0:T(8,128)(2,1)S(1)}, bf16[272,512]{1,0:T(8,128)(2,1)S(1)}, u32[]{:S(2)}, u32[]{:S(2)}) collective-permute-start(bf16[272,512]{1,0:T(8,128)(2,1)S(1)} %collective-permute-done.1.right), channel_id=1, source_target_pairs={{0,32},{8,232},{16,48},{24,248},{32,64},{40,8},{48,80},{56,24},{64... | collective-permute-start | bytes 835592 | tf_op jit(solution)/shard_map/ppermute | solution.py:290
  42.4 8.5 %collective-permute-start.6 = (bf16[272,512]{1,0:T(8,128)(2,1)S(1)}, bf16[272,512]{1,0:T(8,128)(2,1)S(1)}, u32[]{:S(2)}, u32[]{:S(2)}) collective-permute-start(bf16[272,512]{1,0:T(8,128)(2,1)S(1)} %collective-permute-done.5.other), channel_id=1, source_target_pairs={{0,32},{8,232},{16,48},{24,248},{32,64},{40,8},{48,80},{56,24},{64... | collective-permute-start | bytes 835592 | tf_op jit(solution)/shard_map/ppermute | solution.py:290
  45.9 10.0 %collective-permute-start.14 = (bf16[272,512]{1,0:T(8,128)(2,1)S(1)}, bf16[272,512]{1,0:T(8,128)(2,1)S(1)}, u32[]{:S(2)}, u32[]{:S(2)}) collective-permute-start(bf16[272,512]{1,0:T(8,128)(2,1)S(1)} %collective-permute-done.2.right), channel_id=1, source_target_pairs={{8,232},{24,248},{40,8},{56,24},{72,40},{88,56},{104,72},{120,88},... | collective-permute-start | bytes 835592 | tf_op jit(solution)/shard_map/ppermute | solution.py:290
  50.9 7.3 %collective-permute-start.15 = (bf16[272,512]{1,0:T(8,128)(2,1)S(1)}, bf16[272,512]{1,0:T(8,128)(2,1)S(1)}, u32[]{:S(2)}, u32[]{:S(2)}) collective-permute-start(bf16[272,512]{1,0:T(8,128)(2,1)S(1)} %collective-permute-done.6.other), channel_id=1, source_target_pairs={{8,232},{24,248},{40,8},{56,24},{72,40},{88,56},{104,72},{120,88},... | collective-permute-start | bytes 835592 | tf_op jit(solution)/shard_map/ppermute | solution.py:290
  60.0 7.9 %collective-permute-start.16 = (f32[520,128]{1,0:T(8,128)S(1)}, f32[520,128]{1,0:T(8,128)S(1)}, u32[]{:S(2)}, u32[]{:S(2)}) collective-permute-start(f32[520,128]{1,0:T(8,128)S(1)} %get-tuple-element.16), channel_id=1, source_target_pairs={{0,16},{8,24},{16,0},{24,8},{1,17},{9,25},{17,1},{25,9},{2,18},{10... | collective-permute-start | bytes 798728 | tf_op jit(solution)/shard_map/ppermute | solution.py:317
  64.3 3.6 %copy-start.3 = (s32[64]{0:T(128)S(1)}, s32[64]{0:T(128)}, u32[]{:S(2)}) copy-start(s32[64]{0:T(128)} %param.11) | copy-start | bytes 772
  64.4 3.6 %copy-start.7 = (f32[128]{0:T(128)S(1)}, f32[128]{0:T(128)}, u32[]{:S(2)}) copy-start(f32[128]{0:T(128)} %param.17) | copy-start | bytes 1540
  66.2 9.5 %collective-permute-start.12 = (f32[520,128]{1,0:T(8,128)S(1)}, f32[520,128]{1,0:T(8,128)S(1)}, u32[]{:S(2)}, u32[]{:S(2)}) collective-permute-start(f32[520,128]{1,0:T(8,128)S(1)} %get-tuple-element.14), channel_id=1, source_target_pairs={{0,16},{8,24},{16,0},{24,8},{1,17},{9,25},{17,1},{25,9},{2,18},{10... | collective-permute-start | bytes 798728 | tf_op jit(solution)/shard_map/ppermute | solution.py:315
  68.2 7.8 %collective-permute-start.17 = (bf16[512,128]{1,0:T(8,128)(2,1)S(1)}, bf16[512,128]{1,0:T(8,128)(2,1)S(1)}, u32[]{:S(2)}, u32[]{:S(2)}) collective-permute-start(bf16[512,128]{1,0:T(8,128)(2,1)S(1)} %shard_map.104), channel_id=1, source_target_pairs={{0,192},{8,64},{16,0},{24,128},{32,224},{40,96},{48,32},{56,160},{... | collective-permute-start | bytes 393224 | tf_op jit(solution)/shard_map/ppermute | solution.py:327
  75.9 9.4 %collective-permute-start.13 = (bf16[512,128]{1,0:T(8,128)(2,1)S(1)}, bf16[512,128]{1,0:T(8,128)(2,1)S(1)}, u32[]{:S(2)}, u32[]{:S(2)}) collective-permute-start(bf16[512,128]{1,0:T(8,128)(2,1)S(1)} %shard_map.100), channel_id=1, source_target_pairs={{0,224},{8,32},{16,160},{24,96},{32,0},{40,64},{48,192},{56,128},{... | collective-permute-start | bytes 393224 | tf_op jit(solution)/shard_map/ppermute | solution.py:326

commit v6 on v5

--- a/solution.py
+++ b/solution.py
@@ -52,9 +52,10 @@
     out_ref[Z : Z + 4, 0:M] = wl_ref[...]
 
 
-def stack_kernel(a, b, c, d, out):
-    for i, ref in enumerate((a, b, c, d)):
-        out[i] = ref[...]
+def stack_kernel(a, b, out):
+    n = out.shape[0] // 2
+    out[:n] = a[...].reshape(out.shape[0] // 2, Z + 16, Z)
+    out[n:] = b[...].reshape(out.shape[0] // 2, Z + 16, Z)
 
 
 def weight_kernel(near, far, wl_out, w2_out):
@@ -169,22 +170,28 @@
         out[p * 128 : (p + 1) * 128, :] = pair.T
     extra = right[T * C :, :].astype(F32)
     rows = extra[T : T + 1] + other[T * C :, :].astype(F32)[T : T + 1]
-    rows_used = jnp.broadcast_to(jnp.sum(rows, axis=1, keepdims=True), (EXTRA, Z))
+    rows_used = jnp.sum(rows, axis=1, keepdims=True)
+    high = jnp.floor(rows_used * (1.0 / 64.0))
+    rows_used = jnp.where(
+        lax.broadcasted_iota(jnp.int32, (EXTRA, Z), 1) < N // 2,
+        jnp.broadcast_to(high, (EXTRA, Z)),
+        jnp.broadcast_to(rows_used - 64.0 * high, (EXTRA, Z)),
+    )
     lane = lax.broadcasted_iota(jnp.int32, (EXTRA, Z), 1)
     out[ROWS:, :] = jnp.where(lane < N, rows_used, jnp.broadcast_to(extra[:EXTRA, :1], (EXTRA, Z)))
 
 
 def choose(first, a, b, one, two):
-    one[...] = jnp.where(first, a, b)
-    two[...] = jnp.where(first, b, a)
+    one[...] = jnp.where(first, a, b).astype(one.dtype)
+    two[...] = jnp.where(first, b, a).astype(two.dtype)
 
 
 def core():
     return lax.rem(lax.axis_index("col"), 2)
 
 
-def x_half():
-    return lax.axis_index("col") // 2
+def at_home():
+    return lax.axis_index("col") // 2 == lax.axis_index("row") // 4
 
 
 def first_kernel(right, other, lf_own, lf_got, w2, out, spread):
@@ -199,7 +206,7 @@
 
 def odd_kernel(right, other, one, lf_own, lf_got, w2, keep, send, spread, three):
     pair_block(right, other, lf_own, lf_got, w2, spread, three)
-    choose(x_half() == 0, one[...], three[...], keep, send)
+    choose(at_home(), three[...], one[...], keep, send)
 
 
 def even_kernel(right, other, zero, two, lf_own, lf_got, w2, keep, send, spread, last):
@@ -211,13 +218,13 @@
     def _():
         last[...] = zero[...]
 
-    choose(x_half() == 0, two[...], last[...], keep, send)
+    choose(at_home(), last[...], two[...], keep, send)
 
 
 def final_kernel(keep, got, tok_ref, bias_ref, out):
-    total = keep[...] + got[...]
+    total = keep[...] + got[...].astype(F32)
     tail = total[ROWS:, :]
-    rows_used = tail[0:1, 0:1]
+    rows_used = 64.0 * tail[0:1, 0:1] + tail[0:1, N // 2 : N // 2 + 1]
     second = (tail[:, N : N + 1] > 0.0).astype(F32)
     first = column_of(tok_ref[...].astype(F32))
     count = jnp.maximum(rows_used[None] * first[None] * second[:, :, None], 1.0)
@@ -262,18 +269,16 @@
     tok = token_mask.reshape(1, N)
     gain, bias = gain.reshape(1, M), bias.reshape(1, M)
 
-    y_ring = {d: [(a * 4 + b, a * 4 + (b + d) % 4) for a in range(2) for b in range(4)] for d in (1, -1, 2)}
-    x_swap = [(c, (c + 4) % 8) for c in range(8)]
     core_swap = [(0, 1), (1, 0), (2, 3), (3, 2)]
     xh_swap = [(0, 2), (1, 3), (2, 0), (3, 1)]
 
     pack = call(pack_kernel, shape((Z + 16, Z), BF16), wl.T, wo)
-    up = lax.ppermute(pack, "chan", y_ring[1])
-    down = lax.ppermute(pack, "chan", y_ring[-1])
-    over = lax.ppermute(pack, "chan", y_ring[2])
-    four = call(stack_kernel, shape((4, Z + 16, Z), BF16), pack, up, down, over, limit=4)
-    other = lax.ppermute(four, "chan", x_swap)
-    wl_all, w2 = call(weight_kernel, (shape((C, M), BF16), shape((2 * Z, 512), BF16)), four, other, limit=4)
+    packs = pack
+    for step in range(3):
+        got = lax.ppermute(packs, "chan", [(c, c ^ (1 << step)) for c in range(8)])
+        if step < 2:
+            packs = call(stack_kernel, shape((2 << step, Z + 16, Z), BF16), packs, got, limit=4)
+    wl_all, w2 = call(weight_kernel, (shape((C, M), BF16), shape((2 * Z, 512), BF16)), packs, got, limit=4)
 
     small = [in_hbm(a) for a in (row, tok, gain, bias, wr.T)]
     own = call(
@@ -304,6 +309,7 @@
     lf_got = lax.ppermute(lf, "col", core_swap)
 
     block = shape((ROWS + EXTRA, Z), F32)
+    sent = shape((ROWS + EXTRA, Z), BF16)
     one = 1400 << 20
     shared = (lf, lf_got, w2)
     spread = [pltpu.VMEM((T // 2, 512, 256), BF16)]
@@ -311,20 +317,21 @@
     p0 = call(first_kernel, block, *right[0], *shared, scratch=spread, flops=one)
     p1 = call(next_kernel, block, *right[1], *shared, scratch=spread, flops=one)
     p2 = call(next_kernel, block, *right[2], *shared, scratch=spread, flops=one)
-    odd, odd_sent = call(odd_kernel, (block,) * 2, *right[3], p1, *shared, scratch=more, flops=one)
+    odd, odd_sent = call(odd_kernel, (block, sent), *right[3], p1, *shared, scratch=more, flops=one)
     f1 = lax.ppermute(odd_sent, "col", xh_swap)
-    even, even_sent = call(even_kernel, (block,) * 2, *right[4], p0, p2, *shared, scratch=more, flops=one)
+    even, even_sent = call(even_kernel, (block, sent), *right[4], p0, p2, *shared, scratch=more, flops=one)
     f2 = lax.ppermute(even_sent, "col", xh_swap)
     part = shape((ROWS, Z), BF16)
     out_bias = out_bias.reshape(1, Z)
     y1 = call(final_kernel, part, odd, f1, tok, out_bias)
     y2 = call(final_kernel, part, even, f2, tok, out_bias)
 
-    def home(kept):
-        return [(z * 4 + c, (z + kept[c]) % 8 * 4 + z // 2) for z in range(8) for c in range(4)]
-
-    g1 = lax.ppermute(y1, ("row", "col"), home((-1, 1, -3, 3)))
-    g2 = lax.ppermute(y2, ("row", "col"), home((-2, 2, 0, 4)))
+    def home(near, far):
+        kept = {(z, c): (far if c // 2 == z // 4 else near)[c % 2] for z in range(8) for c in range(4)}
+        return [(z * 4 + c, (z + kept[z, c]) % 8 * 4 + z // 2) for z in range(8) for c in range(4)]
+
+    g1 = lax.ppermute(y1, ("row", "col"), home((-1, 1), (-3, 3)))
+    g2 = lax.ppermute(y2, ("row", "col"), home((-2, 2), (0, 4)))
     return call(assemble_kernel, shape((2 * N, T, Z), BF16), g1, g2, scratch=[pltpu.VMEM((2, ROWS, Z), F32)], limit=4)
 
 

time: 86.4 us -> 81.5 us (0.943)
  waiting for transfers between devices: 23.2 us -> 15.2 us
  starting transfers between devices: 42.6 us -> 45.7 us
    ppermute x1, waiting for transfers between devices: 5.52 us -> 0.44 us  [program(): f1 = lax.ppermute(odd_sent, 'col', xh_swap)]
    ppermute x6 -> x5, starting transfers between devices: 8.41 us -> 10.7 us  [the longest x3 6.55 us: program(): got = lax.ppermute(packs, 'chan', [(c, c ^ 1 << step) for c in range(8)])]
    ppermute x6 -> x5, waiting for transfers between devices: 12.1 us -> 10.3 us  [the longest x1 7.22 us: program(): g2 = lax.ppermute(y2, ('row', 'col'), home((-2, 2), (0, 4)))]
    ppermute x1, waiting for transfers between devices: 1.15 us -> 0.01 us  [program(): f2 = lax.ppermute(even_sent, 'col', xh_swap)]
    pallas_call x15 -> x16, Pallas kernels: 17.2 us -> 17.3 us  [call(): pl.pallas_call(kernel, out_shape=out, in_specs=specs or [VMEM] * len(args...]
  transfers between devices with their start and end apart: 18 -> 17, of which waited for: 8 -> 8; matrix products, arithmetic and copies ran while one was open for 0% -> 0% of each run, Pallas kernels for 15% -> 16%
where the time goes in v6:
time: 81.5 us; the launch traced here: 81.2 us
  starting transfers between devices  45.7 us (56%)
  Pallas kernels  17.3 us (21%)
  waiting for transfers between devices  15.2 us (19%)
  local copies, waits for them, and re-layouts  2.77 us (3%)
    ppermute x8, starting transfers between devices, program(): chains = [lax.ppermute(chains[i], ('row', 'col'), pairs) for i in range(2)]  28.1 us
    pallas_call x16, Pallas kernels, call(): pl.pallas_call(kernel, out_shape=out, in_specs=specs or [VMEM] * len(args...  17.3 us
    ppermute x1, waiting for transfers between devices, program(): g2 = lax.ppermute(y2, ('row', 'col'), home((-2, 2), (0, 4)))  7.22 us
    ppermute x3, starting transfers between devices, program(): got = lax.ppermute(packs, 'chan', [(c, c ^ 1 << step) for c in range(8)])  6.55 us
    ppermute x8, waiting for transfers between devices, program(): chains = [lax.ppermute(chains[i], ('row', 'col'), pairs) for i in range(2)]  4.46 us
    ppermute x1, starting transfers between devices, program(): g2 = lax.ppermute(y2, ('row', 'col'), home((-2, 2), (0, 4)))  4.1 us
    ppermute x1, starting transfers between devices, program(): lf_got = lax.ppermute(lf, 'col', core_swap)  3.57 us
    ppermute x3, waiting for transfers between devices, program(): got = lax.ppermute(packs, 'chan', [(c, c ^ 1 << step) for c in range(8)])  3.09 us
  transfers between devices with their start and end apart: 17, of which 8 were waited for; matrix products, arithmetic and copies ran while one was open for 0% of the time, Pallas kernels for 16%

profile of v6, /device:TPU:1, one launch (start us, length us, event | category | flops | bytes accessed | tf_op | source)
XLA Modules:
  0.0 81.2 jit_solution(516603744307294587)
XLA Ops:
  0.0 0.0 copy-start
  0.0 0.8 copy-done
  0.8 0.0 copy-start.8
  0.8 0.7 copy-done.8
  1.4 2.1 %collective-permute-start.7 = (bf16[144,128]{1,0:T(8,128)(2,1)S(1)}, bf16[144,128]{1,0:T(8,128)(2,1)S(1)}, u32[]{:S(2)}, u32[]{:S(2)}) collective-permute-start(bf16[144,128]{1,0:T(8,128)(2,1)S(1)} %shard_map.94.a), channel_id=1, source_target_pairs={{0,1},{1,0},{2,3},{3,2},{4,5},{5,4},{6,7},{7,6},{8,9},{9,8},{10,11... | collective-permute-start | bytes 110600 | tf_op jit(solution)/shard_map/ppermute | solution.py:278
  3.6 1.3 %collective-permute-done.7.b = bf16[144,128]{1,0:T(8,128)(2,1)S(1)} collective-permute-done((bf16[144,128]{1,0:T(8,128)(2,1)S(1)}, bf16[144,128]{1,0:T(8,128)(2,1)S(1)}, u32[]{:S(2)}, u32[]{:S(2)}) %collective-permute-start.7) | collective-permute-done | bytes 36896 | tf_op jit(solution)/shard_map/ppermute | solution.py:278
  4.9 3.1 %collective-permute-start.8 = (bf16[2,144,128]{2,1,0:T(8,128)(2,1)S(1)}, bf16[2,144,128]{2,1,0:T(8,128)(2,1)S(1)}, u32[]{:S(2)}, u32[]{:S(2)}) collective-permute-start(bf16[2,144,128]{2,1,0:T(8,128)(2,1)S(1)} %shard_map.95.a), channel_id=1, source_target_pairs={{0,2},{1,3},{2,0},{3,1},{4,6},{5,7},{6,4},{7,5},{8,10},{9,11},{10,... | collective-permute-start | bytes 221192 | tf_op jit(solution)/shard_map/ppermute | solution.py:278
  8.0 1.7 %collective-permute-done.8.b = bf16[2,144,128]{2,1,0:T(8,128)(2,1)S(1)} collective-permute-done((bf16[2,144,128]{2,1,0:T(8,128)(2,1)S(1)}, bf16[2,144,128]{2,1,0:T(8,128)(2,1)S(1)}, u32[]{:S(2)}, u32[]{:S(2)}) %collective-permute-start.8) | collective-permute-done | bytes 73760 | tf_op jit(solution)/shard_map/ppermute | solution.py:278
  9.7 1.4 %collective-permute-start.9 = (bf16[4,144,128]{2,1,0:T(8,128)(2,1)S(1)}, bf16[4,144,128]{2,1,0:T(8,128)(2,1)S(1)}, u32[]{:S(2)}, u32[]{:S(2)}) collective-permute-start(bf16[4,144,128]{2,1,0:T(8,128)(2,1)S(1)} %shard_map.96.near), channel_id=1, source_target_pairs={{0,4},{1,5},{2,6},{3,7},{4,0},{5,1},{6,2},{7,3},{8,12},{9,13},{10,... | collective-permute-start | bytes 442376 | tf_op jit(solution)/shard_map/ppermute | solution.py:278
  11.1 0.0 copy-start.4
  11.1 0.7 copy-done.4
  11.8 0.0 copy-start.5
  11.8 0.7 copy-done.5
  12.4 0.0 copy-start.6
  12.4 2.7 %shard_map.92.n_a = bf16[2048,512]{1,0:T(8,128)(2,1)S(1)} custom-call(bf16[64,64,512]{2,1,0:T(8,128)(2,1)} %bitcast.30, f32[1,64]{1,0:T(1,128)S(1)} %bitcast.22, f32[1,64]{1,0:T(1,128)S(1)} %bitcast.25), custom_call_target="tpu_custom_call" | custom-call | flops 15728640 | bytes 6291968 | tf_op jit(solution)/shard_map/pallas_call | solution.py:247
  15.1 0.0 copy-done.6
  15.1 0.0 copy-start.1
  15.1 0.0 copy-start.2
  15.1 2.7 %shard_map.93.n_b = bf16[2048,512]{1,0:T(8,128)(2,1)S(1)} custom-call(bf16[64,64,512]{2,1,0:T(8,128)(2,1)} %bitcast.31, f32[1,64]{1,0:T(1,128)S(1)} %bitcast.23, f32[1,64]{1,0:T(1,128)S(1)} %bitcast.26), custom_call_target="tpu_custom_call" | custom-call | flops 15728640 | bytes 6291968 | tf_op jit(solution)/shard_map/pallas_call | solution.py:247
  17.8 0.0 collective-permute-done.9.far
  17.8 0.3 shard_map.97
  18.1 0.0 copy-done.1
  18.1 0.0 copy-done.2
  18.1 1.5 %shard_map.98 = bf16[32,64,512]{2,1,0:T(8,128)(2,1)S(1)} custom-call(bf16[2048,512]{1,0:T(8,128)(2,1)S(1)} %shard_map.92.n_a, bf16[2048,512]{1,0:T(8,128)(2,1)S(1)} %shard_map.93.n_b, bf16[32,64]{1,0:T(8,128)(2,1)S(1)} %get-tuple-element.11.wl_ref, s32[1,512]{1,0:T(1,128)S(1)} %bitcast.16, s32[1,64]{1,0:T(1,128)S(1)} %bitcast.18), custom_call_target="tpu_custom_call" | custom-call | flops 1073741824 | bytes 6297856 | tf_op jit(solution)/shard_map/pallas_call | solution.py:247
  19.6 3.6 %collective-permute-start.10 = (bf16[2048,512]{1,0:T(8,128)(2,1)S(1)}, bf16[2048,512]{1,0:T(8,128)(2,1)S(1)}, u32[]{:S(2)}, u32[]{:S(2)}) collective-permute-start(bf16[2048,512]{1,0:T(8,128)(2,1)S(1)} %bitcast.9), channel_id=1, source_target_pairs={{0,8},{8,0},{16,24},{24,16},{1,9},{9,1},{17,25},{25,17},{2,10},{10... | collective-permute-start | bytes 6291464 | tf_op jit(solution)/shard_map/ppermute | solution.py:309
  23.2 1.6 %shard_map.91.right = bf16[272,512]{1,0:T(8,128)(2,1)S(1)} custom-call(bf16[64,64,512]{2,1,0:T(8,128)(2,1)} %bitcast.32, s32[1,512]{1,0:T(1,128)} %bitcast.15, s32[1,64]{1,0:T(1,128)} %bitcast.17, f32[1,64]{1,0:T(1,128)} %bitcast.21, f32[1,64]{1,0:T(1,128)} %bitcast.24, bf16[32,64]{1,0:T(8,128)(2,1)} %bitcast.33), custom_call_target="tpu_custom_call" | custom-call | flops 20971520 | bytes 4479744 | tf_op jit(solution)/shard_map/pallas_call | solution.py:247
  24.8 0.1 collective-permute-start.3
  24.9 5.4 %collective-permute-start = (bf16[272,512]{1,0:T(8,128)(2,1)S(1)}, bf16[272,512]{1,0:T(8,128)(2,1)S(1)}, u32[]{:S(2)}, u32[]{:S(2)}) collective-permute-start(bf16[272,512]{1,0:T(8,128)(2,1)S(1)} %shard_map.91.right), channel_id=1, source_target_pairs={{0,32},{8,232},{16,48},{24,248},{32,64},{40,8},{48,80},{56,24},{64... | collective-permute-start | bytes 835592 | tf_op jit(solution)/shard_map/ppermute | solution.py:295
  30.3 0.0 collective-permute-done.3.other
  30.3 2.4 %collective-permute-start.4 = (bf16[272,512]{1,0:T(8,128)(2,1)S(1)}, bf16[272,512]{1,0:T(8,128)(2,1)S(1)}, u32[]{:S(2)}, u32[]{:S(2)}) collective-permute-start(bf16[272,512]{1,0:T(8,128)(2,1)S(1)} %collective-permute-done.3.other), channel_id=1, source_target_pairs={{0,32},{8,232},{16,48},{24,248},{32,64},{40,8},{48,80},{56,24},{64... | collective-permute-start | bytes 835592 | tf_op jit(solution)/shard_map/ppermute | solution.py:295
  32.7 1.1 %collective-permute-done.right = bf16[272,512]{1,0:T(8,128)(2,1)S(1)} collective-permute-done((bf16[272,512]{1,0:T(8,128)(2,1)S(1)}, bf16[272,512]{1,0:T(8,128)(2,1)S(1)}, u32[]{:S(2)}, u32[]{:S(2)}) %collective-permute-start) | collective-permute-done | bytes 278560 | tf_op jit(solution)/shard_map/ppermute | solution.py:295
  33.8 3.1 %collective-permute-start.1 = (bf16[272,512]{1,0:T(8,128)(2,1)S(1)}, bf16[272,512]{1,0:T(8,128)(2,1)S(1)}, u32[]{:S(2)}, u32[]{:S(2)}) collective-permute-start(bf16[272,512]{1,0:T(8,128)(2,1)S(1)} %collective-permute-done.right), channel_id=1, source_target_pairs={{0,32},{8,232},{16,48},{24,248},{32,64},{40,8},{48,80},{56,24},{64... | collective-permute-start | bytes 835592 | tf_op jit(solution)/shard_map/ppermute | solution.py:295
  36.9 0.0 collective-permute-done.4.other
  36.9 3.0 %collective-permute-start.5 = (bf16[272,512]{1,0:T(8,128)(2,1)S(1)}, bf16[272,512]{1,0:T(8,128)(2,1)S(1)}, u32[]{:S(2)}, u32[]{:S(2)}) collective-permute-start(bf16[272,512]{1,0:T(8,128)(2,1)S(1)} %collective-permute-done.4.other), channel_id=1, source_target_pairs={{0,32},{8,232},{16,48},{24,248},{32,64},{40,8},{48,80},{56,24},{64... | collective-permute-start | bytes 835592 | tf_op jit(solution)/shard_map/ppermute | solution.py:295
  39.9 0.5 collective-permute-done.1.right
  40.4 3.1 %collective-permute-start.2 = (bf16[272,512]{1,0:T(8,128)(2,1)S(1)}, bf16[272,512]{1,0:T(8,128)(2,1)S(1)}, u32[]{:S(2)}, u32[]{:S(2)}) collective-permute-start(bf16[272,512]{1,0:T(8,128)(2,1)S(1)} %collective-permute-done.1.right), channel_id=1, source_target_pairs={{0,32},{8,232},{16,48},{24,248},{32,64},{40,8},{48,80},{56,24},{64... | collective-permute-start | bytes 835592 | tf_op jit(solution)/shard_map/ppermute | solution.py:295
  43.5 0.0 collective-permute-done.5.other
  43.5 3.0 %collective-permute-start.6 = (bf16[272,512]{1,0:T(8,128)(2,1)S(1)}, bf16[272,512]{1,0:T(8,128)(2,1)S(1)}, u32[]{:S(2)}, u32[]{:S(2)}) collective-permute-start(bf16[272,512]{1,0:T(8,128)(2,1)S(1)} %collective-permute-done.5.other), channel_id=1, source_target_pairs={{0,32},{8,232},{16,48},{24,248},{32,64},{40,8},{48,80},{56,24},{64... | collective-permute-start | bytes 835592 | tf_op jit(solution)/shard_map/ppermute | solution.py:295
  46.5 0.5 collective-permute-done.2.right
  47.0 5.0 %collective-permute-start.13 = (bf16[272,512]{1,0:T(8,128)(2,1)S(1)}, bf16[272,512]{1,0:T(8,128)(2,1)S(1)}, u32[]{:S(2)}, u32[]{:S(2)}) collective-permute-start(bf16[272,512]{1,0:T(8,128)(2,1)S(1)} %collective-permute-done.2.right), channel_id=1, source_target_pairs={{8,232},{24,248},{40,8},{56,24},{72,40},{88,56},{104,72},{120,88},... | collective-permute-start | bytes 835592 | tf_op jit(solution)/shard_map/ppermute | solution.py:295
  52.0 0.0 collective-permute-done.6.other
  52.0 3.1 %collective-permute-start.14 = (bf16[272,512]{1,0:T(8,128)(2,1)S(1)}, bf16[272,512]{1,0:T(8,128)(2,1)S(1)}, u32[]{:S(2)}, u32[]{:S(2)}) collective-permute-start(bf16[272,512]{1,0:T(8,128)(2,1)S(1)} %collective-permute-done.6.other), channel_id=1, source_target_pairs={{8,232},{24,248},{40,8},{56,24},{72,40},{88,56},{104,72},{120,88},... | collective-permute-start | bytes 835592 | tf_op jit(solution)/shard_map/ppermute | solution.py:295
  55.2 0.0 collective-permute-done.10.lf_got
  55.2 1.8 %shard_map.103.two = f32[520,128]{1,0:T(8,128)S(1)} custom-call(bf16[272,512]{1,0:T(8,128)(2,1)S(1)} %collective-permute-done.1.right, bf16[272,512]{1,0:T(8,128)(2,1)S(1)} %collective-permute-done.5.other, bf16[2048,512]{1,0:T(8,128)(2,1)S(1)} %bitcast.10, bf16[2048,512]{1,0:T(8,128)(2,1)S(1)} %collective-permute-done.10.lf_got, ...), custom_call_target="tpu_custom_call" | custom-call | flops 1468006400 | bytes 5279744 | tf_op jit(solution)/shard_map/pallas_call | solution.py:247
  57.0 0.0 collective-permute-done.13.right
  57.0 2.3 %collective-permute-done.14.other = bf16[272,512]{1,0:T(8,128)(2,1)S(1)} collective-permute-done((bf16[272,512]{1,0:T(8,128)(2,1)S(1)}, bf16[272,512]{1,0:T(8,128)(2,1)S(1)}, u32[]{:S(2)}, u32[]{:S(2)}) %collective-permute-start.14) | collective-permute-done | bytes 278560 | tf_op jit(solution)/shard_map/ppermute | solution.py:295
  59.3 1.8 %shard_map.104 = (f32[520,128]{1,0:T(8,128)S(1)}, bf16[520,128]{1,0:T(8,128)(2,1)S(1)}) custom-call(bf16[272,512]{1,0:T(8,128)(2,1)S(1)} %collective-permute-done.13.right, bf16[272,512]{1,0:T(8,128)(2,1)S(1)} %collective-permute-done.14.other, f32[520,128]{1,0:T(8,128)S(1)} %shard_map.102.zero, f32[520,128]{1,0:T(8,128)S(1)} %shard_map.103.two, ...), custom_call_target="tpu_custom_call" | custom-call | flops 1468006400 | bytes 5945344 | tf_op jit(solution)/shard_map/pallas_call | solution.py:247
  61.2 2.5 %collective-permute-start.15 = (bf16[520,128]{1,0:T(8,128)(2,1)S(1)}, bf16[520,128]{1,0:T(8,128)(2,1)S(1)}, u32[]{:S(2)}, u32[]{:S(2)}) collective-permute-start(bf16[520,128]{1,0:T(8,128)(2,1)S(1)} %get-tuple-element.16), channel_id=1, source_target_pairs={{0,16},{8,24},{16,0},{24,8},{1,17},{9,25},{17,1},{25,9},{2,18},{10... | collective-permute-start | bytes 399368 | tf_op jit(solution)/shard_map/ppermute | solution.py:323
  63.7 1.8 %shard_map.99.one = f32[520,128]{1,0:T(8,128)S(1)} custom-call(bf16[272,512]{1,0:T(8,128)(2,1)S(1)} %collective-permute-done.right, bf16[272,512]{1,0:T(8,128)(2,1)S(1)} %collective-permute-done.4.other, bf16[2048,512]{1,0:T(8,128)(2,1)S(1)} %bitcast.13, bf16[2048,512]{1,0:T(8,128)(2,1)S(1)} %collective-permute-done.10.lf_got, ...), custom_call_target="tpu_custom_call" | custom-call | flops 1468006400 | bytes 5279744 | tf_op jit(solution)/shard_map/pallas_call | solution.py:247
  65.5 0.0 copy-start.3
  65.5 0.0 copy-start.7
  65.5 1.8 %shard_map.100 = (f32[520,128]{1,0:T(8,128)S(1)}, bf16[520,128]{1,0:T(8,128)(2,1)S(1)}) custom-call(bf16[272,512]{1,0:T(8,128)(2,1)S(1)} %collective-permute-done.2.right, bf16[272,512]{1,0:T(8,128)(2,1)S(1)} %collective-permute-done.6.other, f32[520,128]{1,0:T(8,128)S(1)} %shard_map.99.one, bf16[2048,512]{1,0:T(8,128)(2,1)S(1)} %bitcast.14, ...), custom_call_target="tpu_custom_call" | custom-call | flops 1468006400 | bytes 5679104 | tf_op jit(solution)/shard_map/pallas_call | solution.py:247
  67.3 0.6 collective-permute-start.11
  67.9 0.0 collective-permute-done.15.got
  67.9 0.0 copy-done.3
  67.9 0.0 copy-done.7
  67.9 0.3 shard_map.105
  68.2 4.1 %collective-permute-start.16 = (bf16[512,128]{1,0:T(8,128)(2,1)S(1)}, bf16[512,128]{1,0:T(8,128)(2,1)S(1)}, u32[]{:S(2)}, u32[]{:S(2)}) collective-permute-start(bf16[512,128]{1,0:T(8,128)(2,1)S(1)} %shard_map.105), channel_id=1, source_target_pairs={{0,0},{8,128},{16,192},{24,64},{32,32},{40,160},{48,224},{56,96},{... | collective-permute-start | bytes 393224 | tf_op jit(solution)/shard_map/ppermute | solution.py:334
  72.3 0.4 collective-permute-done.11.got
  72.8 0.3 shard_map.101
  73.0 0.1 collective-permute-start.12
  73.1 7.2 %collective-permute-done.16.even = bf16[512,128]{1,0:T(8,128)(2,1)S(1)} collective-permute-done((bf16[512,128]{1,0:T(8,128)(2,1)S(1)}, bf16[512,128]{1,0:T(8,128)(2,1)S(1)}, u32[]{:S(2)}, u32[]{:S(2)}) %collective-permute-start.16) | collective-permute-done | bytes 131104 | tf_op jit(solution)/shard_map/ppermute | solution.py:334
  80.3 0.0 collective-permute-done.12.odd
  80.3 0.9 %shard_map.106 = bf16[128,8,128]{2,1,0:T(8,128)(2,1)} custom-call(bf16[512,128]{1,0:T(8,128)(2,1)S(1)} %collective-permute-done.12.odd, bf16[512,128]{1,0:T(8,128)(2,1)S(1)} %collective-permute-done.16.even), custom_call_target="tpu_custom_call" | custom-call | bytes 524288 | tf_op jit(solution)/shard_map/pallas_call | solution.py:247
  (4 shorter events, 0.0 us)
Async XLA Ops:
  0.0 0.8 copy-start
  0.8 0.7 copy-start.8
  1.4 3.5 %collective-permute-start.7 = (bf16[144,128]{1,0:T(8,128)(2,1)S(1)}, bf16[144,128]{1,0:T(8,128)(2,1)S(1)}, u32[]{:S(2)}, u32[]{:S(2)}) collective-permute-start(bf16[144,128]{1,0:T(8,128)(2,1)S(1)} %shard_map.94.a), channel_id=1, source_target_pairs={{0,1},{1,0},{2,3},{3,2},{4,5},{5,4},{6,7},{7,6},{8,9},{9,8},{10,11... | collective-permute-start | bytes 110600 | tf_op jit(solution)/shard_map/ppermute | solution.py:278
  4.9 4.8 %collective-permute-start.8 = (bf16[2,144,128]{2,1,0:T(8,128)(2,1)S(1)}, bf16[2,144,128]{2,1,0:T(8,128)(2,1)S(1)}, u32[]{:S(2)}, u32[]{:S(2)}) collective-permute-start(bf16[2,144,128]{2,1,0:T(8,128)(2,1)S(1)} %shard_map.95.a), channel_id=1, source_target_pairs={{0,2},{1,3},{2,0},{3,1},{4,6},{5,7},{6,4},{7,5},{8,10},{9,11},{10,... | collective-permute-start | bytes 221192 | tf_op jit(solution)/shard_map/ppermute | solution.py:278
  9.7 8.0 %collective-permute-start.9 = (bf16[4,144,128]{2,1,0:T(8,128)(2,1)S(1)}, bf16[4,144,128]{2,1,0:T(8,128)(2,1)S(1)}, u32[]{:S(2)}, u32[]{:S(2)}) collective-permute-start(bf16[4,144,128]{2,1,0:T(8,128)(2,1)S(1)} %shard_map.96.near), channel_id=1, source_target_pairs={{0,4},{1,5},{2,6},{3,7},{4,0},{5,1},{6,2},{7,3},{8,12},{9,13},{10,... | collective-permute-start | bytes 442376 | tf_op jit(solution)/shard_map/ppermute | solution.py:278
  11.1 0.7 copy-start.4
  11.8 0.7 copy-start.5
  12.4 2.7 %copy-start.6 = (f32[64]{0:T(128)S(1)}, f32[64]{0:T(128)}, u32[]{:S(2)}) copy-start(f32[64]{0:T(128)} %param.13) | copy-start | bytes 772
  15.1 3.0 %copy-start.1 = (s32[512]{0:T(512)S(1)}, s32[512]{0:T(512)}, u32[]{:S(2)}) copy-start(s32[512]{0:T(512)} %param.10) | copy-start | bytes 6148
  15.1 3.0 %copy-start.2 = (s32[64]{0:T(128)S(1)}, s32[64]{0:T(128)}, u32[]{:S(2)}) copy-start(s32[64]{0:T(128)} %param.11) | copy-start | bytes 772
  19.6 35.6 %collective-permute-start.10 = (bf16[2048,512]{1,0:T(8,128)(2,1)S(1)}, bf16[2048,512]{1,0:T(8,128)(2,1)S(1)}, u32[]{:S(2)}, u32[]{:S(2)}) collective-permute-start(bf16[2048,512]{1,0:T(8,128)(2,1)S(1)} %bitcast.9), channel_id=1, source_target_pairs={{0,8},{8,0},{16,24},{24,16},{1,9},{9,1},{17,25},{25,17},{2,10},{10... | collective-permute-start | bytes 6291464 | tf_op jit(solution)/shard_map/ppermute | solution.py:309
  24.8 5.5 %collective-permute-start.3 = (bf16[272,512]{1,0:T(8,128)(2,1)S(1)}, bf16[272,512]{1,0:T(8,128)(2,1)S(1)}, u32[]{:S(2)}, u32[]{:S(2)}) collective-permute-start(bf16[272,512]{1,0:T(8,128)(2,1)S(1)} %shard_map.91.right), channel_id=1, source_target_pairs={{0,8},{8,0},{16,24},{24,16},{1,9},{9,1},{17,25},{25,17},{2,10},{10... | collective-permute-start | bytes 835592 | tf_op jit(solution)/shard_map/ppermute | solution.py:291
  24.9 8.9 %collective-permute-start = (bf16[272,512]{1,0:T(8,128)(2,1)S(1)}, bf16[272,512]{1,0:T(8,128)(2,1)S(1)}, u32[]{:S(2)}, u32[]{:S(2)}) collective-permute-start(bf16[272,512]{1,0:T(8,128)(2,1)S(1)} %shard_map.91.right), channel_id=1, source_target_pairs={{0,32},{8,232},{16,48},{24,248},{32,64},{40,8},{48,80},{56,24},{64... | collective-permute-start | bytes 835592 | tf_op jit(solution)/shard_map/ppermute | solution.py:295
  30.3 6.6 %collective-permute-start.4 = (bf16[272,512]{1,0:T(8,128)(2,1)S(1)}, bf16[272,512]{1,0:T(8,128)(2,1)S(1)}, u32[]{:S(2)}, u32[]{:S(2)}) collective-permute-start(bf16[272,512]{1,0:T(8,128)(2,1)S(1)} %collective-permute-done.3.other), channel_id=1, source_target_pairs={{0,32},{8,232},{16,48},{24,248},{32,64},{40,8},{48,80},{56,24},{64... | collective-permute-start | bytes 835592 | tf_op jit(solution)/shard_map/ppermute | solution.py:295
  33.8 6.6 %collective-permute-start.1 = (bf16[272,512]{1,0:T(8,128)(2,1)S(1)}, bf16[272,512]{1,0:T(8,128)(2,1)S(1)}, u32[]{:S(2)}, u32[]{:S(2)}) collective-permute-start(bf16[272,512]{1,0:T(8,128)(2,1)S(1)} %collective-permute-done.right), channel_id=1, source_target_pairs={{0,32},{8,232},{16,48},{24,248},{32,64},{40,8},{48,80},{56,24},{64... | collective-permute-start | bytes 835592 | tf_op jit(solution)/shard_map/ppermute | solution.py:295
  36.9 6.6 %collective-permute-start.5 = (bf16[272,512]{1,0:T(8,128)(2,1)S(1)}, bf16[272,512]{1,0:T(8,128)(2,1)S(1)}, u32[]{:S(2)}, u32[]{:S(2)}) collective-permute-start(bf16[272,512]{1,0:T(8,128)(2,1)S(1)} %collective-permute-done.4.other), channel_id=1, source_target_pairs={{0,32},{8,232},{16,48},{24,248},{32,64},{40,8},{48,80},{56,24},{64... | collective-permute-start | bytes 835592 | tf_op jit(solution)/shard_map/ppermute | solution.py:295
  40.4 6.6 %collective-permute-start.2 = (bf16[272,512]{1,0:T(8,128)(2,1)S(1)}, bf16[272,512]{1,0:T(8,128)(2,1)S(1)}, u32[]{:S(2)}, u32[]{:S(2)}) collective-permute-start(bf16[272,512]{1,0:T(8,128)(2,1)S(1)} %collective-permute-done.1.right), channel_id=1, source_target_pairs={{0,32},{8,232},{16,48},{24,248},{32,64},{40,8},{48,80},{56,24},{64... | collective-permute-start | bytes 835592 | tf_op jit(solution)/shard_map/ppermute | solution.py:295
  43.5 8.5 %collective-permute-start.6 = (bf16[272,512]{1,0:T(8,128)(2,1)S(1)}, bf16[272,512]{1,0:T(8,128)(2,1)S(1)}, u32[]{:S(2)}, u32[]{:S(2)}) collective-permute-start(bf16[272,512]{1,0:T(8,128)(2,1)S(1)} %collective-permute-done.5.other), channel_id=1, source_target_pairs={{0,32},{8,232},{16,48},{24,248},{32,64},{40,8},{48,80},{56,24},{64... | collective-permute-start | bytes 835592 | tf_op jit(solution)/shard_map/ppermute | solution.py:295
  47.0 10.0 %collective-permute-start.13 = (bf16[272,512]{1,0:T(8,128)(2,1)S(1)}, bf16[272,512]{1,0:T(8,128)(2,1)S(1)}, u32[]{:S(2)}, u32[]{:S(2)}) collective-permute-start(bf16[272,512]{1,0:T(8,128)(2,1)S(1)} %collective-permute-done.2.right), channel_id=1, source_target_pairs={{8,232},{24,248},{40,8},{56,24},{72,40},{88,56},{104,72},{120,88},... | collective-permute-start | bytes 835592 | tf_op jit(solution)/shard_map/ppermute | solution.py:295
  52.0 7.3 %collective-permute-start.14 = (bf16[272,512]{1,0:T(8,128)(2,1)S(1)}, bf16[272,512]{1,0:T(8,128)(2,1)S(1)}, u32[]{:S(2)}, u32[]{:S(2)}) collective-permute-start(bf16[272,512]{1,0:T(8,128)(2,1)S(1)} %collective-permute-done.6.other), channel_id=1, source_target_pairs={{8,232},{24,248},{40,8},{56,24},{72,40},{88,56},{104,72},{120,88},... | collective-permute-start | bytes 835592 | tf_op jit(solution)/shard_map/ppermute | solution.py:295
  61.2 6.7 %collective-permute-start.15 = (bf16[520,128]{1,0:T(8,128)(2,1)S(1)}, bf16[520,128]{1,0:T(8,128)(2,1)S(1)}, u32[]{:S(2)}, u32[]{:S(2)}) collective-permute-start(bf16[520,128]{1,0:T(8,128)(2,1)S(1)} %get-tuple-element.16), channel_id=1, source_target_pairs={{0,16},{8,24},{16,0},{24,8},{1,17},{9,25},{17,1},{25,9},{2,18},{10... | collective-permute-start | bytes 399368 | tf_op jit(solution)/shard_map/ppermute | solution.py:323
  65.5 2.4 %copy-start.3 = (s32[64]{0:T(128)S(1)}, s32[64]{0:T(128)}, u32[]{:S(2)}) copy-start(s32[64]{0:T(128)} %param.11) | copy-start | bytes 772
  65.5 2.4 %copy-start.7 = (f32[128]{0:T(128)S(1)}, f32[128]{0:T(128)}, u32[]{:S(2)}) copy-start(f32[128]{0:T(128)} %param.17) | copy-start | bytes 1540
  67.3 5.4 %collective-permute-start.11 = (bf16[520,128]{1,0:T(8,128)(2,1)S(1)}, bf16[520,128]{1,0:T(8,128)(2,1)S(1)}, u32[]{:S(2)}, u32[]{:S(2)}) collective-permute-start(bf16[520,128]{1,0:T(8,128)(2,1)S(1)} %get-tuple-element.14), channel_id=1, source_target_pairs={{0,16},{8,24},{16,0},{24,8},{1,17},{9,25},{17,1},{25,9},{2,18},{10... | collective-permute-start | bytes 399368 | tf_op jit(solution)/shard_map/ppermute | solution.py:321
  68.2 12.1 %collective-permute-start.16 = (bf16[512,128]{1,0:T(8,128)(2,1)S(1)}, bf16[512,128]{1,0:T(8,128)(2,1)S(1)}, u32[]{:S(2)}, u32[]{:S(2)}) collective-permute-start(bf16[512,128]{1,0:T(8,128)(2,1)S(1)} %shard_map.105), channel_id=1, source_target_pairs={{0,0},{8,128},{16,192},{24,64},{32,32},{40,160},{48,224},{56,96},{... | collective-permute-start | bytes 393224 | tf_op jit(solution)/shard_map/ppermute | solution.py:334
  73.0 7.3 %collective-permute-start.12 = (bf16[512,128]{1,0:T(8,128)(2,1)S(1)}, bf16[512,128]{1,0:T(8,128)(2,1)S(1)}, u32[]{:S(2)}, u32[]{:S(2)}) collective-permute-start(bf16[512,128]{1,0:T(8,128)(2,1)S(1)} %shard_map.101), channel_id=1, source_target_pairs={{0,160},{8,96},{16,224},{24,32},{32,192},{40,128},{48,0},{56,64},{... | collective-permute-start | bytes 393224 | tf_op jit(solution)/shard_map/ppermute | solution.py:333

commit v7 on v6

--- a/solution.py
+++ b/solution.py
@@ -118,7 +118,7 @@
             out_ref[pl.ds(pl.multiple_of((g * T + t) * M, M), M), :] = normed[0].astype(BF16)
             return carry
 
-        lax.fori_loop(0, T, one, 0, unroll=4)
+        lax.fori_loop(0, T, one, 0, unroll=8)
 
 
 def left_kernel(n_a, n_b, wl_ref, row_ref, tok_ref, out_ref):
@@ -141,6 +141,11 @@
         n_ref, at = (n_a, g) if g < N // T // 2 else (n_b, g - N // T // 2)
         part = jnp.dot(wide, n_ref[at * T * M : (at + 1) * T * M, :], preferred_element_type=F32)
         out_ref[:, g * T : (g + 1) * T, :] = (part.reshape(C, T, S) * weight[None]).astype(BF16)
+
+
+def join_kernel(own, got, out):
+    out[0] = own[...]
+    out[1] = got[...]
 
 
 def pair_block(right, other, lf_own, lf_got, w2_ref, spread, out):
@@ -190,8 +195,12 @@
     return lax.rem(lax.axis_index("col"), 2)
 
 
-def at_home():
-    return lax.axis_index("col") // 2 == lax.axis_index("row") // 4
+def keeps_three():
+    return lax.axis_index("col") // 2 == lax.rem(lax.axis_index("row"), 2)
+
+
+def keeps_last():
+    return lax.axis_index("col") // 2 != lax.axis_index("row") // 4
 
 
 def first_kernel(right, other, lf_own, lf_got, w2, out, spread):
@@ -206,19 +215,19 @@
 
 def odd_kernel(right, other, one, lf_own, lf_got, w2, keep, send, spread, three):
     pair_block(right, other, lf_own, lf_got, w2, spread, three)
-    choose(at_home(), three[...], one[...], keep, send)
-
-
-def even_kernel(right, other, zero, two, lf_own, lf_got, w2, keep, send, spread, last):
+    choose(keeps_three(), three[...], one[...], keep, send)
+
+
+def even_kernel(rights, zero, two, lf_own, lf_got, w2, keep, send, spread, last):
     @pl.when(core() == 1)
     def _():
-        pair_block(right, other, lf_own, lf_got, w2, spread, last)
+        pair_block(rights.at[0], rights.at[1], lf_own, lf_got, w2, spread, last)
 
     @pl.when(core() == 0)
     def _():
         last[...] = zero[...]
 
-    choose(at_home(), last[...], two[...], keep, send)
+    choose(keeps_last(), last[...], two[...], keep, send)
 
 
 def final_kernel(keep, got, tok_ref, bias_ref, out):
@@ -232,24 +241,34 @@
     out[...] = ((pairs + bias_ref[...][None]) / count).reshape(ROWS, Z).astype(BF16)
 
 
-def assemble_kernel(odd, even, out, flat):
-    low = lax.rem(lax.axis_index("row"), 2) == 0
-    a, b = odd[...].astype(F32), even[...].astype(F32)
-    for h, rows in enumerate((jnp.where(low, b, a), jnp.where(low, a, b))):
-        for t in range(T):
-            flat[h, pl.ds(t, N, stride=T), :] = rows[t * N : (t + 1) * N]
-        out[h * N : (h + 1) * N] = flat[h].reshape(N, T, Z).astype(BF16)
-
-
-def call(kernel, out, *args, specs=None, scratch=(), flops=0, limit=10):
+def place(block, half, out, flat, tile, sem):
+    rows = block[...].astype(F32)
+    for t in range(T):
+        flat[pl.ds(t, N, stride=T), :] = rows[t * N : (t + 1) * N]
+    tile[...] = flat[...].reshape(N, T, Z).astype(BF16)
+    copy = pltpu.make_async_copy(tile, out.at[pl.ds(half * N, N)], sem)
+    copy.start()
+    copy.wait()
+
+
+def odd_half_kernel(block, out, *scratch):
+    place(block, 1 - lax.rem(lax.axis_index("row"), 2), out, *scratch)
+
+
+def even_half_kernel(block, _, out, *scratch):
+    place(block, lax.rem(lax.axis_index("row"), 2), out, *scratch)
+
+
+def call(kernel, out, *args, specs=None, scratch=(), flops=0, limit=10, out_spec=VMEM, alias=None):
     leaves = jax.tree.leaves(out)
     bytes_accessed = sum(a.size * a.dtype.itemsize for a in list(args) + leaves)
     return pl.pallas_call(
         kernel,
         out_shape=out,
         in_specs=specs or [VMEM] * len(args),
-        out_specs=jax.tree.map(lambda _: VMEM, out),
+        out_specs=jax.tree.map(lambda _: out_spec, out),
         scratch_shapes=scratch,
+        input_output_aliases=alias or {},
         compiler_params=pltpu.CompilerParams(vmem_limit_bytes=limit << 20),
         cost_estimate=pl.CostEstimate(flops=flops, bytes_accessed=bytes_accessed, transcendentals=0),
     )(*args)
@@ -292,7 +311,11 @@
     right = [chains]
     for step in range(4):
         pairs = [(z * 4 + c, (z + 1 - 2 * (c % 2)) % 8 * 4 + c) for z in range(8) for c in range(4) if step < 3 or c % 2]
-        chains = [lax.ppermute(chains[i], ("row", "col"), pairs) for i in range(2)]
+        if step == 3:
+            both = call(join_kernel, shape((2, T * C + 16, S), BF16), *chains, limit=4)
+            chains = [lax.ppermute(both, ("row", "col"), pairs)]
+        else:
+            chains = [lax.ppermute(chains[i], ("row", "col"), pairs) for i in range(2)]
         right.append(chains)
 
     normed = [
@@ -326,13 +349,17 @@
     y1 = call(final_kernel, part, odd, f1, tok, out_bias)
     y2 = call(final_kernel, part, even, f2, tok, out_bias)
 
-    def home(near, far):
-        kept = {(z, c): (far if c // 2 == z // 4 else near)[c % 2] for z in range(8) for c in range(4)}
-        return [(z * 4 + c, (z + kept[z, c]) % 8 * 4 + z // 2) for z in range(8) for c in range(4)]
-
-    g1 = lax.ppermute(y1, ("row", "col"), home((-1, 1), (-3, 3)))
-    g2 = lax.ppermute(y2, ("row", "col"), home((-2, 2), (0, 4)))
-    return call(assemble_kernel, shape((2 * N, T, Z), BF16), g1, g2, scratch=[pltpu.VMEM((2, ROWS, Z), F32)], limit=4)
+    def home(kept):
+        return [(z * 4 + c, (z + kept(z, c // 2)[c % 2]) % 8 * 4 + z // 2) for z in range(8) for c in range(4)]
+
+    g1 = lax.ppermute(y1, ("row", "col"), home(lambda z, x: (-3, 3) if x == z % 2 else (-1, 1)))
+    g2 = lax.ppermute(y2, ("row", "col"), home(lambda z, x: (0, 4) if x != z // 4 else (-2, 2)))
+    scratch = [pltpu.VMEM((ROWS, Z), F32), pltpu.VMEM((N, T, Z), BF16), pltpu.SemaphoreType.DMA(())]
+    whole = shape((2 * N, T, Z), BF16)
+    out = call(odd_half_kernel, whole, g1, scratch=scratch, limit=4, out_spec=HBM)
+    return call(
+        even_half_kernel, whole, g2, out, specs=[VMEM, HBM], scratch=scratch, limit=4, out_spec=HBM, alias={1: 0}
+    )
 
 
 def solution(mesh):

time: 81.5 us -> 81.2 us (level)
  the two profiles are of different devices: /device:TPU:1 before, /device:TPU:12 now
where the time goes in v7:
time: 81.2 us; the launch traced here: 81 us
  waiting for transfers between devices  44.4 us (55%)
  Pallas kernels  18 us (22%)
  starting transfers between devices  15.5 us (19%)
  local copies, waits for them, and re-layouts  2.77 us (3%)
    ppermute x6, waiting for transfers between devices, program(): chains = [lax.ppermute(chains[i], ('row', 'col'), pairs) for i in range(2)]  24.6 us
    pallas_call x18, Pallas kernels, call(): pl.pallas_call(kernel, out_shape=out, in_specs=specs or [VMEM] * len(args...  18 us
    ppermute x3, waiting for transfers between devices, program(): got = lax.ppermute(packs, 'chan', [(c, c ^ 1 << step) for c in range(8)])  7.07 us
    ppermute x1, waiting for transfers between devices, program(): f2 = lax.ppermute(even_sent, 'col', xh_swap)  4.35 us
    ppermute x1, waiting for transfers between devices, program(): lax.ppermute(y2, ('row', 'col'), home(lambda z, x: (0, 4) if x != z // 4...  4.26 us
    ppermute x3, starting transfers between devices, program(): got = lax.ppermute(packs, 'chan', [(c, c ^ 1 << step) for c in range(8)])  4.03 us
    ppermute x6, starting transfers between devices, program(): chains = [lax.ppermute(chains[i], ('row', 'col'), pairs) for i in range(2)]  3.85 us
    ppermute x1, waiting for transfers between devices, program(): lax.ppermute(y1, ('row', 'col'), home(lambda z, x: (-3, 3) if x == z % 2...  3.32 us
  transfers between devices with their start and end apart: 16, of which 13 were waited for; matrix products, arithmetic and copies ran while one was open for 0% of the time, Pallas kernels for 19%

profile of v7, /device:TPU:12, one launch (start us, length us, event | category | flops | bytes accessed | tf_op | source)
XLA Modules:
  0.0 81.0 jit_solution(18225270729966936337)
XLA Ops:
  0.0 0.0 copy-start
  0.0 0.8 copy-done
  0.8 0.0 copy-start.8
  0.8 0.7 copy-done.8
  1.4 0.4 collective-permute-start.8
  1.9 3.5 %collective-permute-done.8.b = bf16[144,128]{1,0:T(8,128)(2,1)S(1)} collective-permute-done((bf16[144,128]{1,0:T(8,128)(2,1)S(1)}, bf16[144,128]{1,0:T(8,128)(2,1)S(1)}, u32[]{:S(2)}, u32[]{:S(2)}) %collective-permute-start.8) | collective-permute-done | bytes 36896 | tf_op jit(solution)/shard_map/ppermute | solution.py:297
  5.4 2.3 %collective-permute-start.9 = (bf16[2,144,128]{2,1,0:T(8,128)(2,1)S(1)}, bf16[2,144,128]{2,1,0:T(8,128)(2,1)S(1)}, u32[]{:S(2)}, u32[]{:S(2)}) collective-permute-start(bf16[2,144,128]{2,1,0:T(8,128)(2,1)S(1)} %shard_map.96.a), channel_id=1, source_target_pairs={{0,2},{1,3},{2,0},{3,1},{4,6},{5,7},{6,4},{7,5},{8,10},{9,11},{10,... | collective-permute-start | bytes 221192 | tf_op jit(solution)/shard_map/ppermute | solution.py:297
  7.7 3.6 %collective-permute-done.9.b = bf16[2,144,128]{2,1,0:T(8,128)(2,1)S(1)} collective-permute-done((bf16[2,144,128]{2,1,0:T(8,128)(2,1)S(1)}, bf16[2,144,128]{2,1,0:T(8,128)(2,1)S(1)}, u32[]{:S(2)}, u32[]{:S(2)}) %collective-permute-start.9) | collective-permute-done | bytes 73760 | tf_op jit(solution)/shard_map/ppermute | solution.py:297
  11.3 1.3 %collective-permute-start.10 = (bf16[4,144,128]{2,1,0:T(8,128)(2,1)S(1)}, bf16[4,144,128]{2,1,0:T(8,128)(2,1)S(1)}, u32[]{:S(2)}, u32[]{:S(2)}) collective-permute-start(bf16[4,144,128]{2,1,0:T(8,128)(2,1)S(1)} %shard_map.97.near), channel_id=1, source_target_pairs={{0,4},{1,5},{2,6},{3,7},{4,0},{5,1},{6,2},{7,3},{8,12},{9,13},{10,... | collective-permute-start | bytes 442376 | tf_op jit(solution)/shard_map/ppermute | solution.py:297
  12.6 0.0 copy-start.4
  12.6 0.7 copy-done.4
  13.2 0.0 copy-start.5
  13.2 0.7 copy-done.5
  13.9 0.0 copy-start.6
  13.9 2.6 %shard_map.93.n_a = bf16[2048,512]{1,0:T(8,128)(2,1)S(1)} custom-call(bf16[64,64,512]{2,1,0:T(8,128)(2,1)} %bitcast.30, f32[1,64]{1,0:T(1,128)S(1)} %bitcast.22, f32[1,64]{1,0:T(1,128)S(1)} %bitcast.25), custom_call_target="tpu_custom_call" | custom-call | flops 15728640 | bytes 6291968 | tf_op jit(solution)/shard_map/pallas_call | solution.py:265
  16.5 0.0 copy-done.6
  16.5 0.0 copy-start.1
  16.5 0.0 copy-start.2
  16.5 2.6 %shard_map.94.n_b = bf16[2048,512]{1,0:T(8,128)(2,1)S(1)} custom-call(bf16[64,64,512]{2,1,0:T(8,128)(2,1)} %bitcast.31, f32[1,64]{1,0:T(1,128)S(1)} %bitcast.23, f32[1,64]{1,0:T(1,128)S(1)} %bitcast.26), custom_call_target="tpu_custom_call" | custom-call | flops 15728640 | bytes 6291968 | tf_op jit(solution)/shard_map/pallas_call | solution.py:265
  19.1 0.0 collective-permute-done.10.far
  19.2 0.3 shard_map.98
  19.4 0.0 copy-done.1
  19.4 0.0 copy-done.2
  19.5 1.5 %shard_map.99 = bf16[32,64,512]{2,1,0:T(8,128)(2,1)S(1)} custom-call(bf16[2048,512]{1,0:T(8,128)(2,1)S(1)} %shard_map.93.n_a, bf16[2048,512]{1,0:T(8,128)(2,1)S(1)} %shard_map.94.n_b, bf16[32,64]{1,0:T(8,128)(2,1)S(1)} %get-tuple-element.11.wl_ref, s32[1,512]{1,0:T(1,128)S(1)} %bitcast.16, s32[1,64]{1,0:T(1,128)S(1)} %bitcast.18), custom_call_target="tpu_custom_call" | custom-call | flops 1073741824 | bytes 6297856 | tf_op jit(solution)/shard_map/pallas_call | solution.py:265
  20.9 0.1 collective-permute-start.11
  21.0 1.6 %shard_map.91.right = bf16[272,512]{1,0:T(8,128)(2,1)S(1)} custom-call(bf16[64,64,512]{2,1,0:T(8,128)(2,1)} %bitcast.32, s32[1,512]{1,0:T(1,128)} %bitcast.15, s32[1,64]{1,0:T(1,128)} %bitcast.17, f32[1,64]{1,0:T(1,128)} %bitcast.21, f32[1,64]{1,0:T(1,128)} %bitcast.24, bf16[32,64]{1,0:T(8,128)(2,1)} %bitcast.33), custom_call_target="tpu_custom_call" | custom-call | flops 20971520 | bytes 4479744 | tf_op jit(solution)/shard_map/pallas_call | solution.py:265
  22.7 0.6 collective-permute-start.3
  23.3 1.9 %collective-permute-start = (bf16[272,512]{1,0:T(8,128)(2,1)S(1)}, bf16[272,512]{1,0:T(8,128)(2,1)S(1)}, u32[]{:S(2)}, u32[]{:S(2)}) collective-permute-start(bf16[272,512]{1,0:T(8,128)(2,1)S(1)} %shard_map.91.right), channel_id=1, source_target_pairs={{0,32},{8,232},{16,48},{24,248},{32,64},{40,8},{48,80},{56,24},{64... | collective-permute-start | bytes 835592 | tf_op jit(solution)/shard_map/ppermute | solution.py:318
  25.2 0.4 collective-permute-done.3.other
  25.6 1.9 %collective-permute-start.4 = (bf16[272,512]{1,0:T(8,128)(2,1)S(1)}, bf16[272,512]{1,0:T(8,128)(2,1)S(1)}, u32[]{:S(2)}, u32[]{:S(2)}) collective-permute-start(bf16[272,512]{1,0:T(8,128)(2,1)S(1)} %collective-permute-done.3.other), channel_id=1, source_target_pairs={{0,32},{8,232},{16,48},{24,248},{32,64},{40,8},{48,80},{56,24},{64... | collective-permute-start | bytes 835592 | tf_op jit(solution)/shard_map/ppermute | solution.py:318
  27.5 6.1 %collective-permute-done.right = bf16[272,512]{1,0:T(8,128)(2,1)S(1)} collective-permute-done((bf16[272,512]{1,0:T(8,128)(2,1)S(1)}, bf16[272,512]{1,0:T(8,128)(2,1)S(1)}, u32[]{:S(2)}, u32[]{:S(2)}) %collective-permute-start) | collective-permute-done | bytes 278560 | tf_op jit(solution)/shard_map/ppermute | solution.py:318
  33.6 0.0 collective-permute-start.1
  33.6 3.0 %collective-permute-done.4.other = bf16[272,512]{1,0:T(8,128)(2,1)S(1)} collective-permute-done((bf16[272,512]{1,0:T(8,128)(2,1)S(1)}, bf16[272,512]{1,0:T(8,128)(2,1)S(1)}, u32[]{:S(2)}, u32[]{:S(2)}) %collective-permute-start.4) | collective-permute-done | bytes 278560 | tf_op jit(solution)/shard_map/ppermute | solution.py:318
  36.6 0.0 collective-permute-start.5
  36.6 4.8 %collective-permute-done.1.right = bf16[272,512]{1,0:T(8,128)(2,1)S(1)} collective-permute-done((bf16[272,512]{1,0:T(8,128)(2,1)S(1)}, bf16[272,512]{1,0:T(8,128)(2,1)S(1)}, u32[]{:S(2)}, u32[]{:S(2)}) %collective-permute-start.1) | collective-permute-done | bytes 278560 | tf_op jit(solution)/shard_map/ppermute | solution.py:318
  41.4 0.0 collective-permute-start.2
  41.4 3.0 %collective-permute-done.5.other = bf16[272,512]{1,0:T(8,128)(2,1)S(1)} collective-permute-done((bf16[272,512]{1,0:T(8,128)(2,1)S(1)}, bf16[272,512]{1,0:T(8,128)(2,1)S(1)}, u32[]{:S(2)}, u32[]{:S(2)}) %collective-permute-start.5) | collective-permute-done | bytes 278560 | tf_op jit(solution)/shard_map/ppermute | solution.py:318
  44.4 0.0 collective-permute-start.6
  44.4 4.8 %collective-permute-done.2.own.right = bf16[272,512]{1,0:T(8,128)(2,1)S(1)} collective-permute-done((bf16[272,512]{1,0:T(8,128)(2,1)S(1)}, bf16[272,512]{1,0:T(8,128)(2,1)S(1)}, u32[]{:S(2)}, u32[]{:S(2)}) %collective-permute-start.2) | collective-permute-done | bytes 278560 | tf_op jit(solution)/shard_map/ppermute | solution.py:318
  49.2 3.0 %collective-permute-done.6.got.other = bf16[272,512]{1,0:T(8,128)(2,1)S(1)} collective-permute-done((bf16[272,512]{1,0:T(8,128)(2,1)S(1)}, bf16[272,512]{1,0:T(8,128)(2,1)S(1)}, u32[]{:S(2)}, u32[]{:S(2)}) %collective-permute-start.6) | collective-permute-done | bytes 278560 | tf_op jit(solution)/shard_map/ppermute | solution.py:318
  52.2 0.7 collective-permute-start.7
  52.9 0.0 collective-permute-done.11.lf_got
  52.9 1.8 %shard_map.104.one = f32[520,128]{1,0:T(8,128)S(1)} custom-call(bf16[272,512]{1,0:T(8,128)(2,1)S(1)} %collective-permute-done.right, bf16[272,512]{1,0:T(8,128)(2,1)S(1)} %collective-permute-done.4.other, bf16[2048,512]{1,0:T(8,128)(2,1)S(1)} %bitcast.10, bf16[2048,512]{1,0:T(8,128)(2,1)S(1)} %collective-permute-done.11.lf_got, ...), custom_call_target="tpu_custom_call" | custom-call | flops 1468006400 | bytes 5279744 | tf_op jit(solution)/shard_map/pallas_call | solution.py:265
  54.7 1.8 %shard_map.105 = (f32[520,128]{1,0:T(8,128)S(1)}, bf16[520,128]{1,0:T(8,128)(2,1)S(1)}) custom-call(bf16[272,512]{1,0:T(8,128)(2,1)S(1)} %collective-permute-done.2.own.right, bf16[272,512]{1,0:T(8,128)(2,1)S(1)} %collective-permute-done.6.got.other, f32[520,128]{1,0:T(8,128)S(1)} %shard_map.104.one, bf16[2048,512]{1,0:T(8,128)(2,1)S(1)} %bitcast.11, ...), custom_call_target="tpu_custom_call" | custom-call | flops 1468006400 | bytes 5679104 | tf_op jit(solution)/shard_map/pallas_call | solution.py:265
  56.5 0.9 %collective-permute-start.14 = (bf16[520,128]{1,0:T(8,128)(2,1)S(1)}, bf16[520,128]{1,0:T(8,128)(2,1)S(1)}, u32[]{:S(2)}, u32[]{:S(2)}) collective-permute-start(bf16[520,128]{1,0:T(8,128)(2,1)S(1)} %get-tuple-element.16), channel_id=1, source_target_pairs={{0,16},{8,24},{16,0},{24,8},{1,17},{9,25},{17,1},{25,9},{2,18},{10... | collective-permute-start | bytes 399368 | tf_op jit(solution)/shard_map/ppermute | solution.py:344
  57.4 1.8 %shard_map.101.two = f32[520,128]{1,0:T(8,128)S(1)} custom-call(bf16[272,512]{1,0:T(8,128)(2,1)S(1)} %collective-permute-done.1.right, bf16[272,512]{1,0:T(8,128)(2,1)S(1)} %collective-permute-done.5.other, bf16[2048,512]{1,0:T(8,128)(2,1)S(1)} %bitcast.12, bf16[2048,512]{1,0:T(8,128)(2,1)S(1)} %collective-permute-done.11.lf_got, ...), custom_call_target="tpu_custom_call" | custom-call | flops 1468006400 | bytes 5279744 | tf_op jit(solution)/shard_map/pallas_call | solution.py:265
  59.2 1.8 %shard_map.100.zero = f32[520,128]{1,0:T(8,128)S(1)} custom-call(bf16[272,512]{1,0:T(8,128)(2,1)S(1)} %shard_map.91.right, bf16[272,512]{1,0:T(8,128)(2,1)S(1)} %collective-permute-done.3.other, bf16[2048,512]{1,0:T(8,128)(2,1)S(1)} %bitcast.13, bf16[2048,512]{1,0:T(8,128)(2,1)S(1)} %collective-permute-done.11.lf_got, bf16[256,512]{1,0:T(8,128)(2,1)S(1)} %get-tuple-element.12.w2), custom_call_target="tpu_custom_call" | custom-call | flops 1468006400 | bytes 5279744 | tf_op jit(solution)/shard_map/pallas_call | solution.py:265
  61.0 0.0 copy-start.3
  61.0 0.0 copy-start.7
  61.0 0.0 collective-permute-done.7.rights
  61.1 0.1 shard_map.102
  61.2 2.8 %collective-permute-start.12 = (bf16[520,128]{1,0:T(8,128)(2,1)S(1)}, bf16[520,128]{1,0:T(8,128)(2,1)S(1)}, u32[]{:S(2)}, u32[]{:S(2)}) collective-permute-start(bf16[520,128]{1,0:T(8,128)(2,1)S(1)} %get-tuple-element.14), channel_id=1, source_target_pairs={{0,16},{8,24},{16,0},{24,8},{1,17},{9,25},{17,1},{25,9},{2,18},{10... | collective-permute-start | bytes 399368 | tf_op jit(solution)/shard_map/ppermute | solution.py:346
  64.0 0.4 collective-permute-done.14.got
  64.3 0.0 copy-done.3
  64.3 0.0 copy-done.7
  64.3 0.3 shard_map.106
  64.6 0.1 collective-permute-start.15
  64.7 4.3 %collective-permute-done.12.got = bf16[520,128]{1,0:T(8,128)(2,1)S(1)} collective-permute-done((bf16[520,128]{1,0:T(8,128)(2,1)S(1)}, bf16[520,128]{1,0:T(8,128)(2,1)S(1)}, u32[]{:S(2)}, u32[]{:S(2)}) %collective-permute-start.12) | collective-permute-done | bytes 133152 | tf_op jit(solution)/shard_map/ppermute | solution.py:346
  69.0 0.3 shard_map.103
  69.3 2.5 %collective-permute-start.13 = (bf16[512,128]{1,0:T(8,128)(2,1)S(1)}, bf16[512,128]{1,0:T(8,128)(2,1)S(1)}, u32[]{:S(2)}, u32[]{:S(2)}) collective-permute-start(bf16[512,128]{1,0:T(8,128)(2,1)S(1)} %shard_map.103), channel_id=1, source_target_pairs={{0,192},{8,64},{16,0},{24,128},{32,224},{40,96},{48,32},{56,160},{... | collective-permute-start | bytes 393224 | tf_op jit(solution)/shard_map/ppermute | solution.py:356
  71.8 3.3 %collective-permute-done.15.block = bf16[512,128]{1,0:T(8,128)(2,1)S(1)} collective-permute-done((bf16[512,128]{1,0:T(8,128)(2,1)S(1)}, bf16[512,128]{1,0:T(8,128)(2,1)S(1)}, u32[]{:S(2)}, u32[]{:S(2)}) %collective-permute-start.15) | collective-permute-done | bytes 131104 | tf_op jit(solution)/shard_map/ppermute | solution.py:355
  75.1 0.7 shard_map.107._
  75.8 4.3 %collective-permute-done.13.block = bf16[512,128]{1,0:T(8,128)(2,1)S(1)} collective-permute-done((bf16[512,128]{1,0:T(8,128)(2,1)S(1)}, bf16[512,128]{1,0:T(8,128)(2,1)S(1)}, u32[]{:S(2)}, u32[]{:S(2)}) %collective-permute-start.13) | collective-permute-done | bytes 131104 | tf_op jit(solution)/shard_map/ppermute | solution.py:356
  80.1 0.7 shard_map.108
  (4 shorter events, 0.1 us)
Async XLA Ops:
  0.0 0.8 copy-start
  0.8 0.7 copy-start.8
  1.4 4.0 %collective-permute-start.8 = (bf16[144,128]{1,0:T(8,128)(2,1)S(1)}, bf16[144,128]{1,0:T(8,128)(2,1)S(1)}, u32[]{:S(2)}, u32[]{:S(2)}) collective-permute-start(bf16[144,128]{1,0:T(8,128)(2,1)S(1)} %shard_map.95.a), channel_id=1, source_target_pairs={{0,1},{1,0},{2,3},{3,2},{4,5},{5,4},{6,7},{7,6},{8,9},{9,8},{10,11... | collective-permute-start | bytes 110600 | tf_op jit(solution)/shard_map/ppermute | solution.py:297
  5.4 5.9 %collective-permute-start.9 = (bf16[2,144,128]{2,1,0:T(8,128)(2,1)S(1)}, bf16[2,144,128]{2,1,0:T(8,128)(2,1)S(1)}, u32[]{:S(2)}, u32[]{:S(2)}) collective-permute-start(bf16[2,144,128]{2,1,0:T(8,128)(2,1)S(1)} %shard_map.96.a), channel_id=1, source_target_pairs={{0,2},{1,3},{2,0},{3,1},{4,6},{5,7},{6,4},{7,5},{8,10},{9,11},{10,... | collective-permute-start | bytes 221192 | tf_op jit(solution)/shard_map/ppermute | solution.py:297
  11.3 7.9 %collective-permute-start.10 = (bf16[4,144,128]{2,1,0:T(8,128)(2,1)S(1)}, bf16[4,144,128]{2,1,0:T(8,128)(2,1)S(1)}, u32[]{:S(2)}, u32[]{:S(2)}) collective-permute-start(bf16[4,144,128]{2,1,0:T(8,128)(2,1)S(1)} %shard_map.97.near), channel_id=1, source_target_pairs={{0,4},{1,5},{2,6},{3,7},{4,0},{5,1},{6,2},{7,3},{8,12},{9,13},{10,... | collective-permute-start | bytes 442376 | tf_op jit(solution)/shard_map/ppermute | solution.py:297
  12.6 0.7 copy-start.4
  13.2 0.7 copy-start.5
  13.9 2.6 %copy-start.6 = (f32[64]{0:T(128)S(1)}, f32[64]{0:T(128)}, u32[]{:S(2)}) copy-start(f32[64]{0:T(128)} %param.13) | copy-start | bytes 772
  16.5 2.9 %copy-start.1 = (s32[512]{0:T(512)S(1)}, s32[512]{0:T(512)}, u32[]{:S(2)}) copy-start(s32[512]{0:T(512)} %param.10) | copy-start | bytes 6148
  16.5 2.9 %copy-start.2 = (s32[64]{0:T(128)S(1)}, s32[64]{0:T(128)}, u32[]{:S(2)}) copy-start(s32[64]{0:T(128)} %param.11) | copy-start | bytes 772
  20.9 31.9 %collective-permute-start.11 = (bf16[2048,512]{1,0:T(8,128)(2,1)S(1)}, bf16[2048,512]{1,0:T(8,128)(2,1)S(1)}, u32[]{:S(2)}, u32[]{:S(2)}) collective-permute-start(bf16[2048,512]{1,0:T(8,128)(2,1)S(1)} %bitcast.9), channel_id=1, source_target_pairs={{0,8},{8,0},{16,24},{24,16},{1,9},{9,1},{17,25},{25,17},{2,10},{10... | collective-permute-start | bytes 6291464 | tf_op jit(solution)/shard_map/ppermute | solution.py:332
  22.7 2.9 %collective-permute-start.3 = (bf16[272,512]{1,0:T(8,128)(2,1)S(1)}, bf16[272,512]{1,0:T(8,128)(2,1)S(1)}, u32[]{:S(2)}, u32[]{:S(2)}) collective-permute-start(bf16[272,512]{1,0:T(8,128)(2,1)S(1)} %shard_map.91.right), channel_id=1, source_target_pairs={{0,8},{8,0},{16,24},{24,16},{1,9},{9,1},{17,25},{25,17},{2,10},{10... | collective-permute-start | bytes 835592 | tf_op jit(solution)/shard_map/ppermute | solution.py:310
  23.3 10.4 %collective-permute-start = (bf16[272,512]{1,0:T(8,128)(2,1)S(1)}, bf16[272,512]{1,0:T(8,128)(2,1)S(1)}, u32[]{:S(2)}, u32[]{:S(2)}) collective-permute-start(bf16[272,512]{1,0:T(8,128)(2,1)S(1)} %shard_map.91.right), channel_id=1, source_target_pairs={{0,32},{8,232},{16,48},{24,248},{32,64},{40,8},{48,80},{56,24},{64... | collective-permute-start | bytes 835592 | tf_op jit(solution)/shard_map/ppermute | solution.py:318
  25.6 11.0 %collective-permute-start.4 = (bf16[272,512]{1,0:T(8,128)(2,1)S(1)}, bf16[272,512]{1,0:T(8,128)(2,1)S(1)}, u32[]{:S(2)}, u32[]{:S(2)}) collective-permute-start(bf16[272,512]{1,0:T(8,128)(2,1)S(1)} %collective-permute-done.3.other), channel_id=1, source_target_pairs={{0,32},{8,232},{16,48},{24,248},{32,64},{40,8},{48,80},{56,24},{64... | collective-permute-start | bytes 835592 | tf_op jit(solution)/shard_map/ppermute | solution.py:318
  33.6 7.8 %collective-permute-start.1 = (bf16[272,512]{1,0:T(8,128)(2,1)S(1)}, bf16[272,512]{1,0:T(8,128)(2,1)S(1)}, u32[]{:S(2)}, u32[]{:S(2)}) collective-permute-start(bf16[272,512]{1,0:T(8,128)(2,1)S(1)} %collective-permute-done.right), channel_id=1, source_target_pairs={{0,32},{8,232},{16,48},{24,248},{32,64},{40,8},{48,80},{56,24},{64... | collective-permute-start | bytes 835592 | tf_op jit(solution)/shard_map/ppermute | solution.py:318
  36.6 7.8 %collective-permute-start.5 = (bf16[272,512]{1,0:T(8,128)(2,1)S(1)}, bf16[272,512]{1,0:T(8,128)(2,1)S(1)}, u32[]{:S(2)}, u32[]{:S(2)}) collective-permute-start(bf16[272,512]{1,0:T(8,128)(2,1)S(1)} %collective-permute-done.4.other), channel_id=1, source_target_pairs={{0,32},{8,232},{16,48},{24,248},{32,64},{40,8},{48,80},{56,24},{64... | collective-permute-start | bytes 835592 | tf_op jit(solution)/shard_map/ppermute | solution.py:318
  41.4 7.8 %collective-permute-start.2 = (bf16[272,512]{1,0:T(8,128)(2,1)S(1)}, bf16[272,512]{1,0:T(8,128)(2,1)S(1)}, u32[]{:S(2)}, u32[]{:S(2)}) collective-permute-start(bf16[272,512]{1,0:T(8,128)(2,1)S(1)} %collective-permute-done.1.right), channel_id=1, source_target_pairs={{0,32},{8,232},{16,48},{24,248},{32,64},{40,8},{48,80},{56,24},{64... | collective-permute-start | bytes 835592 | tf_op jit(solution)/shard_map/ppermute | solution.py:318
  44.4 7.8 %collective-permute-start.6 = (bf16[272,512]{1,0:T(8,128)(2,1)S(1)}, bf16[272,512]{1,0:T(8,128)(2,1)S(1)}, u32[]{:S(2)}, u32[]{:S(2)}) collective-permute-start(bf16[272,512]{1,0:T(8,128)(2,1)S(1)} %collective-permute-done.5.other), channel_id=1, source_target_pairs={{0,32},{8,232},{16,48},{24,248},{32,64},{40,8},{48,80},{56,24},{64... | collective-permute-start | bytes 835592 | tf_op jit(solution)/shard_map/ppermute | solution.py:318
  52.2 8.9 %collective-permute-start.7 = (bf16[2,272,512]{2,1,0:T(8,128)(2,1)S(1)}, bf16[2,272,512]{2,1,0:T(8,128)(2,1)S(1)}, u32[]{:S(2)}, u32[]{:S(2)}) collective-permute-start(bf16[2,272,512]{2,1,0:T(8,128)(2,1)S(1)} %shard_map.92), channel_id=1, source_target_pairs={{8,232},{24,248},{40,8},{56,24},{72,40},{88,56},{104,72},{120,88},... | collective-permute-start | bytes 1671176 | tf_op jit(solution)/shard_map/ppermute | solution.py:316
  56.5 7.8 %collective-permute-start.14 = (bf16[520,128]{1,0:T(8,128)(2,1)S(1)}, bf16[520,128]{1,0:T(8,128)(2,1)S(1)}, u32[]{:S(2)}, u32[]{:S(2)}) collective-permute-start(bf16[520,128]{1,0:T(8,128)(2,1)S(1)} %get-tuple-element.16), channel_id=1, source_target_pairs={{0,16},{8,24},{16,0},{24,8},{1,17},{9,25},{17,1},{25,9},{2,18},{10... | collective-permute-start | bytes 399368 | tf_op jit(solution)/shard_map/ppermute | solution.py:344
  61.0 3.3 %copy-start.3 = (s32[64]{0:T(128)S(1)}, s32[64]{0:T(128)}, u32[]{:S(2)}) copy-start(s32[64]{0:T(128)} %param.11) | copy-start | bytes 772
  61.0 3.3 %copy-start.7 = (f32[128]{0:T(128)S(1)}, f32[128]{0:T(128)}, u32[]{:S(2)}) copy-start(f32[128]{0:T(128)} %param.17) | copy-start | bytes 1540
  61.2 7.9 %collective-permute-start.12 = (bf16[520,128]{1,0:T(8,128)(2,1)S(1)}, bf16[520,128]{1,0:T(8,128)(2,1)S(1)}, u32[]{:S(2)}, u32[]{:S(2)}) collective-permute-start(bf16[520,128]{1,0:T(8,128)(2,1)S(1)} %get-tuple-element.14), channel_id=1, source_target_pairs={{0,16},{8,24},{16,0},{24,8},{1,17},{9,25},{17,1},{25,9},{2,18},{10... | collective-permute-start | bytes 399368 | tf_op jit(solution)/shard_map/ppermute | solution.py:346
  64.6 10.5 %collective-permute-start.15 = (bf16[512,128]{1,0:T(8,128)(2,1)S(1)}, bf16[512,128]{1,0:T(8,128)(2,1)S(1)}, u32[]{:S(2)}, u32[]{:S(2)}) collective-permute-start(bf16[512,128]{1,0:T(8,128)(2,1)S(1)} %shard_map.106), channel_id=1, source_target_pairs={{0,160},{8,96},{16,224},{24,32},{32,0},{40,64},{48,192},{56,128},{... | collective-permute-start | bytes 393224 | tf_op jit(solution)/shard_map/ppermute | solution.py:355
  69.3 10.8 %collective-permute-start.13 = (bf16[512,128]{1,0:T(8,128)(2,1)S(1)}, bf16[512,128]{1,0:T(8,128)(2,1)S(1)}, u32[]{:S(2)}, u32[]{:S(2)}) collective-permute-start(bf16[512,128]{1,0:T(8,128)(2,1)S(1)} %shard_map.103), channel_id=1, source_target_pairs={{0,192},{8,64},{16,0},{24,128},{32,224},{40,96},{48,32},{56,160},{... | collective-permute-start | bytes 393224 | tf_op jit(solution)/shard_map/ppermute | solution.py:356

commit v8 on v6

--- a/solution.py
+++ b/solution.py
@@ -118,7 +118,7 @@
             out_ref[pl.ds(pl.multiple_of((g * T + t) * M, M), M), :] = normed[0].astype(BF16)
             return carry
 
-        lax.fori_loop(0, T, one, 0, unroll=4)
+        lax.fori_loop(0, T, one, 0, unroll=8)
 
 
 def left_kernel(n_a, n_b, wl_ref, row_ref, tok_ref, out_ref):
@@ -190,8 +190,12 @@
     return lax.rem(lax.axis_index("col"), 2)
 
 
-def at_home():
-    return lax.axis_index("col") // 2 == lax.axis_index("row") // 4
+def keeps_three():
+    return lax.axis_index("col") // 2 == lax.rem(lax.axis_index("row"), 2)
+
+
+def keeps_last():
+    return lax.axis_index("col") // 2 != lax.axis_index("row") // 4
 
 
 def first_kernel(right, other, lf_own, lf_got, w2, out, spread):
@@ -206,7 +210,7 @@
 
 def odd_kernel(right, other, one, lf_own, lf_got, w2, keep, send, spread, three):
     pair_block(right, other, lf_own, lf_got, w2, spread, three)
-    choose(at_home(), three[...], one[...], keep, send)
+    choose(keeps_three(), three[...], one[...], keep, send)
 
 
 def even_kernel(right, other, zero, two, lf_own, lf_got, w2, keep, send, spread, last):
@@ -218,7 +222,7 @@
     def _():
         last[...] = zero[...]
 
-    choose(at_home(), last[...], two[...], keep, send)
+    choose(keeps_last(), last[...], two[...], keep, send)
 
 
 def final_kernel(keep, got, tok_ref, bias_ref, out):
@@ -326,12 +330,11 @@
     y1 = call(final_kernel, part, odd, f1, tok, out_bias)
     y2 = call(final_kernel, part, even, f2, tok, out_bias)
 
-    def home(near, far):
-        kept = {(z, c): (far if c // 2 == z // 4 else near)[c % 2] for z in range(8) for c in range(4)}
-        return [(z * 4 + c, (z + kept[z, c]) % 8 * 4 + z // 2) for z in range(8) for c in range(4)]
-
-    g1 = lax.ppermute(y1, ("row", "col"), home((-1, 1), (-3, 3)))
-    g2 = lax.ppermute(y2, ("row", "col"), home((-2, 2), (0, 4)))
+    def home(kept):
+        return [(z * 4 + c, (z + kept(z, c // 2)[c % 2]) % 8 * 4 + z // 2) for z in range(8) for c in range(4)]
+
+    g1 = lax.ppermute(y1, ("row", "col"), home(lambda z, x: (-3, 3) if x == z % 2 else (-1, 1)))
+    g2 = lax.ppermute(y2, ("row", "col"), home(lambda z, x: (0, 4) if x != z // 4 else (-2, 2)))
     return call(assemble_kernel, shape((2 * N, T, Z), BF16), g1, g2, scratch=[pltpu.VMEM((2, ROWS, Z), F32)], limit=4)
 
 

time: 81.5 us -> 83.6 us (1.026)
  waiting for transfers between devices: 15.2 us -> 21.6 us
  starting transfers between devices: 45.7 us -> 41.5 us
    ppermute x1, waiting for transfers between devices: 0.44 us -> 5.3 us  [program(): f1 = lax.ppermute(odd_sent, 'col', xh_swap)]
    ppermute x2, starting transfers between devices: 4.19 us -> 0.18 us  [the longest x1 0.09 us: program(): lax.ppermute(y1, ('row', 'col'), home(lambda z, x: (-3, 3) if x == z % 2...]
    ppermute x2, waiting for transfers between devices: 7.22 us -> 8.58 us  [the longest x1 6.76 us: program(): lax.ppermute(y1, ('row', 'col'), home(lambda z, x: (-3, 3) if x == z % 2...]
  transfers between devices with their start and end apart: 17 -> 17, of which waited for: 8 -> 9; matrix products, arithmetic and copies ran while one was open for 0% -> 0% of each run, Pallas kernels for 16% -> 15%
where the time goes in v8:
time: 83.6 us; the launch traced here: 83.3 us
  starting transfers between devices  41.5 us (50%)
  waiting for transfers between devices  21.6 us (26%)
  Pallas kernels  17.2 us (21%)
  local copies, waits for them, and re-layouts  2.77 us (3%)
    ppermute x8, starting transfers between devices, program(): chains = [lax.ppermute(chains[i], ('row', 'col'), pairs) for i in range(2)]  28 us
    pallas_call x16, Pallas kernels, call(): pl.pallas_call(kernel, out_shape=out, in_specs=specs or [VMEM] * len(args...  17.2 us
    ppermute x1, waiting for transfers between devices, program(): lax.ppermute(y1, ('row', 'col'), home(lambda z, x: (-3, 3) if x == z % 2...  6.76 us
    ppermute x3, starting transfers between devices, program(): got = lax.ppermute(packs, 'chan', [(c, c ^ 1 << step) for c in range(8)])  6.55 us
    ppermute x1, waiting for transfers between devices, program(): f1 = lax.ppermute(odd_sent, 'col', xh_swap)  5.3 us
    ppermute x8, waiting for transfers between devices, program(): chains = [lax.ppermute(chains[i], ('row', 'col'), pairs) for i in range(2)]  4.64 us
    ppermute x1, starting transfers between devices, program(): lf_got = lax.ppermute(lf, 'col', core_swap)  3.57 us
    ppermute x3, waiting for transfers between devices, program(): got = lax.ppermute(packs, 'chan', [(c, c ^ 1 << step) for c in range(8)])  3.09 us
  transfers between devices with their start and end apart: 17, of which 9 were waited for; matrix products, arithmetic and copies ran while one was open for 0% of the time, Pallas kernels for 15%

profile of v8, /device:TPU:1, one launch (start us, length us, event | category | flops | bytes accessed | tf_op | source)
XLA Modules:
  0.0 83.3 jit_solution(17283482934633872753)
XLA Ops:
  0.0 0.0 copy-start
  0.0 0.8 copy-done
  0.8 0.0 copy-start.8
  0.8 0.7 copy-done.8
  1.4 2.1 %collective-permute-start.7 = (bf16[144,128]{1,0:T(8,128)(2,1)S(1)}, bf16[144,128]{1,0:T(8,128)(2,1)S(1)}, u32[]{:S(2)}, u32[]{:S(2)}) collective-permute-start(bf16[144,128]{1,0:T(8,128)(2,1)S(1)} %shard_map.94.a), channel_id=1, source_target_pairs={{0,1},{1,0},{2,3},{3,2},{4,5},{5,4},{6,7},{7,6},{8,9},{9,8},{10,11... | collective-permute-start | bytes 110600 | tf_op jit(solution)/shard_map/ppermute | solution.py:282
  3.6 1.3 %collective-permute-done.7.b = bf16[144,128]{1,0:T(8,128)(2,1)S(1)} collective-permute-done((bf16[144,128]{1,0:T(8,128)(2,1)S(1)}, bf16[144,128]{1,0:T(8,128)(2,1)S(1)}, u32[]{:S(2)}, u32[]{:S(2)}) %collective-permute-start.7) | collective-permute-done | bytes 36896 | tf_op jit(solution)/shard_map/ppermute | solution.py:282
  4.9 3.1 %collective-permute-start.8 = (bf16[2,144,128]{2,1,0:T(8,128)(2,1)S(1)}, bf16[2,144,128]{2,1,0:T(8,128)(2,1)S(1)}, u32[]{:S(2)}, u32[]{:S(2)}) collective-permute-start(bf16[2,144,128]{2,1,0:T(8,128)(2,1)S(1)} %shard_map.95.a), channel_id=1, source_target_pairs={{0,2},{1,3},{2,0},{3,1},{4,6},{5,7},{6,4},{7,5},{8,10},{9,11},{10,... | collective-permute-start | bytes 221192 | tf_op jit(solution)/shard_map/ppermute | solution.py:282
  8.0 1.7 %collective-permute-done.8.b = bf16[2,144,128]{2,1,0:T(8,128)(2,1)S(1)} collective-permute-done((bf16[2,144,128]{2,1,0:T(8,128)(2,1)S(1)}, bf16[2,144,128]{2,1,0:T(8,128)(2,1)S(1)}, u32[]{:S(2)}, u32[]{:S(2)}) %collective-permute-start.8) | collective-permute-done | bytes 73760 | tf_op jit(solution)/shard_map/ppermute | solution.py:282
  9.7 1.4 %collective-permute-start.9 = (bf16[4,144,128]{2,1,0:T(8,128)(2,1)S(1)}, bf16[4,144,128]{2,1,0:T(8,128)(2,1)S(1)}, u32[]{:S(2)}, u32[]{:S(2)}) collective-permute-start(bf16[4,144,128]{2,1,0:T(8,128)(2,1)S(1)} %shard_map.96.near), channel_id=1, source_target_pairs={{0,4},{1,5},{2,6},{3,7},{4,0},{5,1},{6,2},{7,3},{8,12},{9,13},{10,... | collective-permute-start | bytes 442376 | tf_op jit(solution)/shard_map/ppermute | solution.py:282
  11.1 0.0 copy-start.4
  11.1 0.7 copy-done.4
  11.8 0.0 copy-start.5
  11.8 0.7 copy-done.5
  12.4 0.0 copy-start.6
  12.4 2.6 %shard_map.92.n_a = bf16[2048,512]{1,0:T(8,128)(2,1)S(1)} custom-call(bf16[64,64,512]{2,1,0:T(8,128)(2,1)} %bitcast.30, f32[1,64]{1,0:T(1,128)S(1)} %bitcast.22, f32[1,64]{1,0:T(1,128)S(1)} %bitcast.25), custom_call_target="tpu_custom_call" | custom-call | flops 15728640 | bytes 6291968 | tf_op jit(solution)/shard_map/pallas_call | solution.py:251
  15.0 0.0 copy-done.6
  15.0 0.0 copy-start.1
  15.1 0.0 copy-start.2
  15.1 2.6 %shard_map.93.n_b = bf16[2048,512]{1,0:T(8,128)(2,1)S(1)} custom-call(bf16[64,64,512]{2,1,0:T(8,128)(2,1)} %bitcast.31, f32[1,64]{1,0:T(1,128)S(1)} %bitcast.23, f32[1,64]{1,0:T(1,128)S(1)} %bitcast.26), custom_call_target="tpu_custom_call" | custom-call | flops 15728640 | bytes 6291968 | tf_op jit(solution)/shard_map/pallas_call | solution.py:251
  17.7 0.0 collective-permute-done.9.far
  17.7 0.3 shard_map.97
  18.0 0.0 copy-done.1
  18.0 0.0 copy-done.2
  18.0 1.5 %shard_map.98 = bf16[32,64,512]{2,1,0:T(8,128)(2,1)S(1)} custom-call(bf16[2048,512]{1,0:T(8,128)(2,1)S(1)} %shard_map.92.n_a, bf16[2048,512]{1,0:T(8,128)(2,1)S(1)} %shard_map.93.n_b, bf16[32,64]{1,0:T(8,128)(2,1)S(1)} %get-tuple-element.11.wl_ref, s32[1,512]{1,0:T(1,128)S(1)} %bitcast.16, s32[1,64]{1,0:T(1,128)S(1)} %bitcast.18), custom_call_target="tpu_custom_call" | custom-call | flops 1073741824 | bytes 6297856 | tf_op jit(solution)/shard_map/pallas_call | solution.py:251
  19.5 3.6 %collective-permute-start.10 = (bf16[2048,512]{1,0:T(8,128)(2,1)S(1)}, bf16[2048,512]{1,0:T(8,128)(2,1)S(1)}, u32[]{:S(2)}, u32[]{:S(2)}) collective-permute-start(bf16[2048,512]{1,0:T(8,128)(2,1)S(1)} %bitcast.9), channel_id=1, source_target_pairs={{0,8},{8,0},{16,24},{24,16},{1,9},{9,1},{17,25},{25,17},{2,10},{10... | collective-permute-start | bytes 6291464 | tf_op jit(solution)/shard_map/ppermute | solution.py:313
  23.1 1.6 %shard_map.91.right = bf16[272,512]{1,0:T(8,128)(2,1)S(1)} custom-call(bf16[64,64,512]{2,1,0:T(8,128)(2,1)} %bitcast.32, s32[1,512]{1,0:T(1,128)} %bitcast.15, s32[1,64]{1,0:T(1,128)} %bitcast.17, f32[1,64]{1,0:T(1,128)} %bitcast.21, f32[1,64]{1,0:T(1,128)} %bitcast.24, bf16[32,64]{1,0:T(8,128)(2,1)} %bitcast.33), custom_call_target="tpu_custom_call" | custom-call | flops 20971520 | bytes 4479744 | tf_op jit(solution)/shard_map/pallas_call | solution.py:251
  24.7 0.1 collective-permute-start.3
  24.8 5.4 %collective-permute-start = (bf16[272,512]{1,0:T(8,128)(2,1)S(1)}, bf16[272,512]{1,0:T(8,128)(2,1)S(1)}, u32[]{:S(2)}, u32[]{:S(2)}) collective-permute-start(bf16[272,512]{1,0:T(8,128)(2,1)S(1)} %shard_map.91.right), channel_id=1, source_target_pairs={{0,32},{8,232},{16,48},{24,248},{32,64},{40,8},{48,80},{56,24},{64... | collective-permute-start | bytes 835592 | tf_op jit(solution)/shard_map/ppermute | solution.py:299
  30.2 0.0 collective-permute-done.3.other
  30.2 2.4 %collective-permute-start.4 = (bf16[272,512]{1,0:T(8,128)(2,1)S(1)}, bf16[272,512]{1,0:T(8,128)(2,1)S(1)}, u32[]{:S(2)}, u32[]{:S(2)}) collective-permute-start(bf16[272,512]{1,0:T(8,128)(2,1)S(1)} %collective-permute-done.3.other), channel_id=1, source_target_pairs={{0,32},{8,232},{16,48},{24,248},{32,64},{40,8},{48,80},{56,24},{64... | collective-permute-start | bytes 835592 | tf_op jit(solution)/shard_map/ppermute | solution.py:299
  32.6 1.1 %collective-permute-done.right = bf16[272,512]{1,0:T(8,128)(2,1)S(1)} collective-permute-done((bf16[272,512]{1,0:T(8,128)(2,1)S(1)}, bf16[272,512]{1,0:T(8,128)(2,1)S(1)}, u32[]{:S(2)}, u32[]{:S(2)}) %collective-permute-start) | collective-permute-done | bytes 278560 | tf_op jit(solution)/shard_map/ppermute | solution.py:299
  33.7 3.1 %collective-permute-start.1 = (bf16[272,512]{1,0:T(8,128)(2,1)S(1)}, bf16[272,512]{1,0:T(8,128)(2,1)S(1)}, u32[]{:S(2)}, u32[]{:S(2)}) collective-permute-start(bf16[272,512]{1,0:T(8,128)(2,1)S(1)} %collective-permute-done.right), channel_id=1, source_target_pairs={{0,32},{8,232},{16,48},{24,248},{32,64},{40,8},{48,80},{56,24},{64... | collective-permute-start | bytes 835592 | tf_op jit(solution)/shard_map/ppermute | solution.py:299
  36.8 0.0 collective-permute-done.4.other
  36.8 3.0 %collective-permute-start.5 = (bf16[272,512]{1,0:T(8,128)(2,1)S(1)}, bf16[272,512]{1,0:T(8,128)(2,1)S(1)}, u32[]{:S(2)}, u32[]{:S(2)}) collective-permute-start(bf16[272,512]{1,0:T(8,128)(2,1)S(1)} %collective-permute-done.4.other), channel_id=1, source_target_pairs={{0,32},{8,232},{16,48},{24,248},{32,64},{40,8},{48,80},{56,24},{64... | collective-permute-start | bytes 835592 | tf_op jit(solution)/shard_map/ppermute | solution.py:299
  39.8 0.5 collective-permute-done.1.right
  40.3 3.1 %collective-permute-start.2 = (bf16[272,512]{1,0:T(8,128)(2,1)S(1)}, bf16[272,512]{1,0:T(8,128)(2,1)S(1)}, u32[]{:S(2)}, u32[]{:S(2)}) collective-permute-start(bf16[272,512]{1,0:T(8,128)(2,1)S(1)} %collective-permute-done.1.right), channel_id=1, source_target_pairs={{0,32},{8,232},{16,48},{24,248},{32,64},{40,8},{48,80},{56,24},{64... | collective-permute-start | bytes 835592 | tf_op jit(solution)/shard_map/ppermute | solution.py:299
  43.4 0.0 collective-permute-done.5.other
  43.4 3.0 %collective-permute-start.6 = (bf16[272,512]{1,0:T(8,128)(2,1)S(1)}, bf16[272,512]{1,0:T(8,128)(2,1)S(1)}, u32[]{:S(2)}, u32[]{:S(2)}) collective-permute-start(bf16[272,512]{1,0:T(8,128)(2,1)S(1)} %collective-permute-done.5.other), channel_id=1, source_target_pairs={{0,32},{8,232},{16,48},{24,248},{32,64},{40,8},{48,80},{56,24},{64... | collective-permute-start | bytes 835592 | tf_op jit(solution)/shard_map/ppermute | solution.py:299
  46.4 0.5 collective-permute-done.2.right
  46.9 5.0 %collective-permute-start.13 = (bf16[272,512]{1,0:T(8,128)(2,1)S(1)}, bf16[272,512]{1,0:T(8,128)(2,1)S(1)}, u32[]{:S(2)}, u32[]{:S(2)}) collective-permute-start(bf16[272,512]{1,0:T(8,128)(2,1)S(1)} %collective-permute-done.2.right), channel_id=1, source_target_pairs={{8,232},{24,248},{40,8},{56,24},{72,40},{88,56},{104,72},{120,88},... | collective-permute-start | bytes 835592 | tf_op jit(solution)/shard_map/ppermute | solution.py:299
  51.9 0.0 collective-permute-done.6.other
  51.9 3.0 %collective-permute-start.14 = (bf16[272,512]{1,0:T(8,128)(2,1)S(1)}, bf16[272,512]{1,0:T(8,128)(2,1)S(1)}, u32[]{:S(2)}, u32[]{:S(2)}) collective-permute-start(bf16[272,512]{1,0:T(8,128)(2,1)S(1)} %collective-permute-done.6.other), channel_id=1, source_target_pairs={{8,232},{24,248},{40,8},{56,24},{72,40},{88,56},{104,72},{120,88},... | collective-permute-start | bytes 835592 | tf_op jit(solution)/shard_map/ppermute | solution.py:299
  54.9 0.0 collective-permute-done.10.lf_got
  54.9 1.8 %shard_map.103.two = f32[520,128]{1,0:T(8,128)S(1)} custom-call(bf16[272,512]{1,0:T(8,128)(2,1)S(1)} %collective-permute-done.1.right, bf16[272,512]{1,0:T(8,128)(2,1)S(1)} %collective-permute-done.5.other, bf16[2048,512]{1,0:T(8,128)(2,1)S(1)} %bitcast.10, bf16[2048,512]{1,0:T(8,128)(2,1)S(1)} %collective-permute-done.10.lf_got, ...), custom_call_target="tpu_custom_call" | custom-call | flops 1468006400 | bytes 5279744 | tf_op jit(solution)/shard_map/pallas_call | solution.py:251
  56.7 0.0 collective-permute-done.13.right
  56.7 2.5 %collective-permute-done.14.other = bf16[272,512]{1,0:T(8,128)(2,1)S(1)} collective-permute-done((bf16[272,512]{1,0:T(8,128)(2,1)S(1)}, bf16[272,512]{1,0:T(8,128)(2,1)S(1)}, u32[]{:S(2)}, u32[]{:S(2)}) %collective-permute-start.14) | collective-permute-done | bytes 278560 | tf_op jit(solution)/shard_map/ppermute | solution.py:299
  59.2 1.8 %shard_map.104 = (f32[520,128]{1,0:T(8,128)S(1)}, bf16[520,128]{1,0:T(8,128)(2,1)S(1)}) custom-call(bf16[272,512]{1,0:T(8,128)(2,1)S(1)} %collective-permute-done.13.right, bf16[272,512]{1,0:T(8,128)(2,1)S(1)} %collective-permute-done.14.other, f32[520,128]{1,0:T(8,128)S(1)} %shard_map.102.zero, f32[520,128]{1,0:T(8,128)S(1)} %shard_map.103.two, ...), custom_call_target="tpu_custom_call" | custom-call | flops 1468006400 | bytes 5945344 | tf_op jit(solution)/shard_map/pallas_call | solution.py:251
  61.1 2.5 %collective-permute-start.15 = (bf16[520,128]{1,0:T(8,128)(2,1)S(1)}, bf16[520,128]{1,0:T(8,128)(2,1)S(1)}, u32[]{:S(2)}, u32[]{:S(2)}) collective-permute-start(bf16[520,128]{1,0:T(8,128)(2,1)S(1)} %get-tuple-element.16), channel_id=1, source_target_pairs={{0,16},{8,24},{16,0},{24,8},{1,17},{9,25},{17,1},{25,9},{2,18},{10... | collective-permute-start | bytes 399368 | tf_op jit(solution)/shard_map/ppermute | solution.py:327
  63.6 1.8 %shard_map.99.one = f32[520,128]{1,0:T(8,128)S(1)} custom-call(bf16[272,512]{1,0:T(8,128)(2,1)S(1)} %collective-permute-done.right, bf16[272,512]{1,0:T(8,128)(2,1)S(1)} %collective-permute-done.4.other, bf16[2048,512]{1,0:T(8,128)(2,1)S(1)} %bitcast.13, bf16[2048,512]{1,0:T(8,128)(2,1)S(1)} %collective-permute-done.10.lf_got, ...), custom_call_target="tpu_custom_call" | custom-call | flops 1468006400 | bytes 5279744 | tf_op jit(solution)/shard_map/pallas_call | solution.py:251
  65.4 0.0 copy-start.3
  65.4 0.0 copy-start.7
  65.4 1.8 %shard_map.100 = (f32[520,128]{1,0:T(8,128)S(1)}, bf16[520,128]{1,0:T(8,128)(2,1)S(1)}) custom-call(bf16[272,512]{1,0:T(8,128)(2,1)S(1)} %collective-permute-done.2.right, bf16[272,512]{1,0:T(8,128)(2,1)S(1)} %collective-permute-done.6.other, f32[520,128]{1,0:T(8,128)S(1)} %shard_map.99.one, bf16[2048,512]{1,0:T(8,128)(2,1)S(1)} %bitcast.14, ...), custom_call_target="tpu_custom_call" | custom-call | flops 1468006400 | bytes 5679104 | tf_op jit(solution)/shard_map/pallas_call | solution.py:251
  67.2 0.6 collective-permute-start.11
  67.8 0.0 collective-permute-done.15.got
  67.8 0.0 copy-done.3
  67.8 0.0 copy-done.7
  67.8 0.3 shard_map.105
  68.1 0.1 collective-permute-start.16
  68.2 5.3 %collective-permute-done.11.got = bf16[520,128]{1,0:T(8,128)(2,1)S(1)} collective-permute-done((bf16[520,128]{1,0:T(8,128)(2,1)S(1)}, bf16[520,128]{1,0:T(8,128)(2,1)S(1)}, u32[]{:S(2)}, u32[]{:S(2)}) %collective-permute-start.11) | collective-permute-done | bytes 133152 | tf_op jit(solution)/shard_map/ppermute | solution.py:325
  73.5 0.3 shard_map.101
  73.8 0.1 collective-permute-start.12
  73.8 1.8 %collective-permute-done.16.even = bf16[512,128]{1,0:T(8,128)(2,1)S(1)} collective-permute-done((bf16[512,128]{1,0:T(8,128)(2,1)S(1)}, bf16[512,128]{1,0:T(8,128)(2,1)S(1)}, u32[]{:S(2)}, u32[]{:S(2)}) %collective-permute-start.16) | collective-permute-done | bytes 131104 | tf_op jit(solution)/shard_map/ppermute | solution.py:337
  75.7 6.8 %collective-permute-done.12.odd = bf16[512,128]{1,0:T(8,128)(2,1)S(1)} collective-permute-done((bf16[512,128]{1,0:T(8,128)(2,1)S(1)}, bf16[512,128]{1,0:T(8,128)(2,1)S(1)}, u32[]{:S(2)}, u32[]{:S(2)}) %collective-permute-start.12) | collective-permute-done | bytes 131104 | tf_op jit(solution)/shard_map/ppermute | solution.py:336
  82.4 0.8 %shard_map.106 = bf16[128,8,128]{2,1,0:T(8,128)(2,1)} custom-call(bf16[512,128]{1,0:T(8,128)(2,1)S(1)} %collective-permute-done.12.odd, bf16[512,128]{1,0:T(8,128)(2,1)S(1)} %collective-permute-done.16.even), custom_call_target="tpu_custom_call" | custom-call | bytes 524288 | tf_op jit(solution)/shard_map/pallas_call | solution.py:251
  (4 shorter events, 0.0 us)
Async XLA Ops:
  0.0 0.8 copy-start
  0.8 0.7 copy-start.8
  1.4 3.5 %collective-permute-start.7 = (bf16[144,128]{1,0:T(8,128)(2,1)S(1)}, bf16[144,128]{1,0:T(8,128)(2,1)S(1)}, u32[]{:S(2)}, u32[]{:S(2)}) collective-permute-start(bf16[144,128]{1,0:T(8,128)(2,1)S(1)} %shard_map.94.a), channel_id=1, source_target_pairs={{0,1},{1,0},{2,3},{3,2},{4,5},{5,4},{6,7},{7,6},{8,9},{9,8},{10,11... | collective-permute-start | bytes 110600 | tf_op jit(solution)/shard_map/ppermute | solution.py:282
  4.9 4.8 %collective-permute-start.8 = (bf16[2,144,128]{2,1,0:T(8,128)(2,1)S(1)}, bf16[2,144,128]{2,1,0:T(8,128)(2,1)S(1)}, u32[]{:S(2)}, u32[]{:S(2)}) collective-permute-start(bf16[2,144,128]{2,1,0:T(8,128)(2,1)S(1)} %shard_map.95.a), channel_id=1, source_target_pairs={{0,2},{1,3},{2,0},{3,1},{4,6},{5,7},{6,4},{7,5},{8,10},{9,11},{10,... | collective-permute-start | bytes 221192 | tf_op jit(solution)/shard_map/ppermute | solution.py:282
  9.7 7.9 %collective-permute-start.9 = (bf16[4,144,128]{2,1,0:T(8,128)(2,1)S(1)}, bf16[4,144,128]{2,1,0:T(8,128)(2,1)S(1)}, u32[]{:S(2)}, u32[]{:S(2)}) collective-permute-start(bf16[4,144,128]{2,1,0:T(8,128)(2,1)S(1)} %shard_map.96.near), channel_id=1, source_target_pairs={{0,4},{1,5},{2,6},{3,7},{4,0},{5,1},{6,2},{7,3},{8,12},{9,13},{10,... | collective-permute-start | bytes 442376 | tf_op jit(solution)/shard_map/ppermute | solution.py:282
  11.1 0.7 copy-start.4
  11.8 0.7 copy-start.5
  12.4 2.6 %copy-start.6 = (f32[64]{0:T(128)S(1)}, f32[64]{0:T(128)}, u32[]{:S(2)}) copy-start(f32[64]{0:T(128)} %param.13) | copy-start | bytes 772
  15.0 2.9 %copy-start.1 = (s32[512]{0:T(512)S(1)}, s32[512]{0:T(512)}, u32[]{:S(2)}) copy-start(s32[512]{0:T(512)} %param.10) | copy-start | bytes 6148
  15.1 2.9 %copy-start.2 = (s32[64]{0:T(128)S(1)}, s32[64]{0:T(128)}, u32[]{:S(2)}) copy-start(s32[64]{0:T(128)} %param.11) | copy-start | bytes 772
  19.5 35.4 %collective-permute-start.10 = (bf16[2048,512]{1,0:T(8,128)(2,1)S(1)}, bf16[2048,512]{1,0:T(8,128)(2,1)S(1)}, u32[]{:S(2)}, u32[]{:S(2)}) collective-permute-start(bf16[2048,512]{1,0:T(8,128)(2,1)S(1)} %bitcast.9), channel_id=1, source_target_pairs={{0,8},{8,0},{16,24},{24,16},{1,9},{9,1},{17,25},{25,17},{2,10},{10... | collective-permute-start | bytes 6291464 | tf_op jit(solution)/shard_map/ppermute | solution.py:313
  24.7 5.5 %collective-permute-start.3 = (bf16[272,512]{1,0:T(8,128)(2,1)S(1)}, bf16[272,512]{1,0:T(8,128)(2,1)S(1)}, u32[]{:S(2)}, u32[]{:S(2)}) collective-permute-start(bf16[272,512]{1,0:T(8,128)(2,1)S(1)} %shard_map.91.right), channel_id=1, source_target_pairs={{0,8},{8,0},{16,24},{24,16},{1,9},{9,1},{17,25},{25,17},{2,10},{10... | collective-permute-start | bytes 835592 | tf_op jit(solution)/shard_map/ppermute | solution.py:295
  24.8 8.9 %collective-permute-start = (bf16[272,512]{1,0:T(8,128)(2,1)S(1)}, bf16[272,512]{1,0:T(8,128)(2,1)S(1)}, u32[]{:S(2)}, u32[]{:S(2)}) collective-permute-start(bf16[272,512]{1,0:T(8,128)(2,1)S(1)} %shard_map.91.right), channel_id=1, source_target_pairs={{0,32},{8,232},{16,48},{24,248},{32,64},{40,8},{48,80},{56,24},{64... | collective-permute-start | bytes 835592 | tf_op jit(solution)/shard_map/ppermute | solution.py:299
  30.2 6.6 %collective-permute-start.4 = (bf16[272,512]{1,0:T(8,128)(2,1)S(1)}, bf16[272,512]{1,0:T(8,128)(2,1)S(1)}, u32[]{:S(2)}, u32[]{:S(2)}) collective-permute-start(bf16[272,512]{1,0:T(8,128)(2,1)S(1)} %collective-permute-done.3.other), channel_id=1, source_target_pairs={{0,32},{8,232},{16,48},{24,248},{32,64},{40,8},{48,80},{56,24},{64... | collective-permute-start | bytes 835592 | tf_op jit(solution)/shard_map/ppermute | solution.py:299
  33.7 6.6 %collective-permute-start.1 = (bf16[272,512]{1,0:T(8,128)(2,1)S(1)}, bf16[272,512]{1,0:T(8,128)(2,1)S(1)}, u32[]{:S(2)}, u32[]{:S(2)}) collective-permute-start(bf16[272,512]{1,0:T(8,128)(2,1)S(1)} %collective-permute-done.right), channel_id=1, source_target_pairs={{0,32},{8,232},{16,48},{24,248},{32,64},{40,8},{48,80},{56,24},{64... | collective-permute-start | bytes 835592 | tf_op jit(solution)/shard_map/ppermute | solution.py:299
  36.8 6.6 %collective-permute-start.5 = (bf16[272,512]{1,0:T(8,128)(2,1)S(1)}, bf16[272,512]{1,0:T(8,128)(2,1)S(1)}, u32[]{:S(2)}, u32[]{:S(2)}) collective-permute-start(bf16[272,512]{1,0:T(8,128)(2,1)S(1)} %collective-permute-done.4.other), channel_id=1, source_target_pairs={{0,32},{8,232},{16,48},{24,248},{32,64},{40,8},{48,80},{56,24},{64... | collective-permute-start | bytes 835592 | tf_op jit(solution)/shard_map/ppermute | solution.py:299
  40.3 6.6 %collective-permute-start.2 = (bf16[272,512]{1,0:T(8,128)(2,1)S(1)}, bf16[272,512]{1,0:T(8,128)(2,1)S(1)}, u32[]{:S(2)}, u32[]{:S(2)}) collective-permute-start(bf16[272,512]{1,0:T(8,128)(2,1)S(1)} %collective-permute-done.1.right), channel_id=1, source_target_pairs={{0,32},{8,232},{16,48},{24,248},{32,64},{40,8},{48,80},{56,24},{64... | collective-permute-start | bytes 835592 | tf_op jit(solution)/shard_map/ppermute | solution.py:299
  43.4 8.5 %collective-permute-start.6 = (bf16[272,512]{1,0:T(8,128)(2,1)S(1)}, bf16[272,512]{1,0:T(8,128)(2,1)S(1)}, u32[]{:S(2)}, u32[]{:S(2)}) collective-permute-start(bf16[272,512]{1,0:T(8,128)(2,1)S(1)} %collective-permute-done.5.other), channel_id=1, source_target_pairs={{0,32},{8,232},{16,48},{24,248},{32,64},{40,8},{48,80},{56,24},{64... | collective-permute-start | bytes 835592 | tf_op jit(solution)/shard_map/ppermute | solution.py:299
  46.9 9.8 %collective-permute-start.13 = (bf16[272,512]{1,0:T(8,128)(2,1)S(1)}, bf16[272,512]{1,0:T(8,128)(2,1)S(1)}, u32[]{:S(2)}, u32[]{:S(2)}) collective-permute-start(bf16[272,512]{1,0:T(8,128)(2,1)S(1)} %collective-permute-done.2.right), channel_id=1, source_target_pairs={{8,232},{24,248},{40,8},{56,24},{72,40},{88,56},{104,72},{120,88},... | collective-permute-start | bytes 835592 | tf_op jit(solution)/shard_map/ppermute | solution.py:299
  51.9 7.3 %collective-permute-start.14 = (bf16[272,512]{1,0:T(8,128)(2,1)S(1)}, bf16[272,512]{1,0:T(8,128)(2,1)S(1)}, u32[]{:S(2)}, u32[]{:S(2)}) collective-permute-start(bf16[272,512]{1,0:T(8,128)(2,1)S(1)} %collective-permute-done.6.other), channel_id=1, source_target_pairs={{8,232},{24,248},{40,8},{56,24},{72,40},{88,56},{104,72},{120,88},... | collective-permute-start | bytes 835592 | tf_op jit(solution)/shard_map/ppermute | solution.py:299
  61.1 6.7 %collective-permute-start.15 = (bf16[520,128]{1,0:T(8,128)(2,1)S(1)}, bf16[520,128]{1,0:T(8,128)(2,1)S(1)}, u32[]{:S(2)}, u32[]{:S(2)}) collective-permute-start(bf16[520,128]{1,0:T(8,128)(2,1)S(1)} %get-tuple-element.16), channel_id=1, source_target_pairs={{0,16},{8,24},{16,0},{24,8},{1,17},{9,25},{17,1},{25,9},{2,18},{10... | collective-permute-start | bytes 399368 | tf_op jit(solution)/shard_map/ppermute | solution.py:327
  65.4 2.4 %copy-start.3 = (s32[64]{0:T(128)S(1)}, s32[64]{0:T(128)}, u32[]{:S(2)}) copy-start(s32[64]{0:T(128)} %param.11) | copy-start | bytes 772
  65.4 2.4 %copy-start.7 = (f32[128]{0:T(128)S(1)}, f32[128]{0:T(128)}, u32[]{:S(2)}) copy-start(f32[128]{0:T(128)} %param.17) | copy-start | bytes 1540
  67.2 6.3 %collective-permute-start.11 = (bf16[520,128]{1,0:T(8,128)(2,1)S(1)}, bf16[520,128]{1,0:T(8,128)(2,1)S(1)}, u32[]{:S(2)}, u32[]{:S(2)}) collective-permute-start(bf16[520,128]{1,0:T(8,128)(2,1)S(1)} %get-tuple-element.14), channel_id=1, source_target_pairs={{0,16},{8,24},{16,0},{24,8},{1,17},{9,25},{17,1},{25,9},{2,18},{10... | collective-permute-start | bytes 399368 | tf_op jit(solution)/shard_map/ppermute | solution.py:325
  68.1 7.6 %collective-permute-start.16 = (bf16[512,128]{1,0:T(8,128)(2,1)S(1)}, bf16[512,128]{1,0:T(8,128)(2,1)S(1)}, u32[]{:S(2)}, u32[]{:S(2)}) collective-permute-start(bf16[512,128]{1,0:T(8,128)(2,1)S(1)} %shard_map.105), channel_id=1, source_target_pairs={{0,192},{8,64},{16,0},{24,128},{32,224},{40,96},{48,32},{56,160},{... | collective-permute-start | bytes 393224 | tf_op jit(solution)/shard_map/ppermute | solution.py:337
  73.8 8.7 %collective-permute-start.12 = (bf16[512,128]{1,0:T(8,128)(2,1)S(1)}, bf16[512,128]{1,0:T(8,128)(2,1)S(1)}, u32[]{:S(2)}, u32[]{:S(2)}) collective-permute-start(bf16[512,128]{1,0:T(8,128)(2,1)S(1)} %shard_map.101), channel_id=1, source_target_pairs={{0,160},{8,96},{16,224},{24,32},{32,0},{40,64},{48,192},{56,128},{... | collective-permute-start | bytes 393224 | tf_op jit(solution)/shard_map/ppermute | solution.py:336
